TPU v7x, 256 devices: a whole 4x4x8 slice. The times are simulated.
256 devices in a mesh: gx: 32 (over z, y), gy: 8 (over x, core).
Axes of the slice: x: 4, y: 4, z: 8, core: 2. Of those that a mesh axis runs over, the one named last changes fastest.
Arguments:
- tracer: float32 [128, 1024, 1024], P(None, 'gx', 'gy'), may hold values from -11 to 11
- velocity: float32 [2, 1024, 1024], P(None, 'gx', 'gy'), may hold values from -0.25 to 0.25
- diffusivity: float32 [128], replicated, may hold values from 0.02 to 0.08
- singular: float32 [94], replicated, may hold values from 0.5 to 8
- basis_vectors: float32 [94, 2, 1024, 1024], P(None, None, 'gx', 'gy'), may hold values from -10 to 10, as said below
Outputs:
- tracer_next: float32 [128, 1024, 1024], P(None, 'gx', 'gy')
- basis_next: float32 [96, 2, 1024, 1024], P(None, None, 'gx', 'gy')
Inputs may be any that keep to these rules, and one draw needn't show every extreme that they name: The 94 vectors basis_vectors[i], each over all 2 x 1024 x 1024 cells, are orthogonal with squared length 2097152, to float32 rounding.
All inputs are finite; a program needn't handle non-finite values.
Results may differ from a plain program's by a relative error of at most 0.0003.
Values sent between devices are 32-bit elements; how exact they have to be, the bound alone decides.
No kernel may reach another device: no remote copies, remote signals or barrier semaphores. Data moves between devices by JAX's collectives and lax.ppermute only.
A program may use at most 64 MiB of HBM per device.

v0:
```python
import jax
import jax.numpy as jnp
from jax import lax
from jax.sharding import Mesh
from jax.sharding import PartitionSpec as P

ROOT_ITERS = 5
GX = ("gx_0", "gx_1")
GY = ("gy_0", "gy_1")
GX_GY = ("gx_0", "gx_1", "gy_0", "gy_1")


def padded_2(cells, sides, width):
    for axis, dim in sides:
        count = lax.axis_size(axis)
        head = lax.slice_in_dim(cells, 0, width, axis=dim)
        tail = lax.slice_in_dim(cells, cells.shape[dim] - width, cells.shape[dim], axis=dim)
        cells = jnp.concatenate(
            [
                lax.ppermute(tail, axis, [(i, (i + 1) % count) for i in range(count)]),
                cells,
                lax.ppermute(head, axis, [((i + 1) % count, i) for i in range(count)]),
            ],
            axis=dim,
        )
    return cells


def by_axis(x, axes):
    for axis in axes:
        x = lax.psum(x, axis)
    return x


def advance(padded, velocity, diffusivity):
    centre = padded[:, 1:-1, 1:-1]
    west_cells = padded[:, :-2, 1:-1]
    east_cells = padded[:, 2:, 1:-1]
    south_cells = padded[:, 1:-1, :-2]
    north_cells = padded[:, 1:-1, 2:]
    level_below = jnp.roll(centre, 1, 0)
    level_above = jnp.roll(centre, -1, 0)
    speed_x = velocity[0]
    speed_y = velocity[1]
    spread = (
        west_cells
        + east_cells
        + south_cells
        + north_cells
        + level_below
        + level_above
        - 6.0 * centre
    )
    carried = (
        jnp.maximum(speed_x, 0.0) * (centre - west_cells)
        + jnp.minimum(speed_x, 0.0) * (east_cells - centre)
        + jnp.maximum(speed_y, 0.0) * (centre - south_cells)
        + jnp.minimum(speed_y, 0.0) * (north_cells - centre)
    )
    return centre + diffusivity[:, None, None] * spread - carried


def upper_factor(gram_matrix):
    first_entry = jnp.sqrt(gram_matrix[0, 0])
    cross_entry = gram_matrix[0, 1] / first_entry
    second_entry = jnp.sqrt(gram_matrix[1, 1] - cross_entry * cross_entry)
    zero_entry = jnp.zeros_like(first_entry)
    return jnp.stack([jnp.stack([first_entry, cross_entry]), jnp.stack([zero_entry, second_entry])])


def orthonormal_columns(residual, factor):
    first_column = residual[0] / factor[0, 0]
    second_column = (residual[1] - factor[0, 1] * first_column) / factor[1, 1]
    return jnp.stack([first_column, second_column])


def inverse_spd(matrix):
    lower_factor = jnp.linalg.cholesky(matrix)
    identity = jnp.eye(matrix.shape[0], dtype=matrix.dtype)
    solved = lax.linalg.triangular_solve(lower_factor, identity, left_side=True, lower=True)
    return jnp.dot(solved.T, solved, precision=lax.Precision.HIGHEST)


def square_root_core(singular, projections, factor):
    vector_count = singular.shape[0]
    core_matrix = jnp.block(
        [[jnp.diag(singular), projections], [jnp.zeros((2, vector_count), jnp.float32), factor]]
    )
    squared = jnp.dot(core_matrix, core_matrix.T, precision=lax.Precision.HIGHEST)
    scale_factor = jnp.trace(squared) / (vector_count + 2)
    current = squared / scale_factor
    partner = jnp.eye(vector_count + 2, dtype=squared.dtype)
    for repeat in range(ROOT_ITERS):
        new_current = 0.5 * (current + inverse_spd(partner))
        new_partner = 0.5 * (partner + inverse_spd(current))
        current = 0.5 * (new_current + new_current.T)
        partner = 0.5 * (new_partner + new_partner.T)
    return jnp.sqrt(scale_factor) * current


def on_device(tracer, velocity, diffusivity, singular, basis_vectors):
    vector_count = basis_vectors.shape[0]
    window = basis_vectors.shape[1]
    cells_x = basis_vectors.shape[2]
    cells_y = basis_vectors.shape[3]
    rows_all = window * cells_x * cells_y * lax.axis_size(GX) * lax.axis_size(GY)
    identity_two = jnp.eye(2, dtype=jnp.float32)
    wider = padded_2(tracer, ((GX, 1), (GY, 2)), 2)
    velocity_cycle = padded_2(velocity, ((GX, 1), (GY, 2)), 1)
    cycle_step = advance(wider, velocity_cycle, diffusivity)
    after_one = cycle_step[:, 1:-1, 1:-1]
    after_two = advance(cycle_step, velocity, diffusivity)
    snapshots = jnp.stack([after_one[:window].reshape(-1), after_two[:window].reshape(-1)])
    flat_basis = basis_vectors.reshape(vector_count, -1)
    local_products = jnp.einsum("kr,mr->km", flat_basis, snapshots, precision=lax.Precision.HIGHEST)
    local_cross = jnp.einsum("mr,nr->mn", snapshots, snapshots, precision=lax.Precision.HIGHEST)
    summed_products, summed_cross = (by_axis(local_products, GX_GY), by_axis(local_cross, GX_GY))
    projections = summed_products / rows_all
    gram_matrix = (
        summed_cross / rows_all
        - jnp.dot(projections.T, projections, precision=lax.Precision.HIGHEST)
        + 1e-06 * identity_two
    )
    residual = snapshots - jnp.einsum(
        "km,kr->mr", projections, flat_basis, precision=lax.Precision.HIGHEST
    )
    factor = upper_factor(gram_matrix)
    columns = orthonormal_columns(residual, factor)
    core_root = square_root_core(singular, projections, factor)
    rotated = jnp.einsum(
        "ij,ir->jr", core_root[:vector_count], flat_basis, precision=lax.Precision.HIGHEST
    ) + jnp.einsum("mj,mr->jr", core_root[vector_count:], columns, precision=lax.Precision.HIGHEST)
    return (after_two, rotated.reshape(vector_count + 2, window, cells_x, cells_y))


def solution(mesh):
    finer = Mesh(mesh.devices.reshape(8, 4, 4, 2), ("gx_0", "gx_1", "gy_0", "gy_1"))
    in_specs = (P(None, GX, GY), P(None, GX, GY), P(), P(), P(None, None, GX, GY))
    out_specs = (P(None, GX, GY), P(None, None, GX, GY))
    return jax.shard_map(
        on_device, mesh=finer, in_specs=in_specs, out_specs=out_specs, check_vma=False
    )
```

profile of v0, /device:TPU:1, one launch (start us, length us, event | category | flops | bytes accessed | tf_op | source)
XLA Modules:
  0.0 276.1 jit_solution(11350857094485461204)
XLA Ops:
  0.6 2.7 copy.28
  3.3 0.9 fusion.101
  4.2 2.1 collective-permute-start
  6.4 6.7 %collective-permute-start.1 = (f32[128,2,128]{0,1,2:T(2,128)}, f32[128,2,128]{0,1,2:T(2,128)S(1)}, u32[]{:S(2)}, u32[]{:S(2)}) collective-permute-start(f32[128,2,128]{0,1,2:T(2,128)} %get-tuple-element.33), channel_id=1, source_target_pairs={{8,0},{16,8},{24,16},{32,24},{40,32},{48,40},{56,48},{64,56},{72,6... | collective-permute-start | bytes 393224 | tf_op jit(solution)/shard_map/ppermute | solution.py:22
  13.1 4.9 %collective-permute-start.5 = (f32[2,1,128]{2,1,0:T(1,128)S(1)}, f32[2,1,128]{2,1,0:T(1,128)S(1)}, u32[]{:S(2)}, u32[]{:S(2)}) collective-permute-start(f32[2,1,128]{2,1,0:T(1,128)S(1)} %get-tuple-element.45), channel_id=1, source_target_pairs={{8,0},{16,8},{24,16},{32,24},{40,32},{48,40},{56,48},{64,56},{72,6... | collective-permute-start | bytes 3080 | tf_op jit(solution)/shard_map/ppermute | solution.py:22
  18.2 8.8 %cholesky.149 = f32[96,96]{1,0:T(8,128)S(1)} custom-call(f32[96,96]{1,0:T(8,128)S(1)} %fusion.45), custom_call_target="Cholesky" | custom-call | tf_op jit(solution)/shard_map/jit(cholesky)/cholesky | solution.py:78
  28.2 7.4 %custom-call.13 = f32[1,96,96]{1,2,0:T(8,128)S(1)} custom-call(f32[1,96,96]{2,1,0:T(8,128)S(1)} %fusion.33), custom_call_target="InvertDiagBlocksLowerTriangular" | custom-call | tf_op jit(solution)/shard_map/triangular_solve/custom-call.0 | solution.py:80
  35.9 2.6 collective-permute-start.6
  38.6 2.1 pad.46
  40.7 2.2 copy.62
  43.5 1.8 collective-permute-start.2
  46.4 2.3 collective-permute-done.3
  49.0 0.8 fusion.97
  49.7 0.8 fusion.98
  50.5 4.9 %fusion.4 = f32[128,34,130]{0,2,1:T(8,128)S(1)} fusion(f32[127,34,130]{0,2,1:T(8,128)S(1)} %get-tuple-element.25, f32[1,34,130]{0,2,1:T(8,128)S(1)} %get-tuple-element.27, f32[1,34,130]{0,2,1:T(8,128)S(1)} %get-tuple-element.26, f32[127,34,130]{0,2,1:T(8,128)S(1)} %get-tuple-element.24, f32[128,36,132]{0,2,1:T(8,128)S(1)} %pad_maximum_fusion.1, ...), kind=kLoop, calls=%fused_computation.11 | loop fusion | flops 14144000 | bytes 16082496 | tf_op jit(solution)/shard_map/sub | solution.py:60
  55.4 0.8 fusion.99
  56.3 0.8 fusion.100
  57.1 1.6 slice.218
  58.7 5.3 %fusion.9 = f32[128,32,128]{0,2,1:T(8,128)} fusion(f32[127,32,128]{0,2,1:T(8,128)S(1)} %get-tuple-element.29, f32[1,32,128]{0,2,1:T(8,128)S(1)} %get-tuple-element.31, f32[1,32,128]{0,2,1:T(8,128)S(1)} %get-tuple-element.30, f32[127,32,128]{0,2,1:T(8,128)S(1)} %get-tuple-element.28, f32[128,34,130]{0,2,1:T(8,128)S(1)} %fusion.4, ...), kind=kLoop, calls=%fused_computation.17 | loop fusion | flops 12058624 | bytes 16843264 | tf_op jit(solution)/shard_map/sub | solution.py:60
  63.9 2.2 copy.39
  66.1 2.2 copy.38
  68.4 0.7 fusion.92
  69.1 2.5 convolution_bitcast_fusion
  71.7 10.9 %all-reduce.1 = (f32[2,2]{1,0:T(2,128)S(1)}, f32[94,2]{0,1:T(2,128)S(1)}) all-reduce(f32[2,2]{1,0:T(2,128)S(1)} %fusion.92, f32[94,2]{0,1:T(2,128)S(1)} %convolution_bitcast_fusion), channel_id=1, replica_groups=mesh['gx_0'=8,'gx_1'=4,'gy_0'=4,'gy_1'=2] {'gx_0'}, use_global_device_ids=true, to_apply=%region_4.5 | all-reduce | flops 192 | bytes 1536 | tf_op jit(solution)/shard_map/psum | solution.py:31
  82.6 6.0 %all-reduce.3 = (f32[2,2]{1,0:T(2,128)S(1)}, f32[94,2]{0,1:T(2,128)S(1)}) all-reduce(f32[2,2]{1,0:T(2,128)S(1)} %get-tuple-element.6, f32[94,2]{0,1:T(2,128)S(1)} %get-tuple-element.7), channel_id=1, replica_groups=mesh['gx_0'=8,'gx_1'=4,'gy_0'=4,'gy_1'=2] {'gx_1'}, use_global_device_ids=true, to_apply=%region_5.6 | all-reduce | flops 192 | bytes 1536 | tf_op jit(solution)/shard_map/psum | solution.py:31
  88.6 9.9 %all-reduce.2 = (f32[2,2]{1,0:T(2,128)S(1)}, f32[94,2]{0,1:T(2,128)S(1)}) all-reduce(f32[2,2]{1,0:T(2,128)S(1)} %get-tuple-element.10, f32[94,2]{0,1:T(2,128)S(1)} %get-tuple-element.11), channel_id=1, replica_groups=mesh['gx_0'=8,'gx_1'=4,'gy_0'=4,'gy_1'=2] {'gy_0'}, use_global_device_ids=true, to_apply=%region_6.7 | all-reduce | flops 192 | bytes 1536 | tf_op jit(solution)/shard_map/psum | solution.py:31
  98.5 7.2 %all-reduce.4 = (f32[2,2]{1,0:T(2,128)S(1)}, f32[94,2]{0,1:T(2,128)S(1)}) all-reduce(f32[2,2]{1,0:T(2,128)S(1)} %get-tuple-element.8, f32[94,2]{0,1:T(2,128)S(1)} %get-tuple-element.9), channel_id=1, replica_groups=mesh['gx_0'=8,'gx_1'=4,'gy_0'=4,'gy_1'=2] {'gy_1'}, use_global_device_ids=true, to_apply=%region_7.8 | all-reduce | flops 192 | bytes 1536 | tf_op jit(solution)/shard_map/psum | solution.py:31
  105.7 1.6 convolution_subtract_fusion
  110.6 0.7 slice.193
  113.2 3.4 %copy.61 = f32[128,32,128]{2,1,0:T(8,128)} copy(f32[128,32,128]{0,2,1:T(8,128)} %fusion.9) | data formatting | bytes 4194304
  116.8 8.8 %cholesky.160 = f32[96,96]{1,0:T(8,128)S(1)} custom-call(f32[96,96]{1,0:T(8,128)S(1)} %copy.45), custom_call_target="Cholesky" | custom-call | tf_op jit(solution)/shard_map/jit(cholesky)/cholesky | solution.py:78
  126.3 0.7 fusion.34
  127.0 7.4 %custom-call.14 = f32[1,96,96]{1,2,0:T(8,128)S(1)} custom-call(f32[1,96,96]{2,1,0:T(8,128)S(1)} %fusion.34), custom_call_target="InvertDiagBlocksLowerTriangular" | custom-call | tf_op jit(solution)/shard_map/triangular_solve/custom-call.0 | solution.py:80
  135.4 8.8 %cholesky.182 = f32[96,96]{1,0:T(8,128)S(1)} custom-call(f32[96,96]{1,0:T(8,128)S(1)} %fusion.78), custom_call_target="Cholesky" | custom-call | tf_op jit(solution)/shard_map/jit(cholesky)/cholesky | solution.py:78
  144.9 0.7 fusion.36
  145.6 7.4 %custom-call.16 = f32[1,96,96]{1,2,0:T(8,128)S(1)} custom-call(f32[1,96,96]{2,1,0:T(8,128)S(1)} %fusion.36), custom_call_target="InvertDiagBlocksLowerTriangular" | custom-call | tf_op jit(solution)/shard_map/triangular_solve/custom-call.0 | solution.py:80
  153.7 8.8 %cholesky.171 = f32[96,96]{1,0:T(8,128)S(1)} custom-call(f32[96,96]{1,0:T(8,128)S(1)} %fusion.82), custom_call_target="Cholesky" | custom-call | tf_op jit(solution)/shard_map/jit(cholesky)/cholesky | solution.py:78
  163.1 0.7 fusion.35
  163.8 7.4 %custom-call.15 = f32[1,96,96]{1,2,0:T(8,128)S(1)} custom-call(f32[1,96,96]{2,1,0:T(8,128)S(1)} %fusion.35), custom_call_target="InvertDiagBlocksLowerTriangular" | custom-call | tf_op jit(solution)/shard_map/triangular_solve/custom-call.0 | solution.py:80
  171.9 8.9 %cholesky.193 = f32[96,96]{1,0:T(8,128)S(1)} custom-call(f32[96,96]{1,0:T(8,128)S(1)} %fusion.74), custom_call_target="Cholesky" | custom-call | tf_op jit(solution)/shard_map/jit(cholesky)/cholesky | solution.py:78
  181.5 0.7 fusion.37
  182.2 7.4 %custom-call.17 = f32[1,96,96]{1,2,0:T(8,128)S(1)} custom-call(f32[1,96,96]{2,1,0:T(8,128)S(1)} %fusion.37), custom_call_target="InvertDiagBlocksLowerTriangular" | custom-call | tf_op jit(solution)/shard_map/triangular_solve/custom-call.0 | solution.py:80
  190.1 0.7 copy.52
  190.8 0.8 fusion.72
  191.7 8.8 %cholesky.204 = f32[96,96]{1,0:T(8,128)S(1)} custom-call(f32[96,96]{1,0:T(8,128)S(1)} %fusion.70), custom_call_target="Cholesky" | custom-call | tf_op jit(solution)/shard_map/jit(cholesky)/cholesky | solution.py:78
  201.1 0.7 fusion.38
  201.8 7.4 %custom-call.18 = f32[1,96,96]{1,2,0:T(8,128)S(1)} custom-call(f32[1,96,96]{2,1,0:T(8,128)S(1)} %fusion.38), custom_call_target="InvertDiagBlocksLowerTriangular" | custom-call | tf_op jit(solution)/shard_map/triangular_solve/custom-call.0 | solution.py:80
  209.9 8.8 %cholesky.226 = f32[96,96]{1,0:T(8,128)S(1)} custom-call(f32[96,96]{1,0:T(8,128)S(1)} %fusion.62), custom_call_target="Cholesky" | custom-call | tf_op jit(solution)/shard_map/jit(cholesky)/cholesky | solution.py:78
  218.7 0.6 compare_reduce_fusion.1
  219.4 0.7 fusion.40
  220.0 7.4 %custom-call.20 = f32[1,96,96]{1,2,0:T(8,128)S(1)} custom-call(f32[1,96,96]{2,1,0:T(8,128)S(1)} %fusion.40), custom_call_target="InvertDiagBlocksLowerTriangular" | custom-call | tf_op jit(solution)/shard_map/triangular_solve/custom-call.0 | solution.py:80
  227.9 0.7 copy.58
  228.6 0.8 fusion.60
  229.6 9.0 %cholesky.215 = f32[96,96]{1,0:T(8,128)S(1)} custom-call(f32[96,96]{1,0:T(8,128)S(1)} %fusion.66), custom_call_target="Cholesky" | custom-call | tf_op jit(solution)/shard_map/jit(cholesky)/cholesky | solution.py:78
  239.2 0.7 fusion.39
  239.9 7.4 %custom-call.19 = f32[1,96,96]{1,2,0:T(8,128)S(1)} custom-call(f32[1,96,96]{2,1,0:T(8,128)S(1)} %fusion.39), custom_call_target="InvertDiagBlocksLowerTriangular" | custom-call | tf_op jit(solution)/shard_map/triangular_solve/custom-call.0 | solution.py:80
  247.9 8.8 %cholesky.237 = f32[96,96]{1,0:T(8,128)S(1)} custom-call(f32[96,96]{1,0:T(8,128)S(1)} %fusion.58), custom_call_target="Cholesky" | custom-call | tf_op jit(solution)/shard_map/jit(cholesky)/cholesky | solution.py:78
  256.8 0.6 compare_reduce_fusion
  257.4 0.7 fusion.41
  258.1 7.4 %custom-call.21 = f32[1,96,96]{1,2,0:T(8,128)S(1)} custom-call(f32[1,96,96]{2,1,0:T(8,128)S(1)} %fusion.41), custom_call_target="InvertDiagBlocksLowerTriangular" | custom-call | tf_op jit(solution)/shard_map/triangular_solve/custom-call.0 | solution.py:80
  266.1 2.9 %fusion.47 = f32[96,8192]{1,0:T(8,128)S(1)} fusion(f32[94,8192]{1,0:T(8,128)S(1)} %bitcast.200, f32[96,96]{0,1:T(8,128)S(1)} %fusion.56), kind=kOutput, calls=%fused_computation.71 | convolution fusion | flops 887095296 | bytes 6262784 | tf_op jit(solution)/shard_map/ij,ir->jr/dot_general | solution.py:130
  269.0 1.9 fusion.89
  271.0 2.7 fusion.10
  273.7 2.2 copy.63
  (109 shorter events, 16.3 us)
Async XLA Ops:
  0.6 12.5 %copy-start.2 = (f32[2,32,128]{2,1,0:T(8,128)S(1)}, f32[2,32,128]{2,1,0:T(8,128)}, u32[]{:S(2)}) copy-start(f32[2,32,128]{2,1,0:T(8,128)} %param.9) | copy-start | bytes 98308
  3.3 37.3 %copy-start = (f32[128,32,128]{0,1,2:T(8,128)}, f32[128,32,128]{0,1,2:T(8,128)S(1)}, u32[]{:S(2)}) copy-start(f32[128,32,128]{0,1,2:T(8,128)S(1)} %copy.28) | copy-start | bytes 6291460
  4.2 38.8 %collective-permute-start = (f32[128,2,128]{0,1,2:T(2,128)}, f32[128,2,128]{0,1,2:T(2,128)S(1)}, u32[]{:S(2)}, u32[]{:S(2)}) collective-permute-start(f32[128,2,128]{0,1,2:T(2,128)} %get-tuple-element.32), channel_id=1, source_target_pairs={{0,8},{8,16},{16,24},{24,32},{32,40},{40,48},{48,56},{56,64},{64,7... | collective-permute-start | bytes 393224 | tf_op jit(solution)/shard_map/ppermute | solution.py:20
  6.4 36.7 %collective-permute-start.1 = (f32[128,2,128]{0,1,2:T(2,128)}, f32[128,2,128]{0,1,2:T(2,128)S(1)}, u32[]{:S(2)}, u32[]{:S(2)}) collective-permute-start(f32[128,2,128]{0,1,2:T(2,128)} %get-tuple-element.33), channel_id=1, source_target_pairs={{8,0},{16,8},{24,16},{32,24},{40,32},{48,40},{56,48},{64,56},{72,6... | collective-permute-start | bytes 393224 | tf_op jit(solution)/shard_map/ppermute | solution.py:22
  13.1 22.7 %collective-permute-start.4 = (f32[2,1,128]{2,1,0:T(1,128)S(1)}, f32[2,1,128]{2,1,0:T(1,128)S(1)}, u32[]{:S(2)}, u32[]{:S(2)}) collective-permute-start(f32[2,1,128]{2,1,0:T(1,128)S(1)} %get-tuple-element.44), channel_id=1, source_target_pairs={{0,8},{8,16},{16,24},{24,32},{32,40},{40,48},{48,56},{56,64},{64,7... | collective-permute-start | bytes 3080 | tf_op jit(solution)/shard_map/ppermute | solution.py:20
  13.1 22.7 %collective-permute-start.5 = (f32[2,1,128]{2,1,0:T(1,128)S(1)}, f32[2,1,128]{2,1,0:T(1,128)S(1)}, u32[]{:S(2)}, u32[]{:S(2)}) collective-permute-start(f32[2,1,128]{2,1,0:T(1,128)S(1)} %get-tuple-element.45), channel_id=1, source_target_pairs={{8,0},{16,8},{24,16},{32,24},{40,32},{48,40},{56,48},{64,56},{72,6... | collective-permute-start | bytes 3080 | tf_op jit(solution)/shard_map/ppermute | solution.py:22
  35.9 7.0 %collective-permute-start.6 = (f32[2,34,1]{2,1,0:T(8,128)S(1)}, f32[2,34,1]{2,1,0:T(8,128)S(1)}, u32[]{:S(2)}, u32[]{:S(2)}) collective-permute-start(f32[2,34,1]{2,1,0:T(8,128)S(1)} %get-tuple-element.38), channel_id=1, source_target_pairs={{0,1},{1,2},{2,3},{3,4},{4,5},{5,6},{6,7},{7,0},{8,9},{9,10},{10,1... | collective-permute-start | bytes 824 | tf_op jit(solution)/shard_map/ppermute | solution.py:20
  38.6 4.3 %collective-permute-start.7 = (f32[2,34,1]{2,1,0:T(8,128)S(1)}, f32[2,34,1]{2,1,0:T(8,128)S(1)}, u32[]{:S(2)}, u32[]{:S(2)}) collective-permute-start(f32[2,34,1]{2,1,0:T(8,128)S(1)} %get-tuple-element.39), channel_id=1, source_target_pairs={{1,0},{2,1},{3,2},{4,3},{5,4},{6,5},{7,6},{0,7},{9,8},{10,9},{11,1... | collective-permute-start | bytes 824 | tf_op jit(solution)/shard_map/ppermute | solution.py:22
  40.7 2.4 copy-start.1
  43.5 2.9 %collective-permute-start.2 = (f32[128,36,2]{0,1,2:T(8,128)S(1)}, f32[128,36,2]{0,1,2:T(8,128)S(1)}, u32[]{:S(2)}, u32[]{:S(2)}) collective-permute-start(f32[128,36,2]{0,1,2:T(8,128)S(1)} %get-tuple-element.22), channel_id=1, source_target_pairs={{0,1},{1,2},{2,3},{3,4},{4,5},{5,6},{6,7},{7,0},{8,9},{9,10},{10,1... | collective-permute-start | bytes 110600 | tf_op jit(solution)/shard_map/ppermute | solution.py:20
  45.3 3.4 %collective-permute-start.3 = (f32[128,36,2]{0,1,2:T(8,128)S(1)}, f32[128,36,2]{0,1,2:T(8,128)S(1)}, u32[]{:S(2)}, u32[]{:S(2)}) collective-permute-start(f32[128,36,2]{0,1,2:T(8,128)S(1)} %get-tuple-element.23), channel_id=1, source_target_pairs={{1,0},{2,1},{3,2},{4,3},{5,4},{6,5},{7,6},{0,7},{9,8},{10,9},{11,1... | collective-permute-start | bytes 110600 | tf_op jit(solution)/shard_map/ppermute | solution.py:22
  49.7 0.8 copy-start.3
  66.1 5.5 %copy-start.4 = (f32[94]{0:T(128)S(1)}, f32[94]{0:T(128)}, u32[]{:S(2)}) copy-start(f32[94]{0:T(128)} %param.11) | copy-start | bytes 1132
where the time goes:
time: 280 us; the launch traced here: 276 us
  other arithmetic  173 us (62%)
  blocking collectives  34 us (12%)
  local copies, waits for them, and re-layouts  28.2 us (10%)
  starting transfers between devices  18.3 us (7%)
  matrix products  15.6 us (6%)
  between operations  4.34 us (2%)
    another operation x27, other arithmetic, inverse_spd(): lower_factor = jnp.linalg.cholesky(matrix)  85.4 us
    another operation x18, other arithmetic, inverse_spd(): lax.linalg.triangular_solve(lower_factor, identity, left_side=True, lower...  72 us
    psum x4, blocking collectives, by_axis(): x = lax.psum(x, axis)  34 us
    unnamed x15, local copies, waits for them, and re-layouts  12.6 us
    ppermute x4, starting transfers between devices, padded_2(): lax.ppermute(head, axis, [((i + 1) % count, i) for i in range(count)])  11.8 us
    sub x2, other arithmetic, advance(): return centre + diffusivity[:, None, None] * spread - carried  10.2 us
    ppermute x4, starting transfers between devices, padded_2(): lax.ppermute(tail, axis, [(i, (i + 1) % count) for i in range(count)])  6.49 us
  transfers between devices with their start and end apart: 8, of which 2 were waited for; matrix products, arithmetic and copies ran while one was open for 8% of the time, Pallas kernels for 0%

commit v1 on v0

v1 whole, which is shorter than its diff:
```python
import math

import jax
import jax.numpy as jnp
from jax import lax
from jax.experimental import pallas as pl
from jax.experimental.pallas import tpu as pltpu
from jax.sharding import Mesh
from jax.sharding import PartitionSpec as P

F32 = jnp.float32
BF16 = jnp.bfloat16
GX = ("z", "y")
GY = ("x", "c")
CHIPS = ("z", "y", "x")
ROOT_ITERS = 5
SHIFTS = 2**ROOT_ITERS
POLES = SHIFTS // 2 - 1
VMEM = pltpu.VMEM


def lanes_of(shape):
    return lax.broadcasted_iota(jnp.int32, shape, len(shape) - 1)


def rows_of(shape):
    return lax.broadcasted_iota(jnp.int32, shape, len(shape) - 2)


def step(c, xm, xp, ym, yp, zm, zp, d, vxp, vxn, vyp, vyn):
    spread = (xm + xp) + (ym + yp) + (zm + zp) - 6.0 * c
    carried = (vxp * (c - xm) + vxn * (xp - c)) + (vyp * (c - ym) + vyn * (yp - c))
    return c + d * spread - carried


def signed_parts(vx, vy):
    return jnp.maximum(vx, 0.0), jnp.minimum(vx, 0.0), jnp.maximum(vy, 0.0), jnp.minimum(vy, 0.0)


def before(c, ghost, axis):
    n = c.shape[axis]
    at = lax.broadcasted_iota(jnp.int32, c.shape, axis)
    return jnp.where(at == 0, ghost, pltpu.roll(c, 1, axis))


def after(c, ghost, axis):
    n = c.shape[axis]
    at = lax.broadcasted_iota(jnp.int32, c.shape, axis)
    return jnp.where(at == n - 1, ghost, pltpu.roll(c, n - 1, axis))


def pack_columns_kernel(levels, tracer, velocity, left, right):
    nx, ny = tracer.shape[1], tracer.shape[2]
    lane = lanes_of((nx, ny))

    def level(z, carry):
        a, b, y, w = carry
        r = pltpu.roll(tracer[z], z, 1)
        rel = (lane - z) & (ny - 1)
        a = jnp.where(rel == 0, r, a)
        b = jnp.where(rel == 1, r, b)
        y = jnp.where(rel == ny - 1, r, y)
        w = jnp.where(rel == ny - 2, r, w)
        return a, b, y, w

    zero = jnp.zeros((nx, ny), F32)
    a, b, y, w = lax.fori_loop(0, levels, level, (zero,) * 4, unroll=8)
    left[0] = a
    left[1] = pltpu.roll(b, ny - 1, 1)
    right[0] = pltpu.roll(y, 1, 1)
    right[1] = pltpu.roll(w, 2, 1)
    vx, vy = velocity[0], velocity[1]
    left[2] = jnp.where(lane == 0, vx, pltpu.roll(vy, 1, 1))
    right[2] = jnp.where(lane == ny - 1, vx, pltpu.roll(vy, ny - 1, 1))


def pack_rows_kernel(low, high, velocity, from_left, from_right, up, down):
    nx = low.shape[1]
    for edge, inner, out in ((0, 1, up), (nx - 1, nx - 2, down)):
        for s in range(6):
            ref, z = (high, s) if s < 2 else (low, s - 2)
            out[s : s + 1, :] = ref[z, edge : edge + 1, :]
            out[8 + s : 9 + s, :] = ref[z, inner : inner + 1, :]
        for s in (6, 7, 14, 15, 20, 21, 22, 23):
            out[s : s + 1, :] = jnp.zeros((1, low.shape[2]), F32)
        out[16:17, :] = velocity[0, edge : edge + 1, :]
        out[17:18, :] = velocity[1, edge : edge + 1, :]
        out[18:19, :] = from_left[0, edge : edge + 1, :]
        out[19:20, :] = from_right[0, edge : edge + 1, :]


def window_kernel(
    diff, low, high, velocity, diff_row, own_left, own_right, from_left, from_right,
    own_up, own_down, from_up, from_down, basis,
    snaps, sums, ghost_left, ghost_right, q0, q1,
):
    nz, nx, ny = diff.shape[0], low.shape[1], low.shape[2]
    count = basis.shape[0]
    dz = diff_row[...]
    for gin, inner, outer, corner, vx_at, vy_at, out in (
        (from_left, None, own_left, 18, ny - 1, ny - 2, ghost_left),
        (from_right, own_right, None, 19, 0, 1, ghost_right),
    ):
        c = gin[0]
        ym = gin[1] if inner is None else inner[0]
        yp = gin[1] if outer is None else outer[0]
        vx = gin[2][:, vx_at : vx_at + 1]
        vy = gin[2][:, vy_at : vy_at + 1]
        parts = signed_parts(vx, vy)
        xm = before(c, from_up[corner : corner + 1, :], 0)
        xp = after(c, from_down[corner : corner + 1, :], 0)
        out[...] = step(c, xm, xp, ym, yp, pltpu.roll(c, 1, 1), pltpu.roll(c, nz - 1, 1), dz, *parts)

    sub = rows_of((8, ny))
    lane = lanes_of((8, ny))
    d_rows = jnp.where(sub == 2, diff[0], diff[1])
    ghost_rows = []
    for gin, own, top in ((from_up, own_up, True), (from_down, own_down, False)):
        c = gin[0:8, :]
        beyond, near = gin[8:16, :], own[0:8, :]
        xm, xp = (beyond, near) if top else (near, beyond)
        west = jnp.where(sub == 2, gin[18:19, 0:1], gin[18:19, 1:2])
        east = jnp.where(sub == 2, gin[19:20, 0:1], gin[19:20, 1:2])
        parts = signed_parts(gin[16:17, :], gin[17:18, :])
        ghost_rows.append(
            step(c, xm, xp, before(c, west, 1), after(c, east, 1),
                 pltpu.roll(c, 1, 0), pltpu.roll(c, 7, 0), d_rows, *parts)
        )

    parts = signed_parts(velocity[0], velocity[1])
    u = [high[0], high[1], low[0], low[1], low[2], low[3]]
    first = []
    for s in range(1, 5):
        z = (s - 2) % nz
        c = u[s]
        xm = before(c, from_up[s : s + 1, :], 0)
        xp = after(c, from_down[s : s + 1, :], 0)
        ym = before(c, from_left[0][:, z : z + 1], 1)
        yp = after(c, from_right[0][:, z : z + 1], 1)
        first.append(step(c, xm, xp, ym, yp, u[s - 1], u[s + 1], diff[z], *parts))
    for z in range(2):
        c = first[z + 1]
        snaps[0, z * nx : (z + 1) * nx, :] = c
        xm = before(c, ghost_rows[0][z + 2 : z + 3, :], 0)
        xp = after(c, ghost_rows[1][z + 2 : z + 3, :], 0)
        ym = before(c, ghost_left[:, z : z + 1], 1)
        yp = after(c, ghost_right[:, z : z + 1], 1)
        snaps[1, z * nx : (z + 1) * nx, :] = step(
            c, xm, xp, ym, yp, first[z], first[z + 2], diff[z], *parts
        )

    rows = 2 * nx
    pieces = rows // 8

    def folded(a, b):
        total = a[0:8, :] * b[0:8, :]
        for i in range(1, pieces):
            total = total + a[8 * i : 8 * i + 8, :] * b[8 * i : 8 * i + 8, :]
        return jnp.sum(total, axis=0, keepdims=True)

    q0[...] = jnp.zeros_like(q0)
    q1[...] = jnp.zeros_like(q1)

    def product(k, carry):
        b = basis[k]
        q0[pl.ds(k, 1), :] = folded(b, snaps[0])
        q1[pl.ds(k, 1), :] = folded(b, snaps[1])
        return carry

    lax.fori_loop(0, count, product, 0, unroll=2)
    cross = folded(snaps[0], snaps[1])
    q0[count : count + 1, :] = folded(snaps[0], snaps[0])
    q0[count + 1 : count + 2, :] = cross
    q1[count : count + 1, :] = cross
    q1[count + 1 : count + 2, :] = folded(snaps[1], snaps[1])
    ones = jnp.ones((8, ny), F32)
    over_lanes = (((1,), (1,)), ((), ()))
    for m, q in enumerate((q0, q1)):
        line = lax.dot_general(
            ones, q[...], over_lanes, precision=lax.Precision.HIGHEST, preferred_element_type=F32
        )
        sums[m : m + 1, :] = line[0:1, :]


def bulk_kernel(
    diff, tracer, velocity, diff_rows, from_left, from_right, ghost_left, ghost_right,
    from_up, from_down, top, bottom, out, first, above, below,
):
    nz, nx, ny = tracer.shape
    eye = rows_of((nz, nz)) == lanes_of((nz, nz))
    d_all = diff_rows[...]

    for gin, bulk, own, is_top, res in (
        (from_up, top, 0, True, above),
        (from_down, bottom, nx - 1, False, below),
    ):
        c, beyond, near = bulk[0], bulk[1], tracer[:, own, :]
        xm, xp = (beyond, near) if is_top else (near, beyond)
        west = jnp.sum(jnp.where(eye, gin[18:19, :], 0.0), axis=1, keepdims=True)
        east = jnp.sum(jnp.where(eye, gin[19:20, :], 0.0), axis=1, keepdims=True)
        parts = signed_parts(gin[16:17, :], gin[17:18, :])
        res[...] = step(c, xm, xp, before(c, west, 1), after(c, east, 1),
                        pltpu.roll(c, 1, 0), pltpu.roll(c, nz - 1, 0), d_all, *parts)

    parts = signed_parts(velocity[0], velocity[1])

    def sweep(src, dst, row_up, row_down, col_left, col_right):
        def level(z, carry):
            c = src[z]
            back = (nz - z) & (nz - 1)
            ym = before(c, pltpu.roll(col_left, back, 1), 1)
            yp = after(c, pltpu.roll(col_right, (nz - 1 - z) & (nz - 1), 1), 1)
            xm = before(c, row_up[pl.ds(z, 1), :], 0)
            xp = after(c, row_down[pl.ds(z, 1), :], 0)
            zm = src[(z + nz - 1) & (nz - 1)]
            zp = src[(z + 1) & (nz - 1)]
            dst[z] = step(c, xm, xp, ym, yp, zm, zp, diff[z], *parts)
            return carry

        lax.fori_loop(0, nz, level, 0, unroll=2)

    sweep(tracer, first, top.at[0], bottom.at[0], from_left[0], from_right[0])
    sweep(first, out, above, below, ghost_left[...], ghost_right[...])


def split_kernel(basis, snaps, upper, lower):
    count, rows, ny = basis.shape
    for b in range(rows // 8):
        part = slice(8 * b, 8 * b + 8)
        x = jnp.concatenate([basis[:, part, :], snaps[:, part, :]], axis=0)
        x = jnp.swapaxes(x, 0, 1)
        for i in range(8):
            pair, half = (8 * b + i) // 2, i % 2
            v = x[i]
            hi = v.astype(BF16)
            upper[pair, :, half * ny : (half + 1) * ny] = hi
            lower[pair, :, half * ny : (half + 1) * ny] = (v - hi.astype(F32)).astype(BF16)


def core_kernel(rows_all, parts, singular, upper, lower, out, block, sems):
    count = out.shape[0] - 2
    n = parts.shape[2]
    total = jnp.sum(parts[...], axis=0)
    total = total + pltpu.roll(total, 2, 0)
    total = total + pltpu.roll(total, 4, 0)
    total = total * (1.0 / rows_all)
    lane = lanes_of((1, n))
    zero = jnp.zeros((1, n), F32)

    def add(x):
        return jnp.sum(x, axis=1, keepdims=True)

    def pick(x, at):
        return add(jnp.where(lane == at, x, zero))

    p0 = jnp.where(lane < count, total[0:1, :], zero)
    p1 = jnp.where(lane < count, total[1:2, :], zero)
    g00 = pick(total[0:1, :], count) - add(p0 * p0) + 1e-06
    g01 = pick(total[0:1, :], count + 1) - add(p0 * p1)
    g11 = pick(total[1:2, :], count + 1) - add(p1 * p1) + 1e-06
    r11 = jnp.sqrt(g00)
    r12 = g01 / r11
    r22 = jnp.sqrt(g11 - r12 * r12)
    u0 = jnp.where(lane == count, r11, p0)
    u1 = jnp.where(lane == count, r12, jnp.where(lane == count + 1, r22, p1))
    s = singular[...]
    squares = s * s
    sigma = add(squares + u0 * u0 + u1 * u1) / (count + 2)
    root = jnp.sqrt(sigma)
    d = squares / sigma
    v0 = u0 / root
    v1 = u1 / root

    half = POLES + 1
    row = rows_of((half, n))
    pole = jnp.zeros((half, n), F32)
    for j in range(POLES):
        pole = jnp.where(row == j, math.tan(math.pi * (j + 1) / SHIFTS) ** 2, pole)
    last = row == POLES
    pole = jnp.where(last, 1.0, pole)
    inverse = jnp.where(last, 1.0, 1.0 / (d + pole))
    weight = 2.0 * (1.0 + pole)
    w0 = inverse * v0
    w1 = inverse * v1
    last_one = last[:, 0:1]
    a = jnp.where(last_one, 1.0, 1.0 + add(w0 * v0))
    b = jnp.where(last_one, 0.0, add(w0 * v1))
    c = jnp.where(last_one, 1.0, 1.0 + add(w1 * v1))
    e = b / a
    c = c - b * e
    strength = jnp.where(last, 1.0, weight * pole)
    w1 = jnp.sqrt(strength / c) * (w1 - e * w0)
    w0 = jnp.sqrt(strength / a) * w0
    low_rank = jnp.concatenate([w0, w1], axis=0)
    gains = 1.0 + d + jnp.sum(jnp.where(last, 0.0, weight * d * inverse), axis=0, keepdims=True)
    square = (n, n)
    core = lax.dot_general(
        low_rank, low_rank, (((0,), (0,)), ((), ())),
        precision=lax.Precision.HIGHEST, preferred_element_type=F32,
    )
    core = core + jnp.where(rows_of(square) == lanes_of(square), gains, 0.0)
    core = core * (root * (1.0 / SHIFTS))
    t0 = jnp.where(lane == count, 1.0, -p0) / r11
    q_lane = jnp.where(lane == count + 1, 1.0, -p1)
    t1 = (q_lane - r12 * t0) / r22
    full = jnp.where(lanes_of(square) < count, core, 0.0)
    full = full + core[:, count : count + 1] * t0 + core[:, count + 1 : count + 2] * t1
    full = full[: count + 2, : count + 2]
    hi = full.astype(BF16)
    lo = (full - hi.astype(F32)).astype(BF16)
    both = jnp.concatenate([hi, lo], axis=0)

    blocks = block.shape[1] // 8
    size = count + 2
    copies = []
    for b in range(blocks):
        tiles = []
        for pair in range(4 * b, 4 * b + 4):
            top = upper[pair]
            r = jnp.dot(both, top, preferred_element_type=F32)
            r = r[:size] + r[size:] + jnp.dot(hi, lower[pair], preferred_element_type=F32)
            tiles.append(r[:, :n])
            tiles.append(r[:, n:])
        block[:, 8 * b : 8 * b + 8, :] = jnp.swapaxes(jnp.stack(tiles), 0, 1)
        copy = pltpu.make_async_copy(
            block.at[:, pl.ds(8 * b, 8), :], out.at[:, pl.ds(8 * b, 8), :], sems.at[b]
        )
        copy.start()
        copies.append(copy)
    for copy in copies:
        copy.wait()


def whole(n):
    return [pl.BlockSpec(memory_space=VMEM)] * n


SMEM_SPEC = pl.BlockSpec(memory_space=pltpu.SMEM)


def shaped(*shape, dtype=F32):
    return jax.ShapeDtypeStruct(shape, dtype)


def cost(flops, moved):
    return pl.CostEstimate(flops=flops, bytes_accessed=moved, transcendentals=0)


def limit(mib):
    return pltpu.CompilerParams(vmem_limit_bytes=mib * 2**20)


def ring(x, axes, by):
    count = lax.axis_size(axes)
    return lax.ppermute(x, axes, [(i, (i + by) % count) for i in range(count)])


def on_device(tracer, velocity, diffusivity, singular, basis_vectors):
    nz, nx, ny = tracer.shape
    count, window = basis_vectors.shape[:2]
    rows = window * nx
    basis = basis_vectors.reshape(count, rows, ny)
    rows_all = rows * ny * lax.axis_size(GX) * lax.axis_size(GY)
    chips = lax.axis_size(CHIPS)

    columns = shaped(3, nx, ny)
    own_left, own_right = pl.pallas_call(
        lambda *refs: pack_columns_kernel(nz, *refs),
        out_shape=(columns, columns), in_specs=whole(2), out_specs=tuple(whole(2)),
        compiler_params=limit(8), cost_estimate=cost(10**6, 2 * 2**20), name="columns",
    )(tracer, velocity)
    from_right = ring(own_left, GY, -1)
    from_left = ring(own_right, GY, 1)

    low_spec = pl.BlockSpec((4, nx, ny), lambda i: (0, 0, 0))
    high_spec = pl.BlockSpec((2, nx, ny), lambda i: (nz // 2 - 1, 0, 0))

    def full(*shape):
        return pl.BlockSpec(shape, lambda i: (0,) * len(shape))

    edge = shaped(24, ny)
    own_up, own_down = pl.pallas_call(
        pack_rows_kernel, grid=(1,),
        out_shape=(edge, edge),
        in_specs=[low_spec, high_spec, full(2, nx, ny), full(3, nx, ny), full(3, nx, ny)],
        out_specs=(full(24, ny), full(24, ny)),
        compiler_params=limit(8), cost_estimate=cost(10**4, 2**17), name="edges",
    )(tracer, tracer, velocity, from_left, from_right)
    from_down = ring(own_up, GX, -1)
    from_up = ring(own_down, GX, 1)

    low_now, high_now = tracer[:4], tracer[nz - 2 :]
    snaps, local, ghost_left, ghost_right = pl.pallas_call(
        window_kernel,
        out_shape=(shaped(2, rows, ny), shaped(2, ny), shaped(nx, nz), shaped(nx, nz)),
        in_specs=[SMEM_SPEC] + whole(13), out_specs=tuple(whole(4)),
        scratch_shapes=[VMEM((ny, ny), F32), VMEM((ny, ny), F32)],
        compiler_params=limit(10), cost_estimate=cost(10**7, 4 * 2**20), name="window",
    )(
        diffusivity, low_now, high_now, velocity, diffusivity.reshape(1, nz), own_left, own_right,
        from_left, from_right, own_up, own_down, from_up, from_down, basis,
    )

    pair = local + lax.ppermute(local, "c", [(0, 1), (1, 0)])
    sent = jnp.broadcast_to(pair[None], (chips, 2, ny))
    parts = lax.all_to_all(sent, CHIPS, 0, 0, tiled=True)

    up_rows = jnp.stack([tracer[:, 0], tracer[:, 1]])
    down_rows = jnp.stack([tracer[:, nx - 1], tracer[:, nx - 2]])
    up_rows, down_rows, _ = lax.optimization_barrier((up_rows, down_rows, from_up))
    bottom = ring(up_rows, GX, -1)
    top = ring(down_rows, GX, 1)

    tracer_next = pl.pallas_call(
        bulk_kernel,
        out_shape=shaped(nz, nx, ny),
        in_specs=[SMEM_SPEC] + whole(11), out_specs=whole(1)[0],
        scratch_shapes=[VMEM((nz, nx, ny), F32), VMEM((nz, ny), F32), VMEM((nz, ny), F32)],
        compiler_params=limit(16), cost_estimate=cost(10**8, 4 * 2**20), name="bulk",
    )(
        diffusivity, tracer, velocity, jnp.broadcast_to(diffusivity[:, None], (nz, ny)),
        from_left, from_right, ghost_left, ghost_right, from_up, from_down, top, bottom,
    )

    halves = shaped(rows // 2, count + 2, 2 * ny, dtype=BF16)
    upper, lower = pl.pallas_call(
        split_kernel,
        out_shape=(halves, halves), in_specs=whole(2), out_specs=tuple(whole(2)),
        compiler_params=limit(16), cost_estimate=cost(10**7, 6 * 2**20), name="split",
    )(basis, snaps)

    basis_next = pl.pallas_call(
        lambda *refs: core_kernel(rows_all, *refs),
        out_shape=shaped(count + 2, rows, ny),
        in_specs=whole(4), out_specs=pl.BlockSpec(memory_space=pl.ANY),
        scratch_shapes=[VMEM((count + 2, rows, ny), F32), pltpu.SemaphoreType.DMA((rows // 8,))],
        compiler_params=limit(16), cost_estimate=cost(10**8, 6 * 2**20), name="core",
    )(
        parts.reshape(chips // 4, 8, ny),
        jnp.pad(singular, (0, ny - count)).reshape(1, ny), upper, lower,
    )
    return tracer_next, basis_next.reshape(count + 2, window, nx, ny)


def solution(mesh):
    finer = Mesh(mesh.devices.reshape(8, 4, 4, 2), ("z", "y", "x", "c"))
    in_specs = (P(None, GX, GY), P(None, GX, GY), P(), P(), P(None, None, GX, GY))
    out_specs = (P(None, GX, GY), P(None, None, GX, GY))
    return jax.shard_map(
        on_device, mesh=finer, in_specs=in_specs, out_specs=out_specs, check_vma=False
    )
```

time: 280 us -> 69.5 us (0.25); the launches traced: 276 us -> 69.2 us
  other arithmetic: 173 us -> 0.02 us
  blocking collectives: 34 us -> 0 us
  Pallas kernels: 0 us -> 24.7 us
  local copies, waits for them, and re-layouts: 28.2 us -> 10.3 us
  matrix products: 15.6 us -> 0 us
  starting transfers between devices: 18.3 us -> 28.7 us
  between operations: 4.34 us -> 0.74 us
    another operation x47 -> x1, other arithmetic: 158 us -> 0.02 us  [on_device(): up_rows = jnp.stack([tracer[:, 0], tracer[:, 1]])]
    psum x4 -> x0, blocking collectives: 34 us -> none  [by_axis(): x = lax.psum(x, axis)]
    pallas_call x0 -> x6, Pallas kernels: none -> 24.7 us  [the longest x1 16.2 us: on_device(): pl.pallas_call(bulk_kernel, out_shape=shaped(nz, nx, ny), in_specs=[SMEM_...]
    dot_general x16 -> x0, matrix products: 13.2 us -> none  [the longest x1 2.93 us: on_device(): jnp.einsum('ij,ir->jr', core_root[:vector_count], flat_basis, precision=l...]
    slice x14 -> x3, local copies, waits for them, and re-layouts: 12.1 us -> 0.19 us  [the longest x1 0.18 us: on_device(): down_rows = jnp.stack([tracer[:, nx - 1], tracer[:, nx - 2]])]
    all_to_all x0 -> x1, starting transfers between devices: none -> 11.4 us  [on_device(): parts = lax.all_to_all(sent, CHIPS, 0, 0, tiled=True)]
    sub x2 -> x0, other arithmetic: 10.2 us -> none  [advance(): return centre + diffusivity[:, None, None] * spread - carried]
    unnamed x15 -> x24, local copies, waits for them, and re-layouts: 12.6 us -> 9.37 us
  transfers between devices with their start and end apart: 8 -> 8, of which waited for: 2 -> 4; matrix products, arithmetic and copies ran while one was open for 8% -> 0% of each run, Pallas kernels for 0% -> 25%
where the time goes in v1:
time: 69.5 us; the launch traced here: 69.2 us
  starting transfers between devices  28.7 us (41%)
  Pallas kernels  24.7 us (36%)
  local copies, waits for them, and re-layouts  10.3 us (15%)
  waiting for transfers between devices  4.65 us (7%)
  between operations  0.74 us (1%)
    ppermute x6, starting transfers between devices, ring(): return lax.ppermute(x, axes, [(i, (i + by) % count) for i in range(count)])  16.3 us
    pallas_call x1, Pallas kernels, on_device(): pl.pallas_call(bulk_kernel, out_shape=shaped(nz, nx, ny), in_specs=[SMEM_...  16.2 us
    all_to_all x1, starting transfers between devices, on_device(): parts = lax.all_to_all(sent, CHIPS, 0, 0, tiled=True)  11.4 us
    unnamed x24, local copies, waits for them, and re-layouts  9.37 us
    ppermute x6, waiting for transfers between devices, ring(): return lax.ppermute(x, axes, [(i, (i + by) % count) for i in range(count)])  3.83 us
    pallas_call x1, Pallas kernels, on_device(): pl.pallas_call(lambda *refs: core_kernel(rows_all, *refs), out_shape=shap...  3.25 us
    pallas_call x1, Pallas kernels, on_device(): pl.pallas_call(window_kernel, out_shape=(shaped(2, rows, ny), shaped(2, n...  2.14 us
    pallas_call x1, Pallas kernels, on_device(): pl.pallas_call(lambda *refs: pack_columns_kernel(nz, *refs), out_shape=(c...  1.73 us
  transfers between devices with their start and end apart: 8, of which 4 were waited for; matrix products, arithmetic and copies ran while one was open for 0% of the time, Pallas kernels for 25%

profile of v1, /device:TPU:1, one launch (start us, length us, event | category | flops | bytes accessed | tf_op | source)
XLA Modules:
  0.0 69.2 jit_solution(11944580162206588640)
XLA Ops:
  0.6 0.0 copy-start
  0.6 1.6 %copy-done = f32[128,32,128]{2,1,0:T(8,128)S(1)} copy-done((f32[128,32,128]{2,1,0:T(8,128)S(1)}, f32[128,32,128]{2,1,0:T(8,128)}, u32[]{:S(2)}) %copy-start) | copy-done | bytes 2097176
  2.2 0.0 copy-start.8
  2.2 0.8 %copy-done.8 = f32[2,32,128]{2,1,0:T(8,128)S(1)} copy-done((f32[2,32,128]{2,1,0:T(8,128)S(1)}, f32[2,32,128]{2,1,0:T(8,128)}, u32[]{:S(2)}) %copy-start.8) | copy-done | bytes 32792
  3.0 0.0 copy-start.2
  3.0 1.7 %columns.1 = (f32[3,32,128]{2,1,0:T(8,128)S(1)}, f32[3,32,128]{2,1,0:T(8,128)S(1)}) custom-call(f32[128,32,128]{2,1,0:T(8,128)S(1)} %copy-done, f32[2,32,128]{2,1,0:T(8,128)S(1)} %copy-done.8), custom_call_target="tpu_custom_call" | custom-call | flops 1000000 | bytes 2097152 | tf_op jit(solution)/shard_map/columns/pallas_call | solution.py:367
  4.7 2.6 %collective-permute-start = (f32[3,32,128]{2,1,0:T(8,128)S(1)}, f32[3,32,128]{2,1,0:T(8,128)S(1)}, u32[]{:S(2)}, u32[]{:S(2)}) collective-permute-start(f32[3,32,128]{2,1,0:T(8,128)S(1)} %get-tuple-element.14.own_right), channel_id=1, source_target_pairs={{0,1},{1,2},{2,3},{3,4},{4,5},{5,6},{6,7},{7,0},{8,9},{9,10},{10,1... | collective-permute-start | bytes 147464 | tf_op jit(solution)/shard_map/ppermute | solution.py:355
  7.3 0.0 copy-start.1
  7.3 0.0 copy-start.9
  7.3 0.0 copy-start.10
  7.3 0.7 collective-permute-start.1
  8.0 0.7 collective-permute-done.from_left
  8.7 2.2 %collective-permute-done.1.from_right = f32[3,32,128]{2,1,0:T(8,128)S(1)} collective-permute-done((f32[3,32,128]{2,1,0:T(8,128)S(1)}, f32[3,32,128]{2,1,0:T(8,128)S(1)}, u32[]{:S(2)}, u32[]{:S(2)}) %collective-permute-start.1) | collective-permute-done | bytes 49184 | tf_op jit(solution)/shard_map/ppermute | solution.py:355
  10.9 1.4 %collective-permute-start.2 = (f32[24,128]{1,0:T(8,128)S(1)}, f32[24,128]{1,0:T(8,128)S(1)}, u32[]{:S(2)}, u32[]{:S(2)}) collective-permute-start(f32[24,128]{1,0:T(8,128)S(1)} %get-tuple-element.17.own_down), channel_id=1, source_target_pairs={{0,8},{8,16},{16,24},{24,32},{32,40},{40,48},{48,56},{56,64},{64,7... | collective-permute-start | bytes 36872 | tf_op jit(solution)/shard_map/ppermute | solution.py:355
  12.2 6.8 %collective-permute-start.3 = (f32[24,128]{1,0:T(8,128)S(1)}, f32[24,128]{1,0:T(8,128)S(1)}, u32[]{:S(2)}, u32[]{:S(2)}) collective-permute-start(f32[24,128]{1,0:T(8,128)S(1)} %get-tuple-element.16.own_up), channel_id=1, source_target_pairs={{0,248},{8,0},{16,8},{24,16},{32,24},{40,32},{48,40},{56,48},{64,5... | collective-permute-start | bytes 36872 | tf_op jit(solution)/shard_map/ppermute | solution.py:355
  19.1 0.0 copy-done.1
  19.1 1.0 %collective-permute-done.2.from_up = f32[24,128]{1,0:T(8,128)S(1)} collective-permute-done((f32[24,128]{1,0:T(8,128)S(1)}, f32[24,128]{1,0:T(8,128)S(1)}, u32[]{:S(2)}, u32[]{:S(2)}) %collective-permute-start.2) | collective-permute-done | bytes 12320 | tf_op jit(solution)/shard_map/ppermute | solution.py:355
  20.1 0.0 collective-permute-done.3.from_down
  20.1 0.0 copy-done.2
  20.1 0.0 copy-done.9
  20.1 0.0 copy-done.10
  20.1 0.0 copy-start.11
  20.1 2.1 %window.1 = (f32[2,64,128]{2,1,0:T(8,128)S(1)}, f32[2,128]{1,0:T(2,128)S(1)}, f32[32,128]{1,0:T(8,128)S(1)}, f32[32,128]{1,0:T(8,128)S(1)}) custom-call(f32[128]{0:T(128)S(1)} %copy-done.10, f32[4,32,128]{2,1,0:T(8,128)S(1)} %slice.18.low, f32[2,32,128]{2,1,0:T(8,128)S(1)} %slice.19.high, f32[2,32,128]{2,1,0:T(8,128)S(1)} %copy-done.9, ...), custom_call_target="tpu_custom_call" | custom-call | flops 10000000 | bytes 4194304 | tf_op jit(solution)/shard_map/window/pallas_call | solution.py:393
  22.2 1.0 %collective-permute-start.6 = (f32[2,128]{1,0:T(2,128)S(1)}, f32[2,128]{1,0:T(2,128)S(1)}, u32[]{:S(2)}, u32[]{:S(2)}) collective-permute-start(f32[2,128]{1,0:T(2,128)S(1)} %get-tuple-element.22), channel_id=1, source_target_pairs={{0,1},{1,0},{2,3},{3,2},{4,5},{5,4},{6,7},{7,6},{8,9},{9,8},{10,11... | collective-permute-start | bytes 3080 | tf_op jit(solution)/shard_map/ppermute | solution.py:404
  23.2 0.8 %collective-permute-done.6 = f32[2,128]{1,0:T(2,128)S(1)} collective-permute-done((f32[2,128]{1,0:T(2,128)S(1)}, f32[2,128]{1,0:T(2,128)S(1)}, u32[]{:S(2)}, u32[]{:S(2)}) %collective-permute-start.6) | collective-permute-done | bytes 1056 | tf_op jit(solution)/shard_map/ppermute | solution.py:404
  24.1 0.7 broadcast_in_dim.5
  24.7 11.4 %all-to-all-start = ((f32[128,2,128]{2,1,0:T(2,128)}), f32[128,2,128]{2,1,0:T(2,128)S(1)}, u32[]{:S(2)}, u32[]{:S(2)}) async-start(f32[128,2,128]{2,1,0:T(2,128)} %broadcast_in_dim.5), calls=%async_computation | async-start | bytes 262144 | tf_op jit(solution)/shard_map/all_to_all | solution.py:406
  36.2 0.2 fusion
  36.4 0.7 collective-permute-start.4
  37.0 4.2 %collective-permute-start.5 = (f32[2,128,128]{2,1,0:T(8,128)S(1)}, f32[2,128,128]{2,1,0:T(8,128)S(1)}, u32[]{:S(2)}, u32[]{:S(2)}) collective-permute-start(f32[2,128,128]{2,1,0:T(8,128)S(1)} %get-tuple-element.21), channel_id=1, source_target_pairs={{0,248},{8,0},{16,8},{24,16},{32,24},{40,32},{48,40},{56,48},{64,5... | collective-permute-start | bytes 393224 | tf_op jit(solution)/shard_map/ppermute | solution.py:355
  41.3 0.0 copy-done.11
  41.3 0.0 copy-start.3
  41.3 1.9 %copy-done.3 = f32[94,2,32,128]{3,2,1,0:T(8,128)S(1)} copy-done((f32[94,2,32,128]{3,2,1,0:T(8,128)S(1)}, f32[94,2,32,128]{3,2,1,0:T(8,128)}, u32[]{:S(2)}) %copy-start.3) | copy-done | bytes 3080216
  43.1 1.4 %split.1 = (bf16[32,96,256]{2,1,0:T(8,128)(2,1)S(1)}, bf16[32,96,256]{2,1,0:T(8,128)(2,1)S(1)}) custom-call(f32[94,64,128]{2,1,0:T(8,128)S(1)} %bitcast.19, f32[2,64,128]{2,1,0:T(8,128)S(1)} %get-tuple-element.23.snaps), custom_call_target="tpu_custom_call" | custom-call | flops 10000000 | bytes 6291456 | tf_op jit(solution)/shard_map/split/pallas_call | solution.py:426
  44.5 0.0 copy-start.4
  44.5 1.1 %copy-done.4 = bf16[32,96,256]{2,1,0:T(8,128)(2,1)} copy-done((bf16[32,96,256]{2,1,0:T(8,128)(2,1)}, bf16[32,96,256]{2,1,0:T(8,128)(2,1)S(1)}, u32[]{:S(2)}) %copy-start.4) | copy-done | bytes 1572888
  45.7 0.0 copy-start.6
  45.7 1.2 %copy-done.6 = bf16[32,96,256]{2,1,0:T(8,128)(2,1)} copy-done((bf16[32,96,256]{2,1,0:T(8,128)(2,1)}, bf16[32,96,256]{2,1,0:T(8,128)(2,1)S(1)}, u32[]{:S(2)}) %copy-start.6) | copy-done | bytes 1572888
  46.8 0.0 collective-permute-done.4.top
  46.8 0.0 collective-permute-done.5.bottom
  46.8 0.1 broadcast_in_dim.4.diff_rows
  46.9 16.2 %bulk.1 = f32[128,32,128]{2,1,0:T(8,128)} custom-call(f32[128]{0:T(128)S(1)} %copy-done.10, f32[128,32,128]{2,1,0:T(8,128)S(1)} %copy-done.1, f32[2,32,128]{2,1,0:T(8,128)S(1)} %copy-done.9, f32[128,128]{1,0:T(8,128)S(1)} %broadcast_in_dim.4.diff_rows, f32[3,32,128]{2,1,0:T(8,128)S(1)} %collective-permute-done.from_left, ...), custom_call_target="tpu_custom_call" | custom-call | flops 100000000 | bytes 4194304 | tf_op jit(solution)/shard_map/bulk/pallas_call | solution.py:414
  63.1 0.0 all-to-all-done
  63.1 0.0 copy-start.5
  63.1 1.4 %copy-done.5 = bf16[32,96,256]{2,1,0:T(8,128)(2,1)S(1)} copy-done((bf16[32,96,256]{2,1,0:T(8,128)(2,1)S(1)}, bf16[32,96,256]{2,1,0:T(8,128)(2,1)}, u32[]{:S(2)}) %copy-start.5) | copy-done | bytes 1572888
  64.5 0.0 copy-start.7
  64.5 1.4 %copy-done.7 = bf16[32,96,256]{2,1,0:T(8,128)(2,1)S(1)} copy-done((bf16[32,96,256]{2,1,0:T(8,128)(2,1)S(1)}, bf16[32,96,256]{2,1,0:T(8,128)(2,1)}, u32[]{:S(2)}) %copy-start.7) | copy-done | bytes 1572888
  65.9 3.2 %core.1 = f32[96,64,128]{2,1,0:T(8,128)} custom-call(f32[32,8,128]{2,1,0:T(8,128)S(1)} %bitcast.20, f32[1,128]{1,0:T(1,128)S(1)} %pad_bitcast_fusion.refs_1_, bf16[32,96,256]{2,1,0:T(8,128)(2,1)S(1)} %copy-done.5, bf16[32,96,256]{2,1,0:T(8,128)(2,1)S(1)} %copy-done.7), custom_call_target="tpu_custom_call" | custom-call | flops 100000000 | bytes 6291456 | tf_op jit(solution)/shard_map/core/pallas_call | solution.py:432
  (6 shorter events, 0.1 us)
Async XLA Ops:
  0.6 1.6 %copy-start = (f32[128,32,128]{2,1,0:T(8,128)S(1)}, f32[128,32,128]{2,1,0:T(8,128)}, u32[]{:S(2)}) copy-start(f32[128,32,128]{2,1,0:T(8,128)} %tracer.1) | copy-start | bytes 6291460
  2.2 0.8 %copy-start.8 = (f32[2,32,128]{2,1,0:T(8,128)S(1)}, f32[2,32,128]{2,1,0:T(8,128)}, u32[]{:S(2)}) copy-start(f32[2,32,128]{2,1,0:T(8,128)} %velocity.5) | copy-start | bytes 98308
  3.0 17.1 %copy-start.2 = (f32[94,2,32,128]{3,2,1,0:T(8,128)S(1)}, f32[94,2,32,128]{3,2,1,0:T(8,128)}, u32[]{:S(2)}) copy-start(f32[94,2,32,128]{3,2,1,0:T(8,128)} %param.9) | copy-start | bytes 9240580
  4.7 3.9 %collective-permute-start = (f32[3,32,128]{2,1,0:T(8,128)S(1)}, f32[3,32,128]{2,1,0:T(8,128)S(1)}, u32[]{:S(2)}, u32[]{:S(2)}) collective-permute-start(f32[3,32,128]{2,1,0:T(8,128)S(1)} %get-tuple-element.14.own_right), channel_id=1, source_target_pairs={{0,1},{1,2},{2,3},{3,4},{4,5},{5,6},{6,7},{7,0},{8,9},{9,10},{10,1... | collective-permute-start | bytes 147464 | tf_op jit(solution)/shard_map/ppermute | solution.py:355
  7.3 11.7 %copy-start.1 = (f32[128,32,128]{2,1,0:T(8,128)S(1)}, f32[128,32,128]{2,1,0:T(8,128)}, u32[]{:S(2)}) copy-start(f32[128,32,128]{2,1,0:T(8,128)} %tracer.1) | copy-start | bytes 6291460
  7.3 12.7 %copy-start.9 = (f32[2,32,128]{2,1,0:T(8,128)S(1)}, f32[2,32,128]{2,1,0:T(8,128)}, u32[]{:S(2)}) copy-start(f32[2,32,128]{2,1,0:T(8,128)} %velocity.5) | copy-start | bytes 98308
  7.3 12.7 %copy-start.10 = (f32[128]{0:T(128)S(1)}, f32[128]{0:T(128)}, u32[]{:S(2)}) copy-start(f32[128]{0:T(128)} %diff.3) | copy-start | bytes 1540
  7.3 3.5 %collective-permute-start.1 = (f32[3,32,128]{2,1,0:T(8,128)S(1)}, f32[3,32,128]{2,1,0:T(8,128)S(1)}, u32[]{:S(2)}, u32[]{:S(2)}) collective-permute-start(f32[3,32,128]{2,1,0:T(8,128)S(1)} %get-tuple-element.15.own_left), channel_id=1, source_target_pairs={{0,7},{1,0},{2,1},{3,2},{4,3},{5,4},{6,5},{7,6},{8,15},{9,8},{10,9... | collective-permute-start | bytes 147464 | tf_op jit(solution)/shard_map/ppermute | solution.py:355
  10.9 9.2 %collective-permute-start.2 = (f32[24,128]{1,0:T(8,128)S(1)}, f32[24,128]{1,0:T(8,128)S(1)}, u32[]{:S(2)}, u32[]{:S(2)}) collective-permute-start(f32[24,128]{1,0:T(8,128)S(1)} %get-tuple-element.17.own_down), channel_id=1, source_target_pairs={{0,8},{8,16},{16,24},{24,32},{32,40},{40,48},{48,56},{56,64},{64,7... | collective-permute-start | bytes 36872 | tf_op jit(solution)/shard_map/ppermute | solution.py:355
  12.2 7.8 %collective-permute-start.3 = (f32[24,128]{1,0:T(8,128)S(1)}, f32[24,128]{1,0:T(8,128)S(1)}, u32[]{:S(2)}, u32[]{:S(2)}) collective-permute-start(f32[24,128]{1,0:T(8,128)S(1)} %get-tuple-element.16.own_up), channel_id=1, source_target_pairs={{0,248},{8,0},{16,8},{24,16},{32,24},{40,32},{48,40},{56,48},{64,5... | collective-permute-start | bytes 36872 | tf_op jit(solution)/shard_map/ppermute | solution.py:355
  20.1 21.2 %copy-start.11 = (f32[94]{0:T(128)S(1)}, f32[94]{0:T(128)}, u32[]{:S(2)}) copy-start(f32[94]{0:T(128)} %param.8) | copy-start | bytes 1132
  22.2 1.8 %collective-permute-start.6 = (f32[2,128]{1,0:T(2,128)S(1)}, f32[2,128]{1,0:T(2,128)S(1)}, u32[]{:S(2)}, u32[]{:S(2)}) collective-permute-start(f32[2,128]{1,0:T(2,128)S(1)} %get-tuple-element.22), channel_id=1, source_target_pairs={{0,1},{1,0},{2,3},{3,2},{4,5},{5,4},{6,7},{7,6},{8,9},{9,8},{10,11... | collective-permute-start | bytes 3080 | tf_op jit(solution)/shard_map/ppermute | solution.py:404
  24.7 38.4 %all-to-all-start = ((f32[128,2,128]{2,1,0:T(2,128)}), f32[128,2,128]{2,1,0:T(2,128)S(1)}, u32[]{:S(2)}, u32[]{:S(2)}) async-start(f32[128,2,128]{2,1,0:T(2,128)} %broadcast_in_dim.5), calls=%async_computation | async-start | bytes 262144 | tf_op jit(solution)/shard_map/all_to_all | solution.py:406
  36.4 10.5 %collective-permute-start.4 = (f32[2,128,128]{2,1,0:T(8,128)S(1)}, f32[2,128,128]{2,1,0:T(8,128)S(1)}, u32[]{:S(2)}, u32[]{:S(2)}) collective-permute-start(f32[2,128,128]{2,1,0:T(8,128)S(1)} %get-tuple-element.20), channel_id=1, source_target_pairs={{0,8},{8,16},{16,24},{24,32},{32,40},{40,48},{48,56},{56,64},{64,7... | collective-permute-start | bytes 393224 | tf_op jit(solution)/shard_map/ppermute | solution.py:355
  37.0 9.8 %collective-permute-start.5 = (f32[2,128,128]{2,1,0:T(8,128)S(1)}, f32[2,128,128]{2,1,0:T(8,128)S(1)}, u32[]{:S(2)}, u32[]{:S(2)}) collective-permute-start(f32[2,128,128]{2,1,0:T(8,128)S(1)} %get-tuple-element.21), channel_id=1, source_target_pairs={{0,248},{8,0},{16,8},{24,16},{32,24},{40,32},{48,40},{56,48},{64,5... | collective-permute-start | bytes 393224 | tf_op jit(solution)/shard_map/ppermute | solution.py:355
  41.3 1.9 %copy-start.3 = (f32[94,2,32,128]{3,2,1,0:T(8,128)S(1)}, f32[94,2,32,128]{3,2,1,0:T(8,128)}, u32[]{:S(2)}) copy-start(f32[94,2,32,128]{3,2,1,0:T(8,128)} %param.9) | copy-start | bytes 9240580
  44.5 1.1 %copy-start.4 = (bf16[32,96,256]{2,1,0:T(8,128)(2,1)}, bf16[32,96,256]{2,1,0:T(8,128)(2,1)S(1)}, u32[]{:S(2)}) copy-start(bf16[32,96,256]{2,1,0:T(8,128)(2,1)S(1)} %get-tuple-element.24.refs_2_) | copy-start | bytes 4718596
  45.7 1.2 %copy-start.6 = (bf16[32,96,256]{2,1,0:T(8,128)(2,1)}, bf16[32,96,256]{2,1,0:T(8,128)(2,1)S(1)}, u32[]{:S(2)}) copy-start(bf16[32,96,256]{2,1,0:T(8,128)(2,1)S(1)} %get-tuple-element.25.refs_3_) | copy-start | bytes 4718596
  63.1 1.4 %copy-start.5 = (bf16[32,96,256]{2,1,0:T(8,128)(2,1)S(1)}, bf16[32,96,256]{2,1,0:T(8,128)(2,1)}, u32[]{:S(2)}) copy-start(bf16[32,96,256]{2,1,0:T(8,128)(2,1)} %copy-done.4) | copy-start | bytes 4718596
  64.5 1.4 %copy-start.7 = (bf16[32,96,256]{2,1,0:T(8,128)(2,1)S(1)}, bf16[32,96,256]{2,1,0:T(8,128)(2,1)}, u32[]{:S(2)}) copy-start(bf16[32,96,256]{2,1,0:T(8,128)(2,1)} %copy-done.6) | copy-start | bytes 4718596

commit v2 on v1

v2 whole, which is shorter than its diff:
```python
import math

import jax
import jax.numpy as jnp
from jax import lax
from jax.experimental import pallas as pl
from jax.experimental.pallas import tpu as pltpu
from jax.sharding import Mesh
from jax.sharding import PartitionSpec as P


F32 = jnp.float32
BF16 = jnp.bfloat16
GX = ("z", "y")
GY = ("x", "c")
CHIPS = ("z", "y", "x")
ROOT_ITERS = 5
SHIFTS = 2**ROOT_ITERS
POLES = SHIFTS // 2 - 1
VMEM = pltpu.VMEM


def lanes_of(shape):
    return lax.broadcasted_iota(jnp.int32, shape, len(shape) - 1)


def rows_of(shape):
    return lax.broadcasted_iota(jnp.int32, shape, len(shape) - 2)


def step(c, xm, xp, ym, yp, zm, zp, d, vxp, vxn, vyp, vyn):
    spread = (xm + xp) + (ym + yp) + (zm + zp) - 6.0 * c
    carried = (vxp * (c - xm) + vxn * (xp - c)) + (vyp * (c - ym) + vyn * (yp - c))
    return c + d * spread - carried


def signed_parts(vx, vy):
    return jnp.maximum(vx, 0.0), jnp.minimum(vx, 0.0), jnp.maximum(vy, 0.0), jnp.minimum(vy, 0.0)


def before(c, ghost, axis):
    at = lax.broadcasted_iota(jnp.int32, c.shape, axis)
    return jnp.where(at == 0, ghost, pltpu.roll(c, 1, axis))


def after(c, ghost, axis):
    n = c.shape[axis]
    at = lax.broadcasted_iota(jnp.int32, c.shape, axis)
    return jnp.where(at == n - 1, ghost, pltpu.roll(c, n - 1, axis))


def pack_columns_kernel(
    chunks, tracer_hbm, velocity_hbm, left, right, near, top, bottom, tracer, velocity, sems
):
    nz, nx, ny = tracer.shape
    size = nz // chunks
    loads = [
        pltpu.make_async_copy(
            tracer_hbm.at[pl.ds(i * size, size)], tracer.at[pl.ds(i * size, size)], sems.at[i]
        )
        for i in range(chunks)
    ]
    loads.append(pltpu.make_async_copy(velocity_hbm, velocity, sems.at[chunks]))
    for load in loads:
        load.start()
    lane = lanes_of((nx, ny))

    def level(z, carry):
        a, b, y, w = carry
        r = pltpu.roll(tracer[z], z, 1)
        rel = (lane - z) & (ny - 1)
        a = jnp.where(rel == 0, r, a)
        b = jnp.where(rel == 1, r, b)
        y = jnp.where(rel == ny - 1, r, y)
        w = jnp.where(rel == ny - 2, r, w)
        return a, b, y, w

    carry = (jnp.zeros((nx, ny), F32),) * 4
    for i in range(chunks):
        loads[i].wait()
        carry = lax.fori_loop(i * size, (i + 1) * size, level, carry, unroll=8)
    a, b, y, w = carry
    left[0] = a
    left[1] = pltpu.roll(b, ny - 1, 1)
    right[0] = pltpu.roll(y, 1, 1)
    right[1] = pltpu.roll(w, 2, 1)
    loads[chunks].wait()
    vx, vy = velocity[0], velocity[1]
    left[2] = jnp.where(lane == 0, vx, pltpu.roll(vy, 1, 1))
    right[2] = jnp.where(lane == ny - 1, vx, pltpu.roll(vy, ny - 1, 1))
    near[0:2] = tracer[nz - 2 : nz]
    near[2:6] = tracer[0:4]
    for i in range(2):
        top[i] = tracer[:, i, :]
        bottom[i] = tracer[:, nx - 1 - i, :]


def pack_rows_kernel(near, velocity, from_left, from_right, up, down):
    nx, ny = near.shape[1:]
    for edge, inner, out in ((0, 1, up), (nx - 1, nx - 2, down)):
        for s in range(6):
            out[s : s + 1, :] = near[s, edge : edge + 1, :]
            out[8 + s : 9 + s, :] = near[s, inner : inner + 1, :]
        for s in (6, 7, 14, 15, 20, 21, 22, 23):
            out[s : s + 1, :] = jnp.zeros((1, ny), F32)
        out[16:17, :] = velocity[0, edge : edge + 1, :]
        out[17:18, :] = velocity[1, edge : edge + 1, :]
        out[18:19, :] = from_left[0, edge : edge + 1, :]
        out[19:20, :] = from_right[0, edge : edge + 1, :]


def window_kernel(
    diff, near, velocity, diff_row, own_left, own_right, from_left, from_right,
    own_up, own_down, from_up, from_down, basis,
    kept_hbm, sums, snaps, sides, q0, q1, sems,
):
    nz, nx, ny = diff.shape[0], near.shape[1], near.shape[2]
    count = basis.shape[0]
    dz = diff_row[...]
    for gin, inner, outer, corner, vx_at, vy_at, out in (
        (from_left, None, own_left, 18, ny - 1, ny - 2, sides.at[0:nx]),
        (from_right, own_right, None, 19, 0, 1, sides.at[nx : 2 * nx]),
    ):
        c = gin[0]
        ym = gin[1] if inner is None else inner[0]
        yp = gin[1] if outer is None else outer[0]
        vx = gin[2][:, vx_at : vx_at + 1]
        vy = gin[2][:, vy_at : vy_at + 1]
        parts = signed_parts(vx, vy)
        xm = before(c, from_up[corner : corner + 1, :], 0)
        xp = after(c, from_down[corner : corner + 1, :], 0)
        out[...] = step(c, xm, xp, ym, yp, pltpu.roll(c, 1, 1), pltpu.roll(c, nz - 1, 1), dz, *parts)

    sub = rows_of((8, ny))
    lane = lanes_of((8, ny))
    d_rows = jnp.where(sub == 2, diff[0], diff[1])
    ghost_rows = []
    for gin, own, top in ((from_up, own_up, True), (from_down, own_down, False)):
        c = gin[0:8, :]
        beyond, inside = gin[8:16, :], own[0:8, :]
        xm, xp = (beyond, inside) if top else (inside, beyond)
        west = jnp.where(sub == 2, gin[18:19, 0:1], gin[18:19, 1:2])
        east = jnp.where(sub == 2, gin[19:20, 0:1], gin[19:20, 1:2])
        parts = signed_parts(gin[16:17, :], gin[17:18, :])
        ghost_rows.append(
            step(c, xm, xp, before(c, west, 1), after(c, east, 1),
                 pltpu.roll(c, 1, 0), pltpu.roll(c, 7, 0), d_rows, *parts)
        )

    parts = signed_parts(velocity[0], velocity[1])
    u = [near[s] for s in range(6)]
    first = []
    for s in range(1, 5):
        z = (s - 2) % nz
        c = u[s]
        xm = before(c, from_up[s : s + 1, :], 0)
        xp = after(c, from_down[s : s + 1, :], 0)
        ym = before(c, from_left[0][:, z : z + 1], 1)
        yp = after(c, from_right[0][:, z : z + 1], 1)
        first.append(step(c, xm, xp, ym, yp, u[s - 1], u[s + 1], diff[z], *parts))
    for z in range(2):
        c = first[z + 1]
        snaps[0, z * nx : (z + 1) * nx, :] = c
        xm = before(c, ghost_rows[0][z + 2 : z + 3, :], 0)
        xp = after(c, ghost_rows[1][z + 2 : z + 3, :], 0)
        ym = before(c, sides[0:nx, z : z + 1], 1)
        yp = after(c, sides[nx : 2 * nx, z : z + 1], 1)
        snaps[1, z * nx : (z + 1) * nx, :] = step(
            c, xm, xp, ym, yp, first[z], first[z + 2], diff[z], *parts
        )

    rows = 2 * nx
    pieces = rows // 8
    sides[rows : rows + 8] = from_up[16:24, :]
    sides[rows + 8 : rows + 16] = from_down[16:24, :]
    keep = [
        pltpu.make_async_copy(ref, kept_hbm.at[pl.ds(at, ref.shape[0])], sems.at[i])
        for i, (ref, at) in enumerate(
            ((snaps.at[0], 0), (snaps.at[1], rows), (sides, 2 * rows))
        )
    ]
    for copy in keep:
        copy.start()

    def folded(a, b):
        total = a[0:8, :] * b[0:8, :]
        for i in range(1, pieces):
            total = total + a[8 * i : 8 * i + 8, :] * b[8 * i : 8 * i + 8, :]
        return jnp.sum(total, axis=0, keepdims=True)

    q0[...] = jnp.zeros_like(q0)
    q1[...] = jnp.zeros_like(q1)

    def product(k, carry):
        b = basis[k]
        q0[pl.ds(k, 1), :] = folded(b, snaps[0])
        q1[pl.ds(k, 1), :] = folded(b, snaps[1])
        return carry

    lax.fori_loop(0, count, product, 0, unroll=2)
    cross = folded(snaps[0], snaps[1])
    q0[count : count + 1, :] = folded(snaps[0], snaps[0])
    q0[count + 1 : count + 2, :] = cross
    q1[count : count + 1, :] = cross
    q1[count + 1 : count + 2, :] = folded(snaps[1], snaps[1])
    ones = jnp.ones((8, ny), F32)
    over_lanes = (((1,), (1,)), ((), ()))
    for m, q in enumerate((q0, q1)):
        line = lax.dot_general(
            ones, q[...], over_lanes, precision=lax.Precision.HIGHEST, preferred_element_type=F32
        )
        sums[m : m + 1, :] = line[0:1, :]
    for copy in keep:
        copy.wait()


def split(basis, snaps, upper, lower):
    _, rows, ny = basis.shape
    for b in range(rows // 8):
        part = slice(8 * b, 8 * b + 8)
        later = slice(rows + 8 * b, rows + 8 * b + 8)
        x = jnp.concatenate([basis[:, part, :], snaps[part, :][None], snaps[later, :][None]], axis=0)
        x = jnp.swapaxes(x, 0, 1)
        for i in range(8):
            pair, half = (8 * b + i) // 2, i % 2
            v = x[i]
            hi = v.astype(BF16)
            upper[pair, :, half * ny : (half + 1) * ny] = hi
            lower[pair, :, half * ny : (half + 1) * ny] = (v - hi.astype(F32)).astype(BF16)


def load_kernel(src, dst, sem):
    copy = pltpu.make_async_copy(src, dst, sem)
    copy.start()
    copy.wait()


def bulk_kernel(
    diff, tracer, basis, kept_hbm, top_hbm, bottom_hbm, velocity, diff_row, from_left, from_right,
    singular, out, upper, lower, line, now, then, vectors, kept, top, bottom, sems,
):
    nz, nx, ny = tracer.shape
    count, _ = basis.shape[:2]
    chunks = sems.shape[0] - 5
    size = nz // chunks
    tile = pl.ds(8, nx)
    loads = [
        pltpu.make_async_copy(src, dst, sems.at[chunks + i])
        for i, (src, dst) in enumerate((
            (tracer, now.at[:, tile, :]), (top_hbm, top), (bottom_hbm, bottom),
            (kept_hbm, kept), (basis, vectors),
        ))
    ]
    for load in loads:
        load.start()
    line[...] = jnp.zeros_like(line)
    line[0:1, :count] = singular[...]
    eye = rows_of((nz, nz)) == lanes_of((nz, nz))
    d_all = jnp.sum(jnp.where(eye, diff_row[...], 0.0), axis=1, keepdims=True)
    edges = ((top, 0, True, 6 * nx), (bottom, nx - 1, False, 6 * nx + 8))

    def ghost_rows():
        for bulk, own, is_top, at in edges:
            gin = kept[at : at + 8, :]
            c, beyond, inside = bulk[0], bulk[1], now[:, 8 + own, :]
            xm, xp = (beyond, inside) if is_top else (inside, beyond)
            west = jnp.sum(jnp.where(eye, gin[2:3, :], 0.0), axis=1, keepdims=True)
            east = jnp.sum(jnp.where(eye, gin[3:4, :], 0.0), axis=1, keepdims=True)
            parts = signed_parts(gin[0:1, :], gin[1:2, :])
            then[:, 7 if is_top else 8 + nx, :] = step(
                c, xm, xp, before(c, west, 1), after(c, east, 1),
                pltpu.roll(c, 1, 0), pltpu.roll(c, nz - 1, 0), d_all, *parts
            )

    xp_pull, xn_pull, yp_pull, yn_pull = signed_parts(velocity[0], velocity[1])
    stay = 1.0 - (xp_pull - xn_pull) - (yp_pull - yn_pull)
    xn_pull, yn_pull = -xn_pull, -yn_pull
    lane = lanes_of((nx, ny))
    is_even = (lane & 1) == 0

    def sweep(src, dst, col_left, col_right, after_chunk):
        shifted = pltpu.roll(col_right, nz - 1, 1)
        columns = (
            jnp.where(is_even, col_left, shifted), jnp.where(is_even, shifted, col_left),
        )

        def level(z, columns_now, zm, c):
            zp = src[(z + 1) & (nz - 1), tile, :]
            side = pltpu.roll(columns_now, (nz - z) & (nz - 1), 1)
            ym = jnp.where(lane == 0, side, pltpu.roll(c, 1, 1))
            yp = jnp.where(lane == ny - 1, side, pltpu.roll(c, ny - 1, 1))
            xm = src[z, pl.ds(7, nx), :]
            xp = src[z, pl.ds(9, nx), :]
            d = diff[z]
            moved = (xp_pull * xm + xn_pull * xp) + (yp_pull * ym + yn_pull * yp)
            spread = ((xm + xp) + (ym + yp)) + (zm + zp)
            dst[z, tile, :] = (c * (stay - 6.0 * d) + moved) + d * spread
            return c, zp

        def pair(i, carry):
            zm, c = carry
            zm, c = level(2 * i, columns[0], zm, c)
            return level(2 * i + 1, columns[1], zm, c)

        carry = (src[nz - 1, tile, :], src[0, tile, :])
        for k in range(chunks):
            carry = lax.fori_loop(k * size // 2, (k + 1) * size // 2, pair, carry, unroll=2)
            after_chunk(k)

    for load in loads[:4]:
        load.wait()
    now[:, 7, :] = top[0]
    now[:, 8 + nx, :] = bottom[0]
    sweep(now, then, from_left[0], from_right[0], lambda k: None)
    ghost_rows()
    stores = []

    def store(k):
        part = pl.ds(k * size, size)
        copy = pltpu.make_async_copy(now.at[part, tile, :], out.at[part], sems.at[k])
        copy.start()
        stores.append(copy)

    sweep(then, now, kept[4 * nx : 5 * nx, :], kept[5 * nx : 6 * nx, :], store)
    loads[4].wait()
    split(vectors, kept, upper, lower)
    for copy in stores:
        copy.wait()


def spread_kernel(mine, other, out):
    both = mine[...] + other[...]
    out[...] = jnp.broadcast_to(both[None], out.shape)


def core_kernel(rows_all, parts, singular, upper, lower, out, block, sems):
    count = out.shape[0] - 2
    n = parts.shape[2]
    total = jnp.sum(parts[...], axis=0)
    total = total + pltpu.roll(total, 2, 0)
    total = total + pltpu.roll(total, 4, 0)
    total = total * (1.0 / rows_all)
    lane = lanes_of((1, n))
    zero = jnp.zeros((1, n), F32)

    def add(x):
        return jnp.sum(x, axis=1, keepdims=True)

    def pick(x, at):
        return add(jnp.where(lane == at, x, zero))

    p0 = jnp.where(lane < count, total[0:1, :], zero)
    p1 = jnp.where(lane < count, total[1:2, :], zero)
    g00 = pick(total[0:1, :], count) - add(p0 * p0) + 1e-06
    g01 = pick(total[0:1, :], count + 1) - add(p0 * p1)
    g11 = pick(total[1:2, :], count + 1) - add(p1 * p1) + 1e-06
    r11 = jnp.sqrt(g00)
    r12 = g01 / r11
    r22 = jnp.sqrt(g11 - r12 * r12)
    u0 = jnp.where(lane == count, r11, p0)
    u1 = jnp.where(lane == count, r12, jnp.where(lane == count + 1, r22, p1))
    s = singular[0:1, :]
    squares = s * s
    sigma = add(squares + u0 * u0 + u1 * u1) / (count + 2)
    root = jnp.sqrt(sigma)
    d = squares / sigma
    v0 = u0 / root
    v1 = u1 / root

    half = POLES + 1
    row = rows_of((half, n))
    pole = jnp.zeros((half, n), F32)
    for j in range(POLES):
        pole = jnp.where(row == j, math.tan(math.pi * (j + 1) / SHIFTS) ** 2, pole)
    last = row == POLES
    pole = jnp.where(last, 1.0, pole)
    inverse = jnp.where(last, 1.0, 1.0 / (d + pole))
    weight = 2.0 * (1.0 + pole)
    w0 = inverse * v0
    w1 = inverse * v1
    last_one = last[:, 0:1]
    a = jnp.where(last_one, 1.0, 1.0 + add(w0 * v0))
    b = jnp.where(last_one, 0.0, add(w0 * v1))
    c = jnp.where(last_one, 1.0, 1.0 + add(w1 * v1))
    e = b / a
    c = c - b * e
    strength = jnp.where(last, 1.0, weight * pole)
    w1 = jnp.sqrt(strength / c) * (w1 - e * w0)
    w0 = jnp.sqrt(strength / a) * w0
    low_rank = jnp.concatenate([w0, w1], axis=0)
    gains = 1.0 + d + jnp.sum(jnp.where(last, 0.0, weight * d * inverse), axis=0, keepdims=True)
    square = (n, n)
    core = lax.dot_general(
        low_rank, low_rank, (((0,), (0,)), ((), ())),
        precision=lax.Precision.HIGHEST, preferred_element_type=F32,
    )
    core = core + jnp.where(rows_of(square) == lanes_of(square), gains, 0.0)
    core = core * (root * (1.0 / SHIFTS))
    t0 = jnp.where(lane == count, 1.0, -p0) / r11
    q_lane = jnp.where(lane == count + 1, 1.0, -p1)
    t1 = (q_lane - r12 * t0) / r22
    full = jnp.where(lanes_of(square) < count, core, 0.0)
    full = full + core[:, count : count + 1] * t0 + core[:, count + 1 : count + 2] * t1
    full = full[: count + 2, : count + 2]
    hi = full.astype(BF16)
    lo = (full - hi.astype(F32)).astype(BF16)
    both = jnp.concatenate([hi, lo], axis=0)

    blocks = block.shape[1] // 8
    size = count + 2
    copies = []
    for b in range(blocks):
        tiles = []
        for pair in range(4 * b, 4 * b + 4):
            top = upper[pair]
            r = jnp.dot(both, top, preferred_element_type=F32)
            r = r[:size] + r[size:] + jnp.dot(hi, lower[pair], preferred_element_type=F32)
            tiles.append(r[:, :n])
            tiles.append(r[:, n:])
        block[:, 8 * b : 8 * b + 8, :] = jnp.swapaxes(jnp.stack(tiles), 0, 1)
        copy = pltpu.make_async_copy(
            block.at[:, pl.ds(8 * b, 8), :], out.at[:, pl.ds(8 * b, 8), :], sems.at[b]
        )
        copy.start()
        copies.append(copy)
    for copy in copies:
        copy.wait()


def whole(n):
    return [pl.BlockSpec(memory_space=VMEM)] * n


SMEM_SPEC = pl.BlockSpec(memory_space=pltpu.SMEM)


def shaped(*shape, dtype=F32):
    return jax.ShapeDtypeStruct(shape, dtype)


def in_hbm(x):
    return pltpu.with_memory_space_constraint(x, pltpu.HBM)


def cost(flops, moved):
    return pl.CostEstimate(flops=flops, bytes_accessed=moved, transcendentals=0)


def limit(mib):
    return pltpu.CompilerParams(vmem_limit_bytes=mib * 2**20)


def ring(x, axes, by):
    count = lax.axis_size(axes)
    return lax.ppermute(x, axes, [(i, (i + by) % count) for i in range(count)])


def steps(tracer, velocity, diffusivity, singular, basis_vectors):
    nz, nx, ny = tracer.shape
    count, window = basis_vectors.shape[:2]
    rows = window * nx
    basis = basis_vectors.reshape(count, rows, ny)
    rows_all = rows * ny * lax.axis_size(GX) * lax.axis_size(GY)
    chips = lax.axis_size(CHIPS)
    diff_row = diffusivity.reshape(1, nz)

    columns = shaped(3, nx, ny)
    bulk_rows = shaped(2, nz, ny)
    own_left, own_right, near, top_rows, bottom_rows = pl.pallas_call(
        lambda *refs: pack_columns_kernel(4, *refs),
        out_shape=(columns, columns, shaped(6, nx, ny), bulk_rows, bulk_rows),
        in_specs=[pl.BlockSpec(memory_space=pltpu.HBM)] * 2, out_specs=tuple(whole(5)),
        scratch_shapes=[
            VMEM((nz, nx, ny), F32), VMEM((2, nx, ny), F32), pltpu.SemaphoreType.DMA((5,)),
        ],
        compiler_params=limit(8), cost_estimate=cost(10**6, 2 * 2**20), name="columns",
    )(in_hbm(tracer), in_hbm(velocity))
    from_right = ring(own_left, GY, -1)
    from_left = ring(own_right, GY, 1)
    vectors = pl.pallas_call(
        load_kernel, out_shape=shaped(count, rows, ny),
        in_specs=[pl.BlockSpec(memory_space=pltpu.HBM)], out_specs=whole(1)[0],
        scratch_shapes=[pltpu.SemaphoreType.DMA],
        compiler_params=limit(2), cost_estimate=cost(0, 6 * 2**20), name="load",
    )(in_hbm(basis))

    edge = shaped(24, ny)
    own_up, own_down = pl.pallas_call(
        pack_rows_kernel, out_shape=(edge, edge), in_specs=whole(4), out_specs=tuple(whole(2)),
        compiler_params=limit(4), cost_estimate=cost(10**4, 2**17), name="edges",
    )(near, velocity, from_left, from_right)
    from_down = ring(own_up, GX, -1)
    from_up = ring(own_down, GX, 1)
    top_sent, bottom_sent, _ = lax.optimization_barrier((top_rows, bottom_rows, own_up))
    bottom = ring(top_sent, GX, -1)
    top = ring(bottom_sent, GX, 1)

    kept, local = pl.pallas_call(
        window_kernel,
        out_shape=(pltpu.HBM((6 * nx + 16, ny), F32), shaped(2, ny)),
        in_specs=[SMEM_SPEC] + whole(12),
        out_specs=(pl.BlockSpec(memory_space=pltpu.HBM), *whole(1)),
        scratch_shapes=[
            VMEM((2, rows, ny), F32), VMEM((rows + 16, ny), F32), VMEM((ny, ny), F32),
            VMEM((ny, ny), F32), pltpu.SemaphoreType.DMA((3,)),
        ],
        compiler_params=limit(4), cost_estimate=cost(10**7, 4 * 2**20), name="window",
    )(
        diffusivity, near, velocity, diff_row, own_left, own_right,
        from_left, from_right, own_up, own_down, from_up, from_down, vectors,
    )

    other = lax.ppermute(local, "c", [(0, 1), (1, 0)])
    sent = pl.pallas_call(
        spread_kernel, out_shape=shaped(chips, 2, ny), in_specs=whole(2), out_specs=whole(1)[0],
        compiler_params=limit(4), cost_estimate=cost(10**4, 2**17), name="spread",
    )(local, other)
    parts = lax.all_to_all(sent, CHIPS, 0, 0, tiled=True)

    hbm_space, any_space = (pl.BlockSpec(memory_space=m) for m in (pltpu.HBM, pl.ANY))
    halves = shaped(rows // 2, count + 2, 2 * ny, dtype=BF16)
    padded = VMEM((nz, nx + 16, ny), F32)
    tracer_next, upper, lower, line = pl.pallas_call(
        bulk_kernel,
        out_shape=(shaped(nz, nx, ny), halves, halves, shaped(8, ny)),
        in_specs=[SMEM_SPEC] + [hbm_space] * 3 + [any_space] * 2 + whole(5),
        out_specs=(any_space, *whole(3)),
        scratch_shapes=[
            padded, padded, VMEM((count, rows, ny), F32), VMEM((6 * nx + 16, ny), F32),
            VMEM((2, nz, ny), F32), VMEM((2, nz, ny), F32), pltpu.SemaphoreType.DMA((9,)),
        ],
        compiler_params=limit(16), cost_estimate=cost(10**8, 10 * 2**20), name="bulk",
    )(
        diffusivity, in_hbm(tracer), in_hbm(basis), in_hbm(kept), top, bottom,
        velocity, diff_row, from_left, from_right, singular.reshape(1, count),
    )

    basis_next = pl.pallas_call(
        lambda *refs: core_kernel(rows_all, *refs),
        out_shape=shaped(count + 2, rows, ny),
        in_specs=whole(4), out_specs=pl.BlockSpec(memory_space=pl.ANY),
        scratch_shapes=[
            VMEM((count + 2, rows, ny), F32),
            pltpu.SemaphoreType.DMA((rows // 8,)),
        ],
        compiler_params=limit(16), cost_estimate=cost(10**8, 6 * 2**20), name="core",
    )(
        parts.reshape(chips // 4, 8, ny), line, upper, lower,
    )
    return tracer_next, basis_next.reshape(count + 2, window, nx, ny)


def solution(mesh):
    finer = Mesh(mesh.devices.reshape(8, 4, 4, 2), ("z", "y", "x", "c"))
    in_specs = (P(None, GX, GY), P(None, GX, GY), P(), P(), P(None, None, GX, GY))
    out_specs = (P(None, GX, GY), P(None, None, GX, GY))
    return jax.shard_map(steps, mesh=finer, in_specs=in_specs, out_specs=out_specs, check_vma=False)
```

time: 69.5 us -> 62.1 us (0.89)
  local copies, waits for them, and re-layouts: 10.3 us -> 0.01 us
  waiting for transfers between devices: 4.65 us -> 7.69 us
  starting transfers between devices: 28.7 us -> 30.4 us
  Pallas kernels: 24.7 us -> 23.1 us
    unnamed x24 -> x6, local copies, waits for them, and re-layouts: 9.37 us -> 0.01 us
    ppermute x1, starting transfers between devices: 1 us -> 4.37 us  [steps(): other = lax.ppermute(local, 'c', [(0, 1), (1, 0)])]
    ppermute x6, waiting for transfers between devices: 3.83 us -> 6.87 us  [ring(): return lax.ppermute(x, axes, [(i, (i + by) % count) for i in range(count)])]
    all_to_all x1, starting transfers between devices: 11.4 us -> 9.76 us  [steps(): parts = lax.all_to_all(sent, CHIPS, 0, 0, tiled=True)]
    pallas_call x6 -> x7, Pallas kernels: 24.7 us -> 23.1 us  [the longest x1 12 us: steps(): pl.pallas_call(bulk_kernel, out_shape=(shaped(nz, nx, ny), halves, halves...]
    broadcast_in_dim x2 -> x0, local copies, waits for them, and re-layouts: 0.75 us -> none  [the longest x1 0.68 us: on_device(): sent = jnp.broadcast_to(pair[None], (chips, 2, ny))]
  transfers between devices with their start and end apart: 8 -> 8, of which waited for: 4 -> 4; matrix products, arithmetic and copies ran while one was open for 0% -> 0% of each run, Pallas kernels for 25% -> 22%
where the time goes in v2:
time: 62.1 us; the launch traced here: 61.9 us
  starting transfers between devices  30.4 us (49%)
  Pallas kernels  23.1 us (37%)
  waiting for transfers between devices  7.69 us (12%)
  between operations  0.73 us (1%)
    ppermute x6, starting transfers between devices, ring(): return lax.ppermute(x, axes, [(i, (i + by) % count) for i in range(count)])  16.3 us
    pallas_call x1, Pallas kernels, steps(): pl.pallas_call(bulk_kernel, out_shape=(shaped(nz, nx, ny), halves, halves...  12 us
    all_to_all x1, starting transfers between devices, steps(): parts = lax.all_to_all(sent, CHIPS, 0, 0, tiled=True)  9.76 us
    ppermute x6, waiting for transfers between devices, ring(): return lax.ppermute(x, axes, [(i, (i + by) % count) for i in range(count)])  6.87 us
    ppermute x1, starting transfers between devices, steps(): other = lax.ppermute(local, 'c', [(0, 1), (1, 0)])  4.37 us
    pallas_call x1, Pallas kernels, steps(): pl.pallas_call(lambda *refs: core_kernel(rows_all, *refs), out_shape=shap...  3.25 us
    pallas_call x1, Pallas kernels, steps(): pl.pallas_call(lambda *refs: pack_columns_kernel(4, *refs), out_shape=(co...  3.06 us
    pallas_call x1, Pallas kernels, steps(): pl.pallas_call(window_kernel, out_shape=(pltpu.HBM((6 * nx + 16, ny), F32...  2.19 us
  transfers between devices with their start and end apart: 8, of which 4 were waited for; matrix products, arithmetic and copies ran while one was open for 0% of the time, Pallas kernels for 22%

profile of v2, /device:TPU:1, one launch (start us, length us, event | category | flops | bytes accessed | tf_op | source)
XLA Modules:
  0.0 61.9 jit_solution(6813022927178350515)
XLA Ops:
  0.6 0.0 copy-start
  0.6 3.1 %columns.1 = (f32[3,32,128]{2,1,0:T(8,128)S(1)}, f32[3,32,128]{2,1,0:T(8,128)S(1)}, f32[6,32,128]{2,1,0:T(8,128)S(1)}, f32[2,128,128]{2,1,0:T(8,128)S(1)}, f32[2,128,128]{2,1,0:T(8,128)S(1)}) custom-call(f32[128,32,128]{2,1,0:T(8,128)} %tracer.1, f32[2,32,128]{2,1,0:T(8,128)} %velocity.5), custom_call_target="tpu_custom_call" | custom-call | flops 1000000 | bytes 2097152 | tf_op jit(solution)/shard_map/columns/pallas_call | solution.py:469
  3.7 3.2 %collective-permute-start.1 = (f32[3,32,128]{2,1,0:T(8,128)S(1)}, f32[3,32,128]{2,1,0:T(8,128)S(1)}, u32[]{:S(2)}, u32[]{:S(2)}) collective-permute-start(f32[3,32,128]{2,1,0:T(8,128)S(1)} %get-tuple-element.18.own_left), channel_id=1, source_target_pairs={{0,7},{1,0},{2,1},{3,2},{4,3},{5,4},{6,5},{7,6},{8,15},{9,8},{10,9... | collective-permute-start | bytes 147464 | tf_op jit(solution)/shard_map/ppermute | solution.py:455
  6.9 0.0 collective-permute-start
  6.9 1.2 %collective-permute-done.1.from_right = f32[3,32,128]{2,1,0:T(8,128)S(1)} collective-permute-done((f32[3,32,128]{2,1,0:T(8,128)S(1)}, f32[3,32,128]{2,1,0:T(8,128)S(1)}, u32[]{:S(2)}, u32[]{:S(2)}) %collective-permute-start.1) | collective-permute-done | bytes 49184 | tf_op jit(solution)/shard_map/ppermute | solution.py:455
  8.1 0.1 collective-permute-done.from_left
  8.2 0.0 copy-done
  8.2 1.4 %collective-permute-start.2 = (f32[24,128]{1,0:T(8,128)S(1)}, f32[24,128]{1,0:T(8,128)S(1)}, u32[]{:S(2)}, u32[]{:S(2)}) collective-permute-start(f32[24,128]{1,0:T(8,128)S(1)} %get-tuple-element.21.own_down), channel_id=1, source_target_pairs={{0,8},{8,16},{16,24},{24,32},{32,40},{40,48},{48,56},{56,64},{64,7... | collective-permute-start | bytes 36872 | tf_op jit(solution)/shard_map/ppermute | solution.py:455
  9.5 6.8 %collective-permute-start.3 = (f32[24,128]{1,0:T(8,128)S(1)}, f32[24,128]{1,0:T(8,128)S(1)}, u32[]{:S(2)}, u32[]{:S(2)}) collective-permute-start(f32[24,128]{1,0:T(8,128)S(1)} %get-tuple-element.20.own_up), channel_id=1, source_target_pairs={{0,248},{8,0},{16,8},{24,16},{32,24},{40,32},{48,40},{56,48},{64,5... | collective-permute-start | bytes 36872 | tf_op jit(solution)/shard_map/ppermute | solution.py:455
  16.4 0.0 copy-start.1
  16.4 1.9 %load.1.basis = f32[94,64,128]{2,1,0:T(8,128)S(1)} custom-call(f32[94,64,128]{2,1,0:T(8,128)} %bitcast.9), custom_call_target="tpu_custom_call" | custom-call | bytes 6291456 | tf_op jit(solution)/shard_map/load/pallas_call | solution.py:480
  18.3 0.0 copy-start.2
  18.3 0.0 collective-permute-done.2.from_up
  18.3 0.0 collective-permute-done.3.from_down
  18.3 0.0 copy-done.1
  18.3 2.2 %window.1 = (f32[208,128]{1,0:T(8,128)}, f32[2,128]{1,0:T(2,128)S(1)}) custom-call(f32[128]{0:T(128)S(1)} %copy-done.1, f32[6,32,128]{2,1,0:T(8,128)S(1)} %get-tuple-element.17.near, f32[2,32,128]{2,1,0:T(8,128)S(1)} %copy-done, f32[1,128]{1,0:T(1,128)S(1)} %bitcast.6, f32[3,32,128]{2,1,0:T(8,128)S(1)} %get-tuple-element.18.own_left, ...), custom_call_target="tpu_custom_call" | custom-call | flops 10000000 | bytes 4194304 | tf_op jit(solution)/shard_map/window/pallas_call | solution.py:498
  20.5 4.4 %collective-permute-start.6 = (f32[2,128]{1,0:T(2,128)S(1)}, f32[2,128]{1,0:T(2,128)S(1)}, u32[]{:S(2)}, u32[]{:S(2)}) collective-permute-start(f32[2,128]{1,0:T(2,128)S(1)} %get-tuple-element.28.mine), channel_id=1, source_target_pairs={{0,1},{1,0},{2,3},{3,2},{4,5},{5,4},{6,7},{7,6},{8,9},{9,8},{10,11... | collective-permute-start | bytes 3080 | tf_op jit(solution)/shard_map/ppermute | solution.py:513
  24.9 0.8 %collective-permute-done.6.other = f32[2,128]{1,0:T(2,128)S(1)} collective-permute-done((f32[2,128]{1,0:T(2,128)S(1)}, f32[2,128]{1,0:T(2,128)S(1)}, u32[]{:S(2)}, u32[]{:S(2)}) %collective-permute-start.6) | collective-permute-done | bytes 1056 | tf_op jit(solution)/shard_map/ppermute | solution.py:513
  25.7 0.7 %spread.1 = f32[128,2,128]{2,1,0:T(2,128)} custom-call(f32[2,128]{1,0:T(2,128)S(1)} %get-tuple-element.28.mine, f32[2,128]{1,0:T(2,128)S(1)} %collective-permute-done.6.other), custom_call_target="tpu_custom_call" | custom-call | flops 10000 | bytes 131072 | tf_op jit(solution)/shard_map/spread/pallas_call | solution.py:514
  26.4 9.8 %all-to-all-start = ((f32[128,2,128]{2,1,0:T(2,128)}), f32[128,2,128]{2,1,0:T(2,128)S(1)}, u32[]{:S(2)}, u32[]{:S(2)}) async-start(f32[128,2,128]{2,1,0:T(2,128)} %spread.1), calls=%async_computation | async-start | bytes 262144 | tf_op jit(solution)/shard_map/all_to_all | solution.py:518
  36.1 0.7 %collective-permute-start.4 = (f32[2,128,128]{2,1,0:T(8,128)S(1)}, f32[2,128,128]{2,1,0:T(8,128)S(1)}, u32[]{:S(2)}, u32[]{:S(2)}) collective-permute-start(f32[2,128,128]{2,1,0:T(8,128)S(1)} %get-tuple-element.25), channel_id=1, source_target_pairs={{0,8},{8,16},{16,24},{24,32},{32,40},{40,48},{48,56},{56,64},{64,7... | collective-permute-start | bytes 393224 | tf_op jit(solution)/shard_map/ppermute | solution.py:455
  36.8 4.2 %collective-permute-start.5 = (f32[2,128,128]{2,1,0:T(8,128)S(1)}, f32[2,128,128]{2,1,0:T(8,128)S(1)}, u32[]{:S(2)}, u32[]{:S(2)}) collective-permute-start(f32[2,128,128]{2,1,0:T(8,128)S(1)} %get-tuple-element.26), channel_id=1, source_target_pairs={{0,248},{8,0},{16,8},{24,16},{32,24},{40,32},{48,40},{56,48},{64,5... | collective-permute-start | bytes 393224 | tf_op jit(solution)/shard_map/ppermute | solution.py:455
  41.0 5.6 %collective-permute-done.4.top_hbm = f32[2,128,128]{2,1,0:T(8,128)S(1)} collective-permute-done((f32[2,128,128]{2,1,0:T(8,128)S(1)}, f32[2,128,128]{2,1,0:T(8,128)S(1)}, u32[]{:S(2)}, u32[]{:S(2)}) %collective-permute-start.4) | collective-permute-done | bytes 131104 | tf_op jit(solution)/shard_map/ppermute | solution.py:455
  46.6 0.0 collective-permute-done.5.bottom_hbm
  46.6 0.0 copy-done.2
  46.6 12.0 %bulk.1 = (f32[128,32,128]{2,1,0:T(8,128)}, bf16[32,96,256]{2,1,0:T(8,128)(2,1)S(1)}, bf16[32,96,256]{2,1,0:T(8,128)(2,1)S(1)}, f32[8,128]{1,0:T(8,128)S(1)}) custom-call(f32[128]{0:T(128)S(1)} %copy-done.1, f32[128,32,128]{2,1,0:T(8,128)} %tracer.1, f32[94,64,128]{2,1,0:T(8,128)} %bitcast.10, f32[208,128]{1,0:T(8,128)} %get-tuple-element.22.kept_hbm, ...), custom_call_target="tpu_custom_call" | custom-call | flops 100000000 | bytes 10485760 | tf_op jit(solution)/shard_map/bulk/pallas_call | solution.py:523
  58.6 0.0 all-to-all-done
  58.6 3.3 %core.1 = f32[96,64,128]{2,1,0:T(8,128)} custom-call(f32[32,8,128]{2,1,0:T(8,128)S(1)} %bitcast.5, f32[8,128]{1,0:T(8,128)S(1)} %get-tuple-element.29.refs_1_, bf16[32,96,256]{2,1,0:T(8,128)(2,1)S(1)} %get-tuple-element.30.refs_2_, bf16[32,96,256]{2,1,0:T(8,128)(2,1)S(1)} %get-tuple-element.31.refs_3_), custom_call_target="tpu_custom_call" | custom-call | flops 100000000 | bytes 6291456 | tf_op jit(solution)/shard_map/core/pallas_call | solution.py:538
  (1 shorter events, 0.0 us)
Async XLA Ops:
  0.6 7.5 %copy-start = (f32[2,32,128]{2,1,0:T(8,128)S(1)}, f32[2,32,128]{2,1,0:T(8,128)}, u32[]{:S(2)}) copy-start(f32[2,32,128]{2,1,0:T(8,128)} %velocity.5) | copy-start | bytes 98308
  3.7 4.4 %collective-permute-start.1 = (f32[3,32,128]{2,1,0:T(8,128)S(1)}, f32[3,32,128]{2,1,0:T(8,128)S(1)}, u32[]{:S(2)}, u32[]{:S(2)}) collective-permute-start(f32[3,32,128]{2,1,0:T(8,128)S(1)} %get-tuple-element.18.own_left), channel_id=1, source_target_pairs={{0,7},{1,0},{2,1},{3,2},{4,3},{5,4},{6,5},{7,6},{8,15},{9,8},{10,9... | collective-permute-start | bytes 147464 | tf_op jit(solution)/shard_map/ppermute | solution.py:455
  6.9 1.2 %collective-permute-start = (f32[3,32,128]{2,1,0:T(8,128)S(1)}, f32[3,32,128]{2,1,0:T(8,128)S(1)}, u32[]{:S(2)}, u32[]{:S(2)}) collective-permute-start(f32[3,32,128]{2,1,0:T(8,128)S(1)} %get-tuple-element.19.own_right), channel_id=1, source_target_pairs={{0,1},{1,2},{2,3},{3,4},{4,5},{5,6},{6,7},{7,0},{8,9},{9,10},{10,1... | collective-permute-start | bytes 147464 | tf_op jit(solution)/shard_map/ppermute | solution.py:455
  8.2 10.1 %collective-permute-start.2 = (f32[24,128]{1,0:T(8,128)S(1)}, f32[24,128]{1,0:T(8,128)S(1)}, u32[]{:S(2)}, u32[]{:S(2)}) collective-permute-start(f32[24,128]{1,0:T(8,128)S(1)} %get-tuple-element.21.own_down), channel_id=1, source_target_pairs={{0,8},{8,16},{16,24},{24,32},{32,40},{40,48},{48,56},{56,64},{64,7... | collective-permute-start | bytes 36872 | tf_op jit(solution)/shard_map/ppermute | solution.py:455
  9.5 8.7 %collective-permute-start.3 = (f32[24,128]{1,0:T(8,128)S(1)}, f32[24,128]{1,0:T(8,128)S(1)}, u32[]{:S(2)}, u32[]{:S(2)}) collective-permute-start(f32[24,128]{1,0:T(8,128)S(1)} %get-tuple-element.20.own_up), channel_id=1, source_target_pairs={{0,248},{8,0},{16,8},{24,16},{32,24},{40,32},{48,40},{56,48},{64,5... | collective-permute-start | bytes 36872 | tf_op jit(solution)/shard_map/ppermute | solution.py:455
  16.4 1.9 %copy-start.1 = (f32[128]{0:T(128)S(1)}, f32[128]{0:T(128)}, u32[]{:S(2)}) copy-start(f32[128]{0:T(128)} %diff.3) | copy-start | bytes 1540
  18.3 28.4 %copy-start.2 = (f32[94]{0:T(128)S(1)}, f32[94]{0:T(128)}, u32[]{:S(2)}) copy-start(f32[94]{0:T(128)} %param.8) | copy-start | bytes 1132
  20.5 5.2 %collective-permute-start.6 = (f32[2,128]{1,0:T(2,128)S(1)}, f32[2,128]{1,0:T(2,128)S(1)}, u32[]{:S(2)}, u32[]{:S(2)}) collective-permute-start(f32[2,128]{1,0:T(2,128)S(1)} %get-tuple-element.28.mine), channel_id=1, source_target_pairs={{0,1},{1,0},{2,3},{3,2},{4,5},{5,4},{6,7},{7,6},{8,9},{9,8},{10,11... | collective-permute-start | bytes 3080 | tf_op jit(solution)/shard_map/ppermute | solution.py:513
  26.4 32.2 %all-to-all-start = ((f32[128,2,128]{2,1,0:T(2,128)}), f32[128,2,128]{2,1,0:T(2,128)S(1)}, u32[]{:S(2)}, u32[]{:S(2)}) async-start(f32[128,2,128]{2,1,0:T(2,128)} %spread.1), calls=%async_computation | async-start | bytes 262144 | tf_op jit(solution)/shard_map/all_to_all | solution.py:518
  36.1 10.5 %collective-permute-start.4 = (f32[2,128,128]{2,1,0:T(8,128)S(1)}, f32[2,128,128]{2,1,0:T(8,128)S(1)}, u32[]{:S(2)}, u32[]{:S(2)}) collective-permute-start(f32[2,128,128]{2,1,0:T(8,128)S(1)} %get-tuple-element.25), channel_id=1, source_target_pairs={{0,8},{8,16},{16,24},{24,32},{32,40},{40,48},{48,56},{56,64},{64,7... | collective-permute-start | bytes 393224 | tf_op jit(solution)/shard_map/ppermute | solution.py:455
  36.8 9.8 %collective-permute-start.5 = (f32[2,128,128]{2,1,0:T(8,128)S(1)}, f32[2,128,128]{2,1,0:T(8,128)S(1)}, u32[]{:S(2)}, u32[]{:S(2)}) collective-permute-start(f32[2,128,128]{2,1,0:T(8,128)S(1)} %get-tuple-element.26), channel_id=1, source_target_pairs={{0,248},{8,0},{16,8},{24,16},{32,24},{40,32},{48,40},{56,48},{64,5... | collective-permute-start | bytes 393224 | tf_op jit(solution)/shard_map/ppermute | solution.py:455

commit v3 on v2

v3 whole, which is shorter than its diff:
```python
import math

import jax
import jax.numpy as jnp
from jax import lax
from jax.experimental import pallas as pl
from jax.experimental.pallas import tpu as pltpu
from jax.sharding import Mesh
from jax.sharding import PartitionSpec as P


F32 = jnp.float32
BF16 = jnp.bfloat16
GX = ("z", "y")
GY = ("x", "c")
CHIPS = ("z", "y", "x")
ROOT_ITERS = 5
SHIFTS = 2**ROOT_ITERS
POLES = SHIFTS // 2 - 1
VMEM = pltpu.VMEM


def lanes_of(shape):
    return lax.broadcasted_iota(jnp.int32, shape, len(shape) - 1)


def rows_of(shape):
    return lax.broadcasted_iota(jnp.int32, shape, len(shape) - 2)


def step(c, xm, xp, ym, yp, zm, zp, d, vxp, vxn, vyp, vyn):
    spread = (xm + xp) + (ym + yp) + (zm + zp) - 6.0 * c
    carried = (vxp * (c - xm) + vxn * (xp - c)) + (vyp * (c - ym) + vyn * (yp - c))
    return c + d * spread - carried


def signed_parts(vx, vy):
    return jnp.maximum(vx, 0.0), jnp.minimum(vx, 0.0), jnp.maximum(vy, 0.0), jnp.minimum(vy, 0.0)


def before(c, ghost, axis):
    at = lax.broadcasted_iota(jnp.int32, c.shape, axis)
    return jnp.where(at == 0, ghost, pltpu.roll(c, 1, axis))


def after(c, ghost, axis):
    n = c.shape[axis]
    at = lax.broadcasted_iota(jnp.int32, c.shape, axis)
    return jnp.where(at == n - 1, ghost, pltpu.roll(c, n - 1, axis))


def gx_is_even():
    return lax.axis_index("y") % 2 == 0


def gy_is_even():
    return lax.axis_index("c") == 0


def to_pairs(even, up, down):
    return jnp.where(even, down, up), jnp.where(even, up, down)


def from_pairs(even, near, far):
    return jnp.where(even, far, near), jnp.where(even, near, far)


def pack_columns_kernel(
    chunks, tracer_hbm, velocity_hbm, near, far, window, rows_near, rows_far, mine,
    tracer, velocity, sems,
):
    nx, ny = velocity.shape[1:]
    nz = tracer.shape[0] // nx
    size = nz // chunks
    loads = [
        pltpu.make_async_copy(
            tracer_hbm.at[pl.ds(i * size * nx, size * nx)],
            tracer.at[pl.ds(i * size * nx, size * nx)], sems.at[i],
        )
        for i in range(chunks)
    ]
    loads.append(pltpu.make_async_copy(velocity_hbm, velocity, sems.at[chunks]))
    for load in loads:
        load.start()
    lane = lanes_of((nx, ny))

    def level(z, carry):
        a, b, y, w = carry
        r = pltpu.roll(tracer[pl.ds(pl.multiple_of(z * nx, nx), nx), :], z, 1)
        rel = (lane - z) & (ny - 1)
        a = jnp.where(rel == 0, r, a)
        b = jnp.where(rel == 1, r, b)
        y = jnp.where(rel == ny - 1, r, y)
        w = jnp.where(rel == ny - 2, r, w)
        return a, b, y, w

    carry = (jnp.zeros((nx, ny), F32),) * 4
    for i in range(chunks):
        loads[i].wait()
        carry = lax.fori_loop(i * size, (i + 1) * size, level, carry, unroll=8)
    a, b, y, w = carry
    loads[chunks].wait()
    vx, vy = velocity[0], velocity[1]
    left = (a, pltpu.roll(b, ny - 1, 1), jnp.where(lane == 0, vx, pltpu.roll(vy, 1, 1)))
    right = (
        pltpu.roll(y, 1, 1), pltpu.roll(w, 2, 1),
        jnp.where(lane == ny - 1, vx, pltpu.roll(vy, ny - 1, 1)),
    )
    even = gy_is_even()
    for i in range(3):
        near[i], far[i] = to_pairs(even, left[i], right[i])
    mine[0], mine[1] = left[0], right[0]
    window[0 : 2 * nx] = tracer[(nz - 2) * nx : nz * nx]
    window[2 * nx : 6 * nx] = tracer[0 : 4 * nx]
    even = gx_is_even()
    for i in range(2):
        top = tracer[pl.ds(i, nz, stride=nx), :]
        bottom = tracer[pl.ds(nx - 1 - i, nz, stride=nx), :]
        rows_near[i], rows_far[i] = to_pairs(even, top, bottom)


def pack_rows_kernel(window, velocity, sides_near, sides_far, near, far, up, down):
    nx, ny = velocity.shape[1:]
    from_left, from_right = from_pairs(gy_is_even(), sides_near[0], sides_far[0])
    for edge, inner, out in ((0, 1, up), (nx - 1, nx - 2, down)):
        for s in range(6):
            out[s : s + 1, :] = window[s * nx + edge : s * nx + edge + 1, :]
            out[8 + s : 9 + s, :] = window[s * nx + inner : s * nx + inner + 1, :]
        for s in (6, 7, 14, 15, 20, 21, 22, 23):
            out[s : s + 1, :] = jnp.zeros((1, ny), F32)
        out[16:17, :] = velocity[0, edge : edge + 1, :]
        out[17:18, :] = velocity[1, edge : edge + 1, :]
        out[18:19, :] = from_left[edge : edge + 1, :]
        out[19:20, :] = from_right[edge : edge + 1, :]
    near[...], far[...] = to_pairs(gx_is_even(), up[...], down[...])


def window_kernel(
    diff, near, velocity, diff_row, mine, sides_near, sides_far,
    own_up, own_down, rows_near, rows_far, basis,
    kept_hbm, sums, snaps, sides, q0, q1, sems,
):
    nz, nx, ny = diff.shape[0], velocity.shape[1], velocity.shape[2]
    count = basis.shape[0]
    dz = diff_row[...]
    even = gy_is_even()
    pairs = [from_pairs(even, sides_near[i], sides_far[i]) for i in range(3)]
    from_left, from_right = [p[0] for p in pairs], [p[1] for p in pairs]
    from_up, from_down = from_pairs(gx_is_even(), rows_near[...], rows_far[...])
    for gin, inner, outer, corner, vx_at, vy_at, out in (
        (from_left, None, mine[0], 18, ny - 1, ny - 2, sides.at[0:nx]),
        (from_right, mine[1], None, 19, 0, 1, sides.at[nx : 2 * nx]),
    ):
        c = gin[0]
        ym = gin[1] if inner is None else inner
        yp = gin[1] if outer is None else outer
        vx = gin[2][:, vx_at : vx_at + 1]
        vy = gin[2][:, vy_at : vy_at + 1]
        parts = signed_parts(vx, vy)
        xm = before(c, from_up[corner : corner + 1, :], 0)
        xp = after(c, from_down[corner : corner + 1, :], 0)
        out[...] = step(c, xm, xp, ym, yp, pltpu.roll(c, 1, 1), pltpu.roll(c, nz - 1, 1), dz, *parts)

    sub = rows_of((8, ny))
    lane = lanes_of((8, ny))
    d_rows = jnp.where(sub == 2, diff[0], diff[1])
    ghost_rows = []
    for gin, own, top in ((from_up, own_up, True), (from_down, own_down, False)):
        c = gin[0:8, :]
        beyond, inside = gin[8:16, :], own[0:8, :]
        xm, xp = (beyond, inside) if top else (inside, beyond)
        west = jnp.where(sub == 2, gin[18:19, 0:1], gin[18:19, 1:2])
        east = jnp.where(sub == 2, gin[19:20, 0:1], gin[19:20, 1:2])
        parts = signed_parts(gin[16:17, :], gin[17:18, :])
        ghost_rows.append(
            step(c, xm, xp, before(c, west, 1), after(c, east, 1),
                 pltpu.roll(c, 1, 0), pltpu.roll(c, 7, 0), d_rows, *parts)
        )

    parts = signed_parts(velocity[0], velocity[1])
    u = [near[s * nx : (s + 1) * nx] for s in range(6)]
    first = []
    for s in range(1, 5):
        z = (s - 2) % nz
        c = u[s]
        xm = before(c, from_up[s : s + 1, :], 0)
        xp = after(c, from_down[s : s + 1, :], 0)
        ym = before(c, from_left[0][:, z : z + 1], 1)
        yp = after(c, from_right[0][:, z : z + 1], 1)
        first.append(step(c, xm, xp, ym, yp, u[s - 1], u[s + 1], diff[z], *parts))
    for z in range(2):
        c = first[z + 1]
        snaps[0, z * nx : (z + 1) * nx, :] = c
        xm = before(c, ghost_rows[0][z + 2 : z + 3, :], 0)
        xp = after(c, ghost_rows[1][z + 2 : z + 3, :], 0)
        ym = before(c, sides[0:nx, z : z + 1], 1)
        yp = after(c, sides[nx : 2 * nx, z : z + 1], 1)
        snaps[1, z * nx : (z + 1) * nx, :] = step(
            c, xm, xp, ym, yp, first[z], first[z + 2], diff[z], *parts
        )

    rows = 2 * nx
    pieces = rows // 8
    sides[rows : rows + 8] = from_up[16:24, :]
    sides[rows + 8 : rows + 16] = from_down[16:24, :]
    keep = [
        pltpu.make_async_copy(ref, kept_hbm.at[pl.ds(at, ref.shape[0])], sems.at[i])
        for i, (ref, at) in enumerate(
            ((snaps.at[0], 0), (snaps.at[1], rows), (sides, 2 * rows))
        )
    ]
    for copy in keep:
        copy.start()

    def folded(a, b):
        total = a[0:8, :] * b[0:8, :]
        for i in range(1, pieces):
            total = total + a[8 * i : 8 * i + 8, :] * b[8 * i : 8 * i + 8, :]
        return total

    def group(vectors, start, size):
        for m, q in enumerate((q0, q1)):
            lines = jnp.stack([folded(v, snaps[m]) for v in vectors])
            q[pl.ds(start, size), :] = jnp.sum(lines, axis=1)

    def eight(i, carry):
        at = pl.multiple_of(8 * i, 8)
        group([basis[at + j] for j in range(8)], at, 8)
        return carry

    full = count // 8 * 8
    lax.fori_loop(0, count // 8, eight, 0)
    group([basis[k] for k in range(full, count)] + [snaps[0], snaps[1]], full, count + 2 - full)
    for q in (q0, q1):
        q[count + 2 :] = jnp.zeros((ny - count - 2, ny), F32)
    ones = jnp.ones((8, ny), F32)
    over_lanes = (((1,), (1,)), ((), ()))
    for m, q in enumerate((q0, q1)):
        line = lax.dot_general(
            ones, q[...], over_lanes, precision=lax.Precision.HIGHEST, preferred_element_type=F32
        )
        sums[m : m + 1, :] = line[0:1, :]
    for copy in keep:
        copy.wait()


def split(basis, snaps, upper, lower):
    rows, ny = snaps.shape[0] // 2, snaps.shape[1]
    count = basis.shape[0] // rows
    for r in range(rows):
        pair, half = r // 2, r % 2
        lanes = slice(half * ny, (half + 1) * ny)
        v = jnp.concatenate(
            [basis[pl.ds(r, count, stride=rows), :], snaps[pl.ds(r, 2, stride=rows), :]], axis=0
        )
        hi = v.astype(BF16)
        upper[pair, :, lanes] = hi
        lower[pair, :, lanes] = (v - hi.astype(F32)).astype(BF16)


def load_kernel(src, dst, sem):
    copy = pltpu.make_async_copy(src, dst, sem)
    copy.start()
    copy.wait()


def sweep(diff, velocity, src, dst, col_left, col_right, chunks, after_chunk):
    nx, ny = velocity.shape[1:]
    pitch = nx + 16
    nz = src.shape[0] // pitch
    size = nz // chunks
    vx, vy = velocity[0], velocity[1]
    east, north = vx > 0.0, vy > 0.0
    speed_x, speed_y = jnp.abs(vx), jnp.abs(vy)
    stay = 1.0 - speed_x - speed_y
    lane = lanes_of((nx, ny))
    first, last = lane == 0, lane == ny - 1
    is_even = (lane & 1) == 0
    shifted = pltpu.roll(col_right, nz - 1, 1)
    columns = (jnp.where(is_even, col_left, shifted), jnp.where(is_even, shifted, col_left))

    def rows_at(z, by):
        return pl.ds(pl.multiple_of(z * pitch, 8) + 8 + by, nx)

    def turned(c, z, which):
        side = pltpu.roll(columns[which], (nz - z) & (nz - 1), 1)
        return pltpu.roll(c, 1, 1), pltpu.roll(c, ny - 1, 1), side

    def level(z, next_parity, state):
        zm, c, south, north_side, side = state
        zn = (z + 1) & (nz - 1)
        zp = src[rows_at(zn, 0), :]
        ahead = turned(zp, zn, next_parity)
        ym = jnp.where(first, side, south)
        yp = jnp.where(last, side, north_side)
        xm = src[rows_at(z, -1), :]
        xp = src[rows_at(z, 1), :]
        d = diff[z]
        moved = speed_x * jnp.where(east, xm, xp) + speed_y * jnp.where(north, ym, yp)
        spread = ((xm + xp) + (ym + yp)) + (zm + zp)
        dst[rows_at(z, 0), :] = (c * (stay - 6.0 * d) + moved) + d * spread
        return (c, zp, *ahead)

    def pair(i, state):
        return level(2 * i + 1, 0, level(2 * i, 1, state))

    c = src[rows_at(0, 0), :]
    state = (src[rows_at(nz - 1, 0), :], c, *turned(c, 0, 0))
    for k in range(chunks):
        state = lax.fori_loop(k * size // 2, (k + 1) * size // 2, pair, state, unroll=2)
        after_chunk(k)


def chunk_stores(src, out, sems, chunks, nx):
    pitch = nx + 16
    nz = src.shape[0] // pitch
    size = nz // chunks
    view = src.reshape(nz, pitch, src.shape[1])
    stores = []

    def store(k):
        part = pl.ds(k * size, size)
        copy = pltpu.make_async_copy(view.at[part, pl.ds(8, nx), :], out.at[part], sems.at[k])
        copy.start()
        stores.append(copy)

    return store, stores


def first_kernel(
    chunks, diff, tracer, velocity, sides_near, sides_far, rows_near, rows_far,
    sent_near, sent_far, out, rows_out, now, then, rows, sems,
):
    nz, nx, ny = tracer.shape
    pitch = nx + 16
    view = now.reshape(nz, pitch, ny)
    load = pltpu.make_async_copy(tracer, view.at[:, pl.ds(8, nx), :], sems.at[chunks])
    load.start()
    even = gx_is_even()
    for i in range(2):
        rows[i], rows[2 + i] = from_pairs(even, rows_near[i], rows_far[i])
    rows[4] = jnp.where(even, sent_far[0], sent_near[0])
    rows[5] = jnp.where(even, sent_near[0], sent_far[0])
    keep = pltpu.make_async_copy(rows, rows_out, sems.at[chunks + 1])
    keep.start()
    now[pl.ds(7, nz, stride=pitch), :] = rows[0]
    now[pl.ds(8 + nx, nz, stride=pitch), :] = rows[2]
    from_left, from_right = from_pairs(gy_is_even(), sides_near[0], sides_far[0])
    load.wait()
    store, stores = chunk_stores(then, out, sems, chunks, nx)
    sweep(diff, velocity, now, then, from_left, from_right, chunks, store)
    keep.wait()
    for copy in stores:
        copy.wait()


def second_kernel(
    chunks, diff, first, basis, kept_hbm, rows_hbm, velocity, diff_row, singular,
    out, upper, lower, line, now, then, vectors, kept, rows, sems,
):
    nz, nx, ny = first.shape
    pitch = nx + 16
    count = singular.shape[1]
    view = now.reshape(nz, pitch, ny)
    loads = [
        pltpu.make_async_copy(src, dst, sems.at[chunks + i])
        for i, (src, dst) in enumerate((
            (first, view.at[:, pl.ds(8, nx), :]), (kept_hbm, kept), (rows_hbm, rows),
            (basis, vectors),
        ))
    ]
    for load in loads:
        load.start()
    line[...] = jnp.zeros_like(line)
    line[0:1, :count] = singular[...]
    eye = rows_of((nz, nz)) == lanes_of((nz, nz))
    d_all = jnp.sum(jnp.where(eye, diff_row[...], 0.0), axis=1, keepdims=True)
    for load in loads[1:3]:
        load.wait()
    for i, own, is_top, at in ((0, 4, True, 6 * nx), (2, 5, False, 6 * nx + 8)):
        gin = kept[at : at + 8, :]
        c, beyond, inside = rows[i], rows[i + 1], rows[own]
        xm, xp = (beyond, inside) if is_top else (inside, beyond)
        west = jnp.sum(jnp.where(eye, gin[2:3, :], 0.0), axis=1, keepdims=True)
        east = jnp.sum(jnp.where(eye, gin[3:4, :], 0.0), axis=1, keepdims=True)
        parts = signed_parts(gin[0:1, :], gin[1:2, :])
        now[pl.ds(7 if is_top else 8 + nx, nz, stride=pitch), :] = step(
            c, xm, xp, before(c, west, 1), after(c, east, 1),
            pltpu.roll(c, 1, 0), pltpu.roll(c, nz - 1, 0), d_all, *parts
        )
    loads[0].wait()
    store, stores = chunk_stores(then, out, sems, chunks, nx)
    sweep(
        diff, velocity, now, then, kept[4 * nx : 5 * nx, :], kept[5 * nx : 6 * nx, :], chunks, store
    )
    loads[3].wait()
    split(vectors, kept.at[0 : 4 * nx], upper, lower)
    for copy in stores:
        copy.wait()


def spread_kernel(mine, other, out):
    both = mine[...] + other[...]
    out[...] = jnp.broadcast_to(both[None], out.shape)


def core_kernel(rows_all, parts, singular, upper, lower, out, block, sems):
    count = out.shape[0] - 2
    n = parts.shape[2]
    total = jnp.sum(parts[...], axis=0)
    total = total + pltpu.roll(total, 2, 0)
    total = total + pltpu.roll(total, 4, 0)
    total = total * (1.0 / rows_all)
    lane = lanes_of((1, n))
    zero = jnp.zeros((1, n), F32)

    def add(x):
        return jnp.sum(x, axis=1, keepdims=True)

    def pick(x, at):
        return add(jnp.where(lane == at, x, zero))

    p0 = jnp.where(lane < count, total[0:1, :], zero)
    p1 = jnp.where(lane < count, total[1:2, :], zero)
    g00 = pick(total[0:1, :], count) - add(p0 * p0) + 1e-06
    g01 = pick(total[0:1, :], count + 1) - add(p0 * p1)
    g11 = pick(total[1:2, :], count + 1) - add(p1 * p1) + 1e-06
    r11 = jnp.sqrt(g00)
    r12 = g01 / r11
    r22 = jnp.sqrt(g11 - r12 * r12)
    u0 = jnp.where(lane == count, r11, p0)
    u1 = jnp.where(lane == count, r12, jnp.where(lane == count + 1, r22, p1))
    s = singular[0:1, :]
    squares = s * s
    sigma = add(squares + u0 * u0 + u1 * u1) / (count + 2)
    root = jnp.sqrt(sigma)
    d = squares / sigma
    v0 = u0 / root
    v1 = u1 / root

    half = POLES + 1
    row = rows_of((half, n))
    pole = jnp.zeros((half, n), F32)
    for j in range(POLES):
        pole = jnp.where(row == j, math.tan(math.pi * (j + 1) / SHIFTS) ** 2, pole)
    last = row == POLES
    pole = jnp.where(last, 1.0, pole)
    inverse = jnp.where(last, 1.0, 1.0 / (d + pole))
    weight = 2.0 * (1.0 + pole)
    w0 = inverse * v0
    w1 = inverse * v1
    last_one = last[:, 0:1]
    a = jnp.where(last_one, 1.0, 1.0 + add(w0 * v0))
    b = jnp.where(last_one, 0.0, add(w0 * v1))
    c = jnp.where(last_one, 1.0, 1.0 + add(w1 * v1))
    e = b / a
    c = c - b * e
    strength = jnp.where(last, 1.0, weight * pole)
    w1 = jnp.sqrt(strength / c) * (w1 - e * w0)
    w0 = jnp.sqrt(strength / a) * w0
    low_rank = jnp.concatenate([w0, w1], axis=0)
    gains = 1.0 + d + jnp.sum(jnp.where(last, 0.0, weight * d * inverse), axis=0, keepdims=True)
    square = (n, n)
    core = lax.dot_general(
        low_rank, low_rank, (((0,), (0,)), ((), ())),
        precision=lax.Precision.HIGHEST, preferred_element_type=F32,
    )
    core = core + jnp.where(rows_of(square) == lanes_of(square), gains, 0.0)
    core = core * (root * (1.0 / SHIFTS))
    t0 = jnp.where(lane == count, 1.0, -p0) / r11
    q_lane = jnp.where(lane == count + 1, 1.0, -p1)
    t1 = (q_lane - r12 * t0) / r22
    full = jnp.where(lanes_of(square) < count, core, 0.0)
    full = full + core[:, count : count + 1] * t0 + core[:, count + 1 : count + 2] * t1
    full = full[: count + 2, : count + 2]
    hi = full.astype(BF16)
    lo = (full - hi.astype(F32)).astype(BF16)
    both = jnp.concatenate([hi, lo], axis=0)

    size = count + 2
    rows = out.shape[1]
    view = block.reshape(size, rows, n)
    copies = []
    for b in range(rows // 8):
        for pair in range(4 * b, 4 * b + 4):
            r = jnp.dot(both, upper[pair], preferred_element_type=F32)
            r = r[:size] + r[size:] + jnp.dot(hi, lower[pair], preferred_element_type=F32)
            for half in range(2):
                at = pl.ds(2 * pair + half, size, stride=rows)
                block[at, :] = r[:, half * n : (half + 1) * n]
        part = pl.ds(8 * b, 8)
        copy = pltpu.make_async_copy(view.at[:, part, :], out.at[:, part, :], sems.at[b])
        copy.start()
        copies.append(copy)
    for copy in copies:
        copy.wait()


def whole(n):
    return [pl.BlockSpec(memory_space=VMEM)] * n


SMEM_SPEC = pl.BlockSpec(memory_space=pltpu.SMEM)


def shaped(*shape, dtype=F32):
    return jax.ShapeDtypeStruct(shape, dtype)


def in_hbm(x):
    return pltpu.with_memory_space_constraint(x, pltpu.HBM)


def cost(flops, moved):
    return pl.CostEstimate(flops=flops, bytes_accessed=moved, transcendentals=0)


def limit(mib):
    return pltpu.CompilerParams(vmem_limit_bytes=mib * 2**20)


def swap(x, axes, far):
    count = lax.axis_size(axes)
    shift = 1 if far else 0
    pairs = [((i + shift) % count, ((i ^ 1) + shift) % count) for i in range(count)]
    return lax.ppermute(x, axes, pairs)


def steps(tracer, velocity, diffusivity, singular, basis_vectors):
    nz, nx, ny = tracer.shape
    count, window = basis_vectors.shape[:2]
    rows = window * nx
    basis = basis_vectors.reshape(count, rows, ny)
    rows_all = rows * ny * lax.axis_size(GX) * lax.axis_size(GY)
    chips = lax.axis_size(CHIPS)
    diff_row = diffusivity.reshape(1, nz)

    columns = shaped(3, nx, ny)
    bulk_rows = shaped(2, nz, ny)
    hbm_space, any_space = (pl.BlockSpec(memory_space=m) for m in (pltpu.HBM, pl.ANY))
    columns_near, columns_far, near, sent_near, sent_far, mine = pl.pallas_call(
        lambda *refs: pack_columns_kernel(4, *refs),
        out_shape=(columns, columns, shaped(6 * nx, ny), bulk_rows, bulk_rows, shaped(2, nx, ny)),
        in_specs=[hbm_space] * 2, out_specs=tuple(whole(6)),
        scratch_shapes=[
            VMEM((nz * nx, ny), F32), VMEM((2, nx, ny), F32), pltpu.SemaphoreType.DMA((5,)),
        ],
        compiler_params=limit(4), cost_estimate=cost(10**6, 2 * 2**20), name="columns",
    )(in_hbm(tracer.reshape(nz * nx, ny)), in_hbm(velocity))
    sides_far = swap(columns_far, GY, True)
    sides_near = swap(columns_near, GY, False)
    rows_far = swap(sent_far, GX, True)
    rows_near = swap(sent_near, GX, False)

    edge = shaped(24, ny)
    edges_near, edges_far, own_up, own_down = pl.pallas_call(
        pack_rows_kernel, out_shape=(edge,) * 4, in_specs=whole(4), out_specs=tuple(whole(4)),
        compiler_params=limit(2), cost_estimate=cost(10**4, 2**17), name="edges",
    )(near, velocity, sides_near, sides_far)
    window_far = swap(edges_far, GX, True)
    window_near = swap(edges_near, GX, False)

    vectors = pl.pallas_call(
        load_kernel, out_shape=shaped(count, rows, ny),
        in_specs=[hbm_space], out_specs=whole(1)[0],
        scratch_shapes=[pltpu.SemaphoreType.DMA],
        compiler_params=limit(2), cost_estimate=cost(0, 6 * 2**20), name="load",
    )(in_hbm(basis))
    padded = VMEM((nz * (nx + 16), ny), F32)
    first, rows_kept = pl.pallas_call(
        lambda *refs: first_kernel(4, *refs),
        out_shape=(pltpu.HBM((nz, nx, ny), F32), pltpu.HBM((6, nz, ny), F32)),
        in_specs=[SMEM_SPEC, hbm_space] + whole(7), out_specs=(hbm_space, hbm_space),
        scratch_shapes=[padded, padded, VMEM((6, nz, ny), F32), pltpu.SemaphoreType.DMA((6,))],
        compiler_params=limit(8), cost_estimate=cost(10**8, 4 * 2**20), name="first",
    )(
        diffusivity, in_hbm(tracer), velocity, sides_near, sides_far, rows_near, rows_far,
        sent_near, sent_far,
    )

    kept, local = pl.pallas_call(
        window_kernel,
        out_shape=(pltpu.HBM((6 * nx + 16, ny), F32), shaped(2, ny)),
        in_specs=[SMEM_SPEC] + whole(11), out_specs=(hbm_space, *whole(1)),
        scratch_shapes=[
            VMEM((2, rows, ny), F32), VMEM((rows + 16, ny), F32), VMEM((ny, ny), F32),
            VMEM((ny, ny), F32), pltpu.SemaphoreType.DMA((3,)),
        ],
        compiler_params=limit(4), cost_estimate=cost(10**7, 4 * 2**20), name="window",
    )(
        diffusivity, near, velocity, diff_row, mine, sides_near, sides_far,
        own_up, own_down, window_near, window_far, vectors,
    )

    other = lax.ppermute(local, "c", [(0, 1), (1, 0)])
    sent = pl.pallas_call(
        spread_kernel, out_shape=shaped(chips, 2, ny), in_specs=whole(2), out_specs=whole(1)[0],
        compiler_params=limit(4), cost_estimate=cost(10**4, 2**17), name="spread",
    )(local, other)
    parts = lax.all_to_all(sent, CHIPS, 0, 0, tiled=True)

    halves = shaped(rows // 2, count + 2, 2 * ny, dtype=BF16)
    tracer_next, upper, lower, line = pl.pallas_call(
        lambda *refs: second_kernel(4, *refs),
        out_shape=(shaped(nz, nx, ny), halves, halves, shaped(8, ny)),
        in_specs=[SMEM_SPEC] + [hbm_space] * 4 + whole(3), out_specs=(any_space, *whole(3)),
        scratch_shapes=[
            padded, padded, VMEM((count * rows, ny), F32), VMEM((6 * nx + 16, ny), F32),
            VMEM((6, nz, ny), F32), pltpu.SemaphoreType.DMA((8,)),
        ],
        compiler_params=limit(12), cost_estimate=cost(10**8, 10 * 2**20), name="second",
    )(
        diffusivity, in_hbm(first), in_hbm(basis_vectors.reshape(count * rows, ny)), in_hbm(kept),
        in_hbm(rows_kept), velocity, diff_row, singular.reshape(1, count),
    )

    basis_next = pl.pallas_call(
        lambda *refs: core_kernel(rows_all, *refs),
        out_shape=shaped(count + 2, rows, ny),
        in_specs=whole(4), out_specs=pl.BlockSpec(memory_space=pl.ANY),
        scratch_shapes=[
            VMEM(((count + 2) * rows, ny), F32),
            pltpu.SemaphoreType.DMA((rows // 8,)),
        ],
        compiler_params=limit(16), cost_estimate=cost(10**8, 6 * 2**20), name="core",
    )(
        parts.reshape(chips // 4, 8, ny), line, upper, lower,
    )
    return tracer_next, basis_next.reshape(count + 2, window, nx, ny)


def solution(mesh):
    finer = Mesh(mesh.devices.reshape(8, 4, 4, 2), ("z", "y", "x", "c"))
    in_specs = (P(None, GX, GY), P(None, GX, GY), P(), P(), P(None, None, GX, GY))
    out_specs = (P(None, GX, GY), P(None, None, GX, GY))
    return jax.shard_map(steps, mesh=finer, in_specs=in_specs, out_specs=out_specs, check_vma=False)
```

time: 62.1 us -> 65.9 us (1.061)
  Pallas kernels: 23.1 us -> 27.9 us
  starting transfers between devices: 30.4 us -> 27 us
  waiting for transfers between devices: 7.69 us -> 9.88 us
    pallas_call x2 -> x3, Pallas kernels: 12 us -> 16.1 us  [the longest x1 9.04 us: steps(): pl.pallas_call(lambda *refs: second_kernel(4, *refs), out_shape=(shaped(n...]
    ppermute x1, starting transfers between devices: 4.37 us -> 1.96 us  [steps(): other = lax.ppermute(local, 'c', [(0, 1), (1, 0)])]
    ppermute x6, waiting for transfers between devices: 6.87 us -> 9.06 us  [swap(): return lax.ppermute(x, axes, pairs)]
    pallas_call x1, Pallas kernels: 3.25 us -> 4.26 us  [steps(): pl.pallas_call(lambda *refs: core_kernel(rows_all, *refs), out_shape=shap...]
    ppermute x6, starting transfers between devices: 16.3 us -> 15.4 us  [swap(): return lax.ppermute(x, axes, pairs)]
  transfers between devices with their start and end apart: 8 -> 8, of which waited for: 4 -> 4; matrix products, arithmetic and copies ran while one was open for 0% -> 0% of each run, Pallas kernels for 22% -> 27%
where the time goes in v3:
time: 65.9 us; the launch traced here: 65.7 us
  Pallas kernels  27.9 us (42%)
  starting transfers between devices  27 us (41%)
  waiting for transfers between devices  9.88 us (15%)
  between operations  0.91 us (1%)
    ppermute x6, starting transfers between devices, swap(): return lax.ppermute(x, axes, pairs)  15.4 us
    all_to_all x1, starting transfers between devices, steps(): parts = lax.all_to_all(sent, CHIPS, 0, 0, tiled=True)  9.68 us
    ppermute x6, waiting for transfers between devices, swap(): return lax.ppermute(x, axes, pairs)  9.06 us
    pallas_call x1, Pallas kernels, steps(): pl.pallas_call(lambda *refs: second_kernel(4, *refs), out_shape=(shaped(n...  9.04 us
    pallas_call x1, Pallas kernels, steps(): pl.pallas_call(lambda *refs: first_kernel(4, *refs), out_shape=(pltpu.HBM...  7.03 us
    pallas_call x1, Pallas kernels, steps(): pl.pallas_call(lambda *refs: core_kernel(rows_all, *refs), out_shape=shap...  4.26 us
    pallas_call x1, Pallas kernels, steps(): pl.pallas_call(lambda *refs: pack_columns_kernel(4, *refs), out_shape=(co...  2.96 us
    pallas_call x1, Pallas kernels, steps(): pl.pallas_call(window_kernel, out_shape=(pltpu.HBM((6 * nx + 16, ny), F32...  1.96 us
  transfers between devices with their start and end apart: 8, of which 4 were waited for; matrix products, arithmetic and copies ran while one was open for 0% of the time, Pallas kernels for 27%

profile of v3, /device:TPU:1, one launch (start us, length us, event | category | flops | bytes accessed | tf_op | source)
XLA Modules:
  0.0 65.7 jit_solution(17577456038428467492)
XLA Ops:
  0.6 0.0 copy-start
  0.6 3.0 %columns.1 = (f32[3,32,128]{2,1,0:T(8,128)S(1)}, f32[3,32,128]{2,1,0:T(8,128)S(1)}, f32[192,128]{1,0:T(8,128)S(1)}, f32[2,128,128]{2,1,0:T(8,128)S(1)}, f32[2,12...) custom-call(f32[4096,128]{1,0:T(8,128)} %bitcast.13, f32[2,32,128]{2,1,0:T(8,128)} %refs_5_.1), custom_call_target="tpu_custom_call" | custom-call | flops 1000000 | bytes 2097152 | tf_op jit(solution)/shard_map/columns/pallas_call | solution.py:541
  3.6 3.3 %collective-permute-start = (f32[3,32,128]{2,1,0:T(8,128)S(1)}, f32[3,32,128]{2,1,0:T(8,128)S(1)}, u32[]{:S(2)}, u32[]{:S(2)}) collective-permute-start(f32[3,32,128]{2,1,0:T(8,128)S(1)} %get-tuple-element.20), channel_id=1, source_target_pairs={{0,1},{1,0},{2,3},{3,2},{4,5},{5,4},{6,7},{7,6},{8,9},{9,8},{10,11... | collective-permute-start | bytes 147464 | tf_op jit(solution)/shard_map/ppermute | solution.py:526
  6.9 0.0 collective-permute-start.1
  6.9 0.9 %collective-permute-done.refs_3_.sides_near = f32[3,32,128]{2,1,0:T(8,128)S(1)} collective-permute-done((f32[3,32,128]{2,1,0:T(8,128)S(1)}, f32[3,32,128]{2,1,0:T(8,128)S(1)}, u32[]{:S(2)}, u32[]{:S(2)}) %collective-permute-start) | collective-permute-done | bytes 49184 | tf_op jit(solution)/shard_map/ppermute | solution.py:526
  7.8 2.6 %collective-permute-done.1.refs_4_.sides_far = f32[3,32,128]{2,1,0:T(8,128)S(1)} collective-permute-done((f32[3,32,128]{2,1,0:T(8,128)S(1)}, f32[3,32,128]{2,1,0:T(8,128)S(1)}, u32[]{:S(2)}, u32[]{:S(2)}) %collective-permute-start.1) | collective-permute-done | bytes 49184 | tf_op jit(solution)/shard_map/ppermute | solution.py:526
  10.4 0.0 copy-done
  10.4 0.1 collective-permute-start.4
  10.5 6.8 %collective-permute-start.5 = (f32[24,128]{1,0:T(8,128)S(1)}, f32[24,128]{1,0:T(8,128)S(1)}, u32[]{:S(2)}, u32[]{:S(2)}) collective-permute-start(f32[24,128]{1,0:T(8,128)S(1)} %get-tuple-element.30), channel_id=1, source_target_pairs={{8,16},{16,8},{24,32},{32,24},{40,48},{48,40},{56,64},{64,56},{72,... | collective-permute-start | bytes 36872 | tf_op jit(solution)/shard_map/ppermute | solution.py:526
  17.3 0.0 copy-start.1
  17.3 1.9 %load.1.basis = f32[94,64,128]{2,1,0:T(8,128)S(1)} custom-call(f32[94,64,128]{2,1,0:T(8,128)} %bitcast.11), custom_call_target="tpu_custom_call" | custom-call | bytes 6291456 | tf_op jit(solution)/shard_map/load/pallas_call | solution.py:563
  19.2 0.0 collective-permute-done.4.rows_near
  19.2 0.0 collective-permute-done.5.rows_far
  19.2 0.0 copy-done.1
  19.2 2.0 %window.1 = (f32[208,128]{1,0:T(8,128)}, f32[2,128]{1,0:T(2,128)S(1)}) custom-call(f32[128]{0:T(128)S(1)} %copy-done.1, f32[192,128]{1,0:T(8,128)S(1)} %get-tuple-element.25.window.near, f32[2,32,128]{2,1,0:T(8,128)S(1)} %copy-done, f32[1,128]{1,0:T(1,128)S(1)} %bitcast.8, f32[2,32,128]{2,1,0:T(8,128)S(1)} %get-tuple-element.26.mine, ...), custom_call_target="tpu_custom_call" | custom-call | flops 10000000 | bytes 4194304 | tf_op jit(solution)/shard_map/window/pallas_call | solution.py:581
  21.2 0.0 copy-start.2
  21.2 2.0 %collective-permute-start.6 = (f32[2,128]{1,0:T(2,128)S(1)}, f32[2,128]{1,0:T(2,128)S(1)}, u32[]{:S(2)}, u32[]{:S(2)}) collective-permute-start(f32[2,128]{1,0:T(2,128)S(1)} %get-tuple-element.34.mine), channel_id=1, source_target_pairs={{0,1},{1,0},{2,3},{3,2},{4,5},{5,4},{6,7},{7,6},{8,9},{9,8},{10,11... | collective-permute-start | bytes 3080 | tf_op jit(solution)/shard_map/ppermute | solution.py:595
  23.2 0.8 %collective-permute-done.6.other = f32[2,128]{1,0:T(2,128)S(1)} collective-permute-done((f32[2,128]{1,0:T(2,128)S(1)}, f32[2,128]{1,0:T(2,128)S(1)}, u32[]{:S(2)}, u32[]{:S(2)}) %collective-permute-start.6) | collective-permute-done | bytes 1056 | tf_op jit(solution)/shard_map/ppermute | solution.py:595
  24.0 0.7 %spread.1 = f32[128,2,128]{2,1,0:T(2,128)} custom-call(f32[2,128]{1,0:T(2,128)S(1)} %get-tuple-element.34.mine, f32[2,128]{1,0:T(2,128)S(1)} %collective-permute-done.6.other), custom_call_target="tpu_custom_call" | custom-call | flops 10000 | bytes 131072 | tf_op jit(solution)/shard_map/spread/pallas_call | solution.py:596
  24.7 9.7 %all-to-all-start = ((f32[128,2,128]{2,1,0:T(2,128)}), f32[128,2,128]{2,1,0:T(2,128)S(1)}, u32[]{:S(2)}, u32[]{:S(2)}) async-start(f32[128,2,128]{2,1,0:T(2,128)} %spread.1), calls=%async_computation | async-start | bytes 262144 | tf_op jit(solution)/shard_map/all_to_all | solution.py:600
  34.4 0.7 %collective-permute-start.2 = (f32[2,128,128]{2,1,0:T(8,128)S(1)}, f32[2,128,128]{2,1,0:T(8,128)S(1)}, u32[]{:S(2)}, u32[]{:S(2)}) collective-permute-start(f32[2,128,128]{2,1,0:T(8,128)S(1)} %get-tuple-element.22.refs_7_), channel_id=1, source_target_pairs={{0,8},{8,0},{16,24},{24,16},{32,40},{40,32},{48,56},{56,48},{64,72... | collective-permute-start | bytes 393224 | tf_op jit(solution)/shard_map/ppermute | solution.py:526
  35.0 4.6 %collective-permute-start.3 = (f32[2,128,128]{2,1,0:T(8,128)S(1)}, f32[2,128,128]{2,1,0:T(8,128)S(1)}, u32[]{:S(2)}, u32[]{:S(2)}) collective-permute-start(f32[2,128,128]{2,1,0:T(8,128)S(1)} %get-tuple-element.23.refs_8_), channel_id=1, source_target_pairs={{8,16},{16,8},{24,32},{32,24},{40,48},{48,40},{56,64},{64,56},{72,... | collective-permute-start | bytes 393224 | tf_op jit(solution)/shard_map/ppermute | solution.py:526
  39.6 0.0 collective-permute-done.2.refs_5_
  39.6 5.5 %collective-permute-done.3.refs_6_ = f32[2,128,128]{2,1,0:T(8,128)S(1)} collective-permute-done((f32[2,128,128]{2,1,0:T(8,128)S(1)}, f32[2,128,128]{2,1,0:T(8,128)S(1)}, u32[]{:S(2)}, u32[]{:S(2)}) %collective-permute-start.3) | collective-permute-done | bytes 131104 | tf_op jit(solution)/shard_map/ppermute | solution.py:526
  45.2 7.0 %first.1 = (f32[128,32,128]{2,1,0:T(8,128)}, f32[6,128,128]{2,1,0:T(8,128)}) custom-call(f32[128]{0:T(128)S(1)} %copy-done.1, f32[128,32,128]{2,1,0:T(8,128)} %refs_1_.3, f32[2,32,128]{2,1,0:T(8,128)S(1)} %copy-done, f32[3,32,128]{2,1,0:T(8,128)S(1)} %collective-permute-done.refs_3_.sides_near, f32[3,32,128]{2,1,0:T(8,128)S(1)} %collective-permute-done.1.refs_4_.sides_far, ...), custom_call_target="tpu_custom_call" | custom-call | flops 100000000 | bytes 4194304 | tf_op jit(solution)/shard_map/first/pallas_call | solution.py:570
  52.2 0.0 copy-done.2
  52.2 9.0 %second.1 = (f32[128,32,128]{2,1,0:T(8,128)}, bf16[32,96,256]{2,1,0:T(8,128)(2,1)S(1)}, bf16[32,96,256]{2,1,0:T(8,128)(2,1)S(1)}, f32[8,128]{1,0:T(8,128)S(1)}) custom-call(f32[128]{0:T(128)S(1)} %copy-done.1, f32[128,32,128]{2,1,0:T(8,128)} %get-tuple-element.24.refs_1_, f32[6016,128]{1,0:T(8,128)} %bitcast.12, f32[208,128]{1,0:T(8,128)} %get-tuple-element.31.refs_3_, ...), custom_call_target="tpu_custom_call" | custom-call | flops 100000000 | bytes 10485760 | tf_op jit(solution)/shard_map/second/pallas_call | solution.py:603
  61.3 0.0 all-to-all-done
  61.3 4.3 %core.1 = f32[96,64,128]{2,1,0:T(8,128)} custom-call(f32[32,8,128]{2,1,0:T(8,128)S(1)} %bitcast.7, f32[8,128]{1,0:T(8,128)S(1)} %get-tuple-element.35.refs_1_, bf16[32,96,256]{2,1,0:T(8,128)(2,1)S(1)} %get-tuple-element.36.refs_2_, bf16[32,96,256]{2,1,0:T(8,128)(2,1)S(1)} %get-tuple-element.37.refs_3_), custom_call_target="tpu_custom_call" | custom-call | flops 100000000 | bytes 6291456 | tf_op jit(solution)/shard_map/core/pallas_call | solution.py:617
  (1 shorter events, 0.0 us)
Async XLA Ops:
  0.6 9.8 %copy-start = (f32[2,32,128]{2,1,0:T(8,128)S(1)}, f32[2,32,128]{2,1,0:T(8,128)}, u32[]{:S(2)}) copy-start(f32[2,32,128]{2,1,0:T(8,128)} %refs_5_.1) | copy-start | bytes 98308
  3.6 4.2 %collective-permute-start = (f32[3,32,128]{2,1,0:T(8,128)S(1)}, f32[3,32,128]{2,1,0:T(8,128)S(1)}, u32[]{:S(2)}, u32[]{:S(2)}) collective-permute-start(f32[3,32,128]{2,1,0:T(8,128)S(1)} %get-tuple-element.20), channel_id=1, source_target_pairs={{0,1},{1,0},{2,3},{3,2},{4,5},{5,4},{6,7},{7,6},{8,9},{9,8},{10,11... | collective-permute-start | bytes 147464 | tf_op jit(solution)/shard_map/ppermute | solution.py:526
  6.9 3.5 %collective-permute-start.1 = (f32[3,32,128]{2,1,0:T(8,128)S(1)}, f32[3,32,128]{2,1,0:T(8,128)S(1)}, u32[]{:S(2)}, u32[]{:S(2)}) collective-permute-start(f32[3,32,128]{2,1,0:T(8,128)S(1)} %get-tuple-element.21), channel_id=1, source_target_pairs={{1,2},{2,1},{3,4},{4,3},{5,6},{6,5},{7,0},{0,7},{9,10},{10,9},{11,... | collective-permute-start | bytes 147464 | tf_op jit(solution)/shard_map/ppermute | solution.py:526
  10.4 8.8 %collective-permute-start.4 = (f32[24,128]{1,0:T(8,128)S(1)}, f32[24,128]{1,0:T(8,128)S(1)}, u32[]{:S(2)}, u32[]{:S(2)}) collective-permute-start(f32[24,128]{1,0:T(8,128)S(1)} %get-tuple-element.29), channel_id=1, source_target_pairs={{0,8},{8,0},{16,24},{24,16},{32,40},{40,32},{48,56},{56,48},{64,72... | collective-permute-start | bytes 36872 | tf_op jit(solution)/shard_map/ppermute | solution.py:526
  10.5 8.7 %collective-permute-start.5 = (f32[24,128]{1,0:T(8,128)S(1)}, f32[24,128]{1,0:T(8,128)S(1)}, u32[]{:S(2)}, u32[]{:S(2)}) collective-permute-start(f32[24,128]{1,0:T(8,128)S(1)} %get-tuple-element.30), channel_id=1, source_target_pairs={{8,16},{16,8},{24,32},{32,24},{40,48},{48,40},{56,64},{64,56},{72,... | collective-permute-start | bytes 36872 | tf_op jit(solution)/shard_map/ppermute | solution.py:526
  17.3 1.9 %copy-start.1 = (f32[128]{0:T(128)S(1)}, f32[128]{0:T(128)}, u32[]{:S(2)}) copy-start(f32[128]{0:T(128)} %refs_0_.3) | copy-start | bytes 1540
  21.2 31.0 %copy-start.2 = (f32[94]{0:T(128)S(1)}, f32[94]{0:T(128)}, u32[]{:S(2)}) copy-start(f32[94]{0:T(128)} %param.8) | copy-start | bytes 1132
  21.2 2.8 %collective-permute-start.6 = (f32[2,128]{1,0:T(2,128)S(1)}, f32[2,128]{1,0:T(2,128)S(1)}, u32[]{:S(2)}, u32[]{:S(2)}) collective-permute-start(f32[2,128]{1,0:T(2,128)S(1)} %get-tuple-element.34.mine), channel_id=1, source_target_pairs={{0,1},{1,0},{2,3},{3,2},{4,5},{5,4},{6,7},{7,6},{8,9},{9,8},{10,11... | collective-permute-start | bytes 3080 | tf_op jit(solution)/shard_map/ppermute | solution.py:595
  24.7 36.6 %all-to-all-start = ((f32[128,2,128]{2,1,0:T(2,128)}), f32[128,2,128]{2,1,0:T(2,128)S(1)}, u32[]{:S(2)}, u32[]{:S(2)}) async-start(f32[128,2,128]{2,1,0:T(2,128)} %spread.1), calls=%async_computation | async-start | bytes 262144 | tf_op jit(solution)/shard_map/all_to_all | solution.py:600
  34.4 5.3 %collective-permute-start.2 = (f32[2,128,128]{2,1,0:T(8,128)S(1)}, f32[2,128,128]{2,1,0:T(8,128)S(1)}, u32[]{:S(2)}, u32[]{:S(2)}) collective-permute-start(f32[2,128,128]{2,1,0:T(8,128)S(1)} %get-tuple-element.22.refs_7_), channel_id=1, source_target_pairs={{0,8},{8,0},{16,24},{24,16},{32,40},{40,32},{48,56},{56,48},{64,72... | collective-permute-start | bytes 393224 | tf_op jit(solution)/shard_map/ppermute | solution.py:526
  35.0 10.1 %collective-permute-start.3 = (f32[2,128,128]{2,1,0:T(8,128)S(1)}, f32[2,128,128]{2,1,0:T(8,128)S(1)}, u32[]{:S(2)}, u32[]{:S(2)}) collective-permute-start(f32[2,128,128]{2,1,0:T(8,128)S(1)} %get-tuple-element.23.refs_8_), channel_id=1, source_target_pairs={{8,16},{16,8},{24,32},{32,24},{40,48},{48,40},{56,64},{64,56},{72,... | collective-permute-start | bytes 393224 | tf_op jit(solution)/shard_map/ppermute | solution.py:526

commit v4 on v3

--- a/solution.py
+++ b/solution.py
@@ -244,27 +244,51 @@
         copy.wait()
 
 
-def split(basis, snaps, upper, lower):
-    rows, ny = snaps.shape[0] // 2, snaps.shape[1]
-    count = basis.shape[0] // rows
+def split(vectors, snaps, upper, lower):
+    rows, ny = vectors.shape[0], vectors.shape[2]
     for r in range(rows):
         pair, half = r // 2, r % 2
         lanes = slice(half * ny, (half + 1) * ny)
         v = jnp.concatenate(
-            [basis[pl.ds(r, count, stride=rows), :], snaps[pl.ds(r, 2, stride=rows), :]], axis=0
+            [vectors[r], snaps[r : r + 1, :], snaps[rows + r : rows + r + 1, :]], axis=0
         )
         hi = v.astype(BF16)
         upper[pair, :, lanes] = hi
         lower[pair, :, lanes] = (v - hi.astype(F32)).astype(BF16)
 
 
-def load_kernel(src, dst, sem):
-    copy = pltpu.make_async_copy(src, dst, sem)
-    copy.start()
-    copy.wait()
-
-
-def sweep(diff, velocity, src, dst, col_left, col_right, chunks, after_chunk):
+def load_kernel(src, dst, sems):
+    parts = sems.shape[0]
+    size = src.shape[0] // parts
+    copies = [
+        pltpu.make_async_copy(src.at[pl.ds(i * size, size)], dst.at[pl.ds(i * size, size)], sems.at[i])
+        for i in range(parts)
+    ]
+    for copy in copies:
+        copy.start()
+    for copy in copies:
+        copy.wait()
+
+
+def level_loads(src, dst, sems, chunks, nx):
+    pitch = nx + 16
+    nz = src.shape[0]
+    size = nz // chunks
+    view = dst.reshape(nz, pitch, dst.shape[1])
+
+    def copy(at, length, sem):
+        part = pl.ds(at, length)
+        return pltpu.make_async_copy(src.at[part], view.at[part, pl.ds(8, nx), :], sem)
+
+    def chunk(k):
+        return copy(k * size, size, sems.at[k])
+
+    end = copy(nz - size, size - 1, sems.at[chunks - 1])
+    last = copy(nz - 1, 1, sems.at[chunks])
+    return chunk, end, last
+
+
+def sweep(diff, velocity, src, dst, col_left, col_right, wait, after_block, chunks):
     nx, ny = velocity.shape[1:]
     pitch = nx + 16
     nz = src.shape[0] // pitch
@@ -301,102 +325,114 @@
         dst[rows_at(z, 0), :] = (c * (stay - 6.0 * d) + moved) + d * spread
         return (c, zp, *ahead)
 
-    def pair(i, state):
-        return level(2 * i + 1, 0, level(2 * i, 1, state))
+    def block(k, state):
+        wait(k)
+        for i in range(0, size, 2):
+            z = k * size + i
+            state = level(z + 1, 0, level(z, 1, state))
+        after_block(k)
+        return state
 
     c = src[rows_at(0, 0), :]
     state = (src[rows_at(nz - 1, 0), :], c, *turned(c, 0, 0))
-    for k in range(chunks):
-        state = lax.fori_loop(k * size // 2, (k + 1) * size // 2, pair, state, unroll=2)
-        after_chunk(k)
-
-
-def chunk_stores(src, out, sems, chunks, nx):
+    lax.fori_loop(0, chunks, block, state)
+
+
+def level_store(src, out, sems, chunks, nx):
     pitch = nx + 16
     nz = src.shape[0] // pitch
     size = nz // chunks
     view = src.reshape(nz, pitch, src.shape[1])
-    stores = []
 
     def store(k):
         part = pl.ds(k * size, size)
-        copy = pltpu.make_async_copy(view.at[part, pl.ds(8, nx), :], out.at[part], sems.at[k])
-        copy.start()
-        stores.append(copy)
-
-    return store, stores
-
-
-def first_kernel(
-    chunks, diff, tracer, velocity, sides_near, sides_far, rows_near, rows_far,
-    sent_near, sent_far, out, rows_out, now, then, rows, sems,
+        return pltpu.make_async_copy(view.at[part, pl.ds(8, nx), :], out.at[part], sems.at[k])
+
+    return store
+
+
+def start_loads(loads, chunks):
+    chunk, end, last = loads
+    last.start()
+    for k in range(chunks - 1):
+        chunk(k).start()
+    end.start()
+
+
+def bulk_kernel(
+    chunks, diff, tracer, basis, kept_hbm, rows_near, rows_far, velocity, diff_row, singular,
+    sides_near, sides_far, out, upper, lower, line, now, then, vectors, kept, got_near, got_far,
+    load_sems, store_sems, sems,
 ):
-    nz, nx, ny = tracer.shape
-    pitch = nx + 16
-    view = now.reshape(nz, pitch, ny)
-    load = pltpu.make_async_copy(tracer, view.at[:, pl.ds(8, nx), :], sems.at[chunks])
-    load.start()
-    even = gx_is_even()
-    for i in range(2):
-        rows[i], rows[2 + i] = from_pairs(even, rows_near[i], rows_far[i])
-    rows[4] = jnp.where(even, sent_far[0], sent_near[0])
-    rows[5] = jnp.where(even, sent_near[0], sent_far[0])
-    keep = pltpu.make_async_copy(rows, rows_out, sems.at[chunks + 1])
-    keep.start()
-    now[pl.ds(7, nz, stride=pitch), :] = rows[0]
-    now[pl.ds(8 + nx, nz, stride=pitch), :] = rows[2]
-    from_left, from_right = from_pairs(gy_is_even(), sides_near[0], sides_far[0])
-    load.wait()
-    store, stores = chunk_stores(then, out, sems, chunks, nx)
-    sweep(diff, velocity, now, then, from_left, from_right, chunks, store)
-    keep.wait()
-    for copy in stores:
-        copy.wait()
-
-
-def second_kernel(
-    chunks, diff, first, basis, kept_hbm, rows_hbm, velocity, diff_row, singular,
-    out, upper, lower, line, now, then, vectors, kept, rows, sems,
-):
-    nz, nx, ny = first.shape
+    nz, nx, _ = tracer.shape
     pitch = nx + 16
     count = singular.shape[1]
-    view = now.reshape(nz, pitch, ny)
-    loads = [
-        pltpu.make_async_copy(src, dst, sems.at[chunks + i])
-        for i, (src, dst) in enumerate((
-            (first, view.at[:, pl.ds(8, nx), :]), (kept_hbm, kept), (rows_hbm, rows),
-            (basis, vectors),
-        ))
+    small = [
+        pltpu.make_async_copy(src, dst, sems.at[i])
+        for i, (src, dst) in enumerate(
+            ((rows_near, got_near), (rows_far, got_far), (kept_hbm, kept))
+        )
     ]
-    for load in loads:
+    for load in small:
         load.start()
+    loads = level_loads(tracer, now, load_sems, chunks, nx)
+    start_loads(loads, chunks)
+    gathers = [
+        pltpu.make_async_copy(basis.at[:, r, 0, :], vectors.at[r], sems.at[3 + r])
+        for r in range(vectors.shape[0])
+    ]
+    for gather in gathers:
+        gather.start()
     line[...] = jnp.zeros_like(line)
     line[0:1, :count] = singular[...]
     eye = rows_of((nz, nz)) == lanes_of((nz, nz))
     d_all = jnp.sum(jnp.where(eye, diff_row[...], 0.0), axis=1, keepdims=True)
-    for load in loads[1:3]:
-        load.wait()
-    for i, own, is_top, at in ((0, 4, True, 6 * nx), (2, 5, False, 6 * nx + 8)):
+    small[0].wait()
+    small[1].wait()
+    even = gx_is_even()
+    from_up, from_down = from_pairs(even, got_near[0], got_far[0])
+    now[pl.ds(7, nz, stride=pitch), :] = from_up
+    now[pl.ds(8 + nx, nz, stride=pitch), :] = from_down
+    chunk, end, final = loads
+    final.wait()
+    chunk(0).wait()
+
+    def wait(k):
+        @pl.when(k < chunks - 2)
+        def _():
+            chunk(k + 1).wait()
+
+        @pl.when(k == chunks - 2)
+        def _():
+            end.wait()
+
+    from_left, from_right = from_pairs(gy_is_even(), sides_near[0], sides_far[0])
+    sweep(diff, velocity, now, then, from_left, from_right, wait, lambda k: None, chunks)
+    small[2].wait()
+    nearest = from_pairs(even, got_near[0], got_far[0])
+    beyonds = from_pairs(even, got_near[1], got_far[1])
+    for is_top, c, beyond, at in zip((True, False), nearest, beyonds, (6 * nx, 6 * nx + 8)):
         gin = kept[at : at + 8, :]
-        c, beyond, inside = rows[i], rows[i + 1], rows[own]
+        inside = now[pl.ds(8 if is_top else 7 + nx, nz, stride=pitch), :]
         xm, xp = (beyond, inside) if is_top else (inside, beyond)
         west = jnp.sum(jnp.where(eye, gin[2:3, :], 0.0), axis=1, keepdims=True)
         east = jnp.sum(jnp.where(eye, gin[3:4, :], 0.0), axis=1, keepdims=True)
         parts = signed_parts(gin[0:1, :], gin[1:2, :])
-        now[pl.ds(7 if is_top else 8 + nx, nz, stride=pitch), :] = step(
+        then[pl.ds(7 if is_top else 8 + nx, nz, stride=pitch), :] = step(
             c, xm, xp, before(c, west, 1), after(c, east, 1),
             pltpu.roll(c, 1, 0), pltpu.roll(c, nz - 1, 0), d_all, *parts
         )
-    loads[0].wait()
-    store, stores = chunk_stores(then, out, sems, chunks, nx)
+    store = level_store(now, out, store_sems, chunks, nx)
+    col_left, col_right = kept[4 * nx : 5 * nx, :], kept[5 * nx : 6 * nx, :]
     sweep(
-        diff, velocity, now, then, kept[4 * nx : 5 * nx, :], kept[5 * nx : 6 * nx, :], chunks, store
+        diff, velocity, then, now, col_left, col_right, lambda k: None,
+        lambda k: store(k).start(), chunks,
     )
-    loads[3].wait()
-    split(vectors, kept.at[0 : 4 * nx], upper, lower)
-    for copy in stores:
-        copy.wait()
+    for gather in gathers:
+        gather.wait()
+    split(vectors, kept, upper, lower)
+    for k in range(chunks):
+        store(k).wait()
 
 
 def spread_kernel(mine, other, out):
@@ -478,20 +514,16 @@
     both = jnp.concatenate([hi, lo], axis=0)
 
     size = count + 2
-    rows = out.shape[1]
-    view = block.reshape(size, rows, n)
     copies = []
-    for b in range(rows // 8):
-        for pair in range(4 * b, 4 * b + 4):
-            r = jnp.dot(both, upper[pair], preferred_element_type=F32)
-            r = r[:size] + r[size:] + jnp.dot(hi, lower[pair], preferred_element_type=F32)
-            for half in range(2):
-                at = pl.ds(2 * pair + half, size, stride=rows)
-                block[at, :] = r[:, half * n : (half + 1) * n]
-        part = pl.ds(8 * b, 8)
-        copy = pltpu.make_async_copy(view.at[:, part, :], out.at[:, part, :], sems.at[b])
-        copy.start()
-        copies.append(copy)
+    for pair in range(upper.shape[0]):
+        r = jnp.dot(both, upper[pair], preferred_element_type=F32)
+        r = r[:size] + r[size:] + jnp.dot(hi, lower[pair], preferred_element_type=F32)
+        for half in range(2):
+            at = 2 * pair + half
+            block[at] = r[:, half * n : (half + 1) * n]
+            copy = pltpu.make_async_copy(block.at[at], out.at[:, at, 0, :], sems.at[at])
+            copy.start()
+            copies.append(copy)
     for copy in copies:
         copy.wait()
 
@@ -539,18 +571,21 @@
     bulk_rows = shaped(2, nz, ny)
     hbm_space, any_space = (pl.BlockSpec(memory_space=m) for m in (pltpu.HBM, pl.ANY))
     columns_near, columns_far, near, sent_near, sent_far, mine = pl.pallas_call(
-        lambda *refs: pack_columns_kernel(4, *refs),
-        out_shape=(columns, columns, shaped(6 * nx, ny), bulk_rows, bulk_rows, shaped(2, nx, ny)),
+        lambda *refs: pack_columns_kernel(8, *refs),
+        out_shape=(
+            columns, columns, shaped(6 * nx, ny), bulk_rows, bulk_rows, shaped(2, nx, ny),
+        ),
         in_specs=[hbm_space] * 2, out_specs=tuple(whole(6)),
         scratch_shapes=[
-            VMEM((nz * nx, ny), F32), VMEM((2, nx, ny), F32), pltpu.SemaphoreType.DMA((5,)),
+            VMEM((nz * nx, ny), F32), VMEM((2, nx, ny), F32), pltpu.SemaphoreType.DMA((9,)),
         ],
         compiler_params=limit(4), cost_estimate=cost(10**6, 2 * 2**20), name="columns",
     )(in_hbm(tracer.reshape(nz * nx, ny)), in_hbm(velocity))
     sides_far = swap(columns_far, GY, True)
     sides_near = swap(columns_near, GY, False)
-    rows_far = swap(sent_far, GX, True)
-    rows_near = swap(sent_near, GX, False)
+    sent_near, sent_far = in_hbm(sent_near), in_hbm(sent_far)
+    rows_far = in_hbm(swap(sent_far, GX, True))
+    rows_near = in_hbm(swap(sent_near, GX, False))
 
     edge = shaped(24, ny)
     edges_near, edges_far, own_up, own_down = pl.pallas_call(
@@ -563,21 +598,9 @@
     vectors = pl.pallas_call(
         load_kernel, out_shape=shaped(count, rows, ny),
         in_specs=[hbm_space], out_specs=whole(1)[0],
-        scratch_shapes=[pltpu.SemaphoreType.DMA],
+        scratch_shapes=[pltpu.SemaphoreType.DMA((2,))],
         compiler_params=limit(2), cost_estimate=cost(0, 6 * 2**20), name="load",
     )(in_hbm(basis))
-    padded = VMEM((nz * (nx + 16), ny), F32)
-    first, rows_kept = pl.pallas_call(
-        lambda *refs: first_kernel(4, *refs),
-        out_shape=(pltpu.HBM((nz, nx, ny), F32), pltpu.HBM((6, nz, ny), F32)),
-        in_specs=[SMEM_SPEC, hbm_space] + whole(7), out_specs=(hbm_space, hbm_space),
-        scratch_shapes=[padded, padded, VMEM((6, nz, ny), F32), pltpu.SemaphoreType.DMA((6,))],
-        compiler_params=limit(8), cost_estimate=cost(10**8, 4 * 2**20), name="first",
-    )(
-        diffusivity, in_hbm(tracer), velocity, sides_near, sides_far, rows_near, rows_far,
-        sent_near, sent_far,
-    )
-
     kept, local = pl.pallas_call(
         window_kernel,
         out_shape=(pltpu.HBM((6 * nx + 16, ny), F32), shaped(2, ny)),
@@ -600,27 +623,30 @@
     parts = lax.all_to_all(sent, CHIPS, 0, 0, tiled=True)
 
     halves = shaped(rows // 2, count + 2, 2 * ny, dtype=BF16)
+    padded = VMEM((nz * (nx + 16), ny), F32)
     tracer_next, upper, lower, line = pl.pallas_call(
-        lambda *refs: second_kernel(4, *refs),
+        lambda *refs: bulk_kernel(8, *refs),
         out_shape=(shaped(nz, nx, ny), halves, halves, shaped(8, ny)),
-        in_specs=[SMEM_SPEC] + [hbm_space] * 4 + whole(3), out_specs=(any_space, *whole(3)),
+        in_specs=[SMEM_SPEC] + [hbm_space] * 3 + [hbm_space] * 2 + whole(5),
+        out_specs=(any_space, *whole(3)),
         scratch_shapes=[
-            padded, padded, VMEM((count * rows, ny), F32), VMEM((6 * nx + 16, ny), F32),
-            VMEM((6, nz, ny), F32), pltpu.SemaphoreType.DMA((8,)),
+            padded, padded, VMEM((rows, count, ny), F32), VMEM((6 * nx + 16, ny), F32),
+            VMEM((2, nz, ny), F32), VMEM((2, nz, ny), F32), pltpu.SemaphoreType.DMA((9,)),
+            pltpu.SemaphoreType.DMA((8,)), pltpu.SemaphoreType.DMA((3 + rows,)),
         ],
-        compiler_params=limit(12), cost_estimate=cost(10**8, 10 * 2**20), name="second",
+        compiler_params=limit(12), cost_estimate=cost(10**8, 10 * 2**20), name="bulk",
     )(
-        diffusivity, in_hbm(first), in_hbm(basis_vectors.reshape(count * rows, ny)), in_hbm(kept),
-        in_hbm(rows_kept), velocity, diff_row, singular.reshape(1, count),
+        diffusivity, in_hbm(tracer), in_hbm(basis.reshape(count, rows, 1, ny)), in_hbm(kept),
+        rows_near, rows_far, velocity, diff_row, singular.reshape(1, count), sides_near, sides_far,
     )
 
     basis_next = pl.pallas_call(
         lambda *refs: core_kernel(rows_all, *refs),
-        out_shape=shaped(count + 2, rows, ny),
+        out_shape=shaped(count + 2, rows, 1, ny),
         in_specs=whole(4), out_specs=pl.BlockSpec(memory_space=pl.ANY),
         scratch_shapes=[
-            VMEM(((count + 2) * rows, ny), F32),
-            pltpu.SemaphoreType.DMA((rows // 8,)),
+            VMEM((rows, count + 2, ny), F32),
+            pltpu.SemaphoreType.DMA((rows,)),
         ],
         compiler_params=limit(16), cost_estimate=cost(10**8, 6 * 2**20), name="core",
     )(

time: 65.9 us -> 58.5 us (0.89)
  Pallas kernels: 27.9 us -> 20 us
    pallas_call x3 -> x2, Pallas kernels: 19 us -> 12 us  [the longest x1 9.14 us: steps(): pl.pallas_call(lambda *refs: bulk_kernel(8, *refs), out_shape=(shaped(nz,...]
    pallas_call x1, Pallas kernels: 4.26 us -> 3.4 us  [steps(): pl.pallas_call(lambda *refs: core_kernel(rows_all, *refs), out_shape=shap...]
  transfers between devices with their start and end apart: 8 -> 8, of which waited for: 4 -> 4; matrix products, arithmetic and copies ran while one was open for 0% -> 0% of each run, Pallas kernels for 27% -> 19%
where the time goes in v4:
time: 58.5 us; the launch traced here: 58.3 us
  starting transfers between devices  27 us (46%)
  Pallas kernels  20 us (34%)
  waiting for transfers between devices  9.88 us (17%)
  between operations  0.74 us (1%)
  local copies, waits for them, and re-layouts  0.65 us (1%)
    ppermute x6, starting transfers between devices, swap(): return lax.ppermute(x, axes, pairs)  15.4 us
    all_to_all x1, starting transfers between devices, steps(): parts = lax.all_to_all(sent, CHIPS, 0, 0, tiled=True)  9.67 us
    pallas_call x1, Pallas kernels, steps(): pl.pallas_call(lambda *refs: bulk_kernel(8, *refs), out_shape=(shaped(nz,...  9.14 us
    ppermute x6, waiting for transfers between devices, swap(): return lax.ppermute(x, axes, pairs)  9.06 us
    pallas_call x1, Pallas kernels, steps(): pl.pallas_call(lambda *refs: core_kernel(rows_all, *refs), out_shape=shap...  3.4 us
    pallas_call x1, Pallas kernels, steps(): pl.pallas_call(lambda *refs: pack_columns_kernel(8, *refs), out_shape=(co...  2.91 us
    pallas_call x1, Pallas kernels, steps(): pl.pallas_call(window_kernel, out_shape=(pltpu.HBM((6 * nx + 16, ny), F32...  1.97 us
    ppermute x1, starting transfers between devices, steps(): other = lax.ppermute(local, 'c', [(0, 1), (1, 0)])  1.96 us
  transfers between devices with their start and end apart: 8, of which 4 were waited for; matrix products, arithmetic and copies ran while one was open for 0% of the time, Pallas kernels for 19%

profile of v4, /device:TPU:1, one launch (start us, length us, event | category | flops | bytes accessed | tf_op | source)
XLA Modules:
  0.0 58.3 jit_solution(2427377396511400996)
XLA Ops:
  0.6 0.0 copy-start
  0.6 2.9 %columns.1 = (f32[3,32,128]{2,1,0:T(8,128)S(1)}, f32[3,32,128]{2,1,0:T(8,128)S(1)}, f32[192,128]{1,0:T(8,128)S(1)}, f32[2,128,128]{2,1,0:T(8,128)S(1)}, f32[2,12...) custom-call(f32[4096,128]{1,0:T(8,128)} %bitcast.13, f32[2,32,128]{2,1,0:T(8,128)} %refs_6_.1), custom_call_target="tpu_custom_call" | custom-call | flops 1000000 | bytes 2097152 | tf_op jit(solution)/shard_map/columns/pallas_call | solution.py:573
  3.6 3.3 %collective-permute-start = (f32[3,32,128]{2,1,0:T(8,128)S(1)}, f32[3,32,128]{2,1,0:T(8,128)S(1)}, u32[]{:S(2)}, u32[]{:S(2)}) collective-permute-start(f32[3,32,128]{2,1,0:T(8,128)S(1)} %get-tuple-element.20), channel_id=1, source_target_pairs={{0,1},{1,0},{2,3},{3,2},{4,5},{5,4},{6,7},{7,6},{8,9},{9,8},{10,11... | collective-permute-start | bytes 147464 | tf_op jit(solution)/shard_map/ppermute | solution.py:558
  6.8 0.0 collective-permute-start.1
  6.8 0.9 %collective-permute-done.sides_near.refs_9_ = f32[3,32,128]{2,1,0:T(8,128)S(1)} collective-permute-done((f32[3,32,128]{2,1,0:T(8,128)S(1)}, f32[3,32,128]{2,1,0:T(8,128)S(1)}, u32[]{:S(2)}, u32[]{:S(2)}) %collective-permute-start) | collective-permute-done | bytes 49184 | tf_op jit(solution)/shard_map/ppermute | solution.py:558
  7.7 2.6 %collective-permute-done.1.sides_far.refs_10_ = f32[3,32,128]{2,1,0:T(8,128)S(1)} collective-permute-done((f32[3,32,128]{2,1,0:T(8,128)S(1)}, f32[3,32,128]{2,1,0:T(8,128)S(1)}, u32[]{:S(2)}, u32[]{:S(2)}) %collective-permute-start.1) | collective-permute-done | bytes 49184 | tf_op jit(solution)/shard_map/ppermute | solution.py:558
  10.4 0.0 copy-done
  10.4 0.1 collective-permute-start.2
  10.5 6.8 %collective-permute-start.3 = (f32[24,128]{1,0:T(8,128)S(1)}, f32[24,128]{1,0:T(8,128)S(1)}, u32[]{:S(2)}, u32[]{:S(2)}) collective-permute-start(f32[24,128]{1,0:T(8,128)S(1)} %get-tuple-element.25), channel_id=1, source_target_pairs={{8,16},{16,8},{24,32},{32,24},{40,48},{48,40},{56,64},{64,56},{72,... | collective-permute-start | bytes 36872 | tf_op jit(solution)/shard_map/ppermute | solution.py:558
  17.3 0.0 copy-start.1
  17.3 1.9 %load.1.basis = f32[94,64,128]{2,1,0:T(8,128)S(1)} custom-call(f32[94,64,128]{2,1,0:T(8,128)} %bitcast.11), custom_call_target="tpu_custom_call" | custom-call | bytes 6291456 | tf_op jit(solution)/shard_map/load/pallas_call | solution.py:598
  19.2 0.0 copy-start.2
  19.2 0.0 collective-permute-done.2.rows_near
  19.2 0.0 collective-permute-done.3.rows_far
  19.2 0.0 copy-done.1
  19.2 2.0 %window.1 = (f32[208,128]{1,0:T(8,128)}, f32[2,128]{1,0:T(2,128)S(1)}) custom-call(f32[128]{0:T(128)S(1)} %copy-done.1, f32[192,128]{1,0:T(8,128)S(1)} %get-tuple-element.18.window.near, f32[2,32,128]{2,1,0:T(8,128)S(1)} %copy-done, f32[1,128]{1,0:T(1,128)S(1)} %bitcast.8, f32[2,32,128]{2,1,0:T(8,128)S(1)} %get-tuple-element.19.mine, ...), custom_call_target="tpu_custom_call" | custom-call | flops 10000000 | bytes 4194304 | tf_op jit(solution)/shard_map/window/pallas_call | solution.py:604
  21.2 2.0 %collective-permute-start.6 = (f32[2,128]{1,0:T(2,128)S(1)}, f32[2,128]{1,0:T(2,128)S(1)}, u32[]{:S(2)}, u32[]{:S(2)}) collective-permute-start(f32[2,128]{1,0:T(2,128)S(1)} %get-tuple-element.30.mine), channel_id=1, source_target_pairs={{0,1},{1,0},{2,3},{3,2},{4,5},{5,4},{6,7},{7,6},{8,9},{9,8},{10,11... | collective-permute-start | bytes 3080 | tf_op jit(solution)/shard_map/ppermute | solution.py:618
  23.1 0.8 %collective-permute-done.6.other = f32[2,128]{1,0:T(2,128)S(1)} collective-permute-done((f32[2,128]{1,0:T(2,128)S(1)}, f32[2,128]{1,0:T(2,128)S(1)}, u32[]{:S(2)}, u32[]{:S(2)}) %collective-permute-start.6) | collective-permute-done | bytes 1056 | tf_op jit(solution)/shard_map/ppermute | solution.py:618
  24.0 0.7 %spread.1 = f32[128,2,128]{2,1,0:T(2,128)} custom-call(f32[2,128]{1,0:T(2,128)S(1)} %get-tuple-element.30.mine, f32[2,128]{1,0:T(2,128)S(1)} %collective-permute-done.6.other), custom_call_target="tpu_custom_call" | custom-call | flops 10000 | bytes 131072 | tf_op jit(solution)/shard_map/spread/pallas_call | solution.py:619
  24.6 9.7 %all-to-all-start = ((f32[128,2,128]{2,1,0:T(2,128)}), f32[128,2,128]{2,1,0:T(2,128)S(1)}, u32[]{:S(2)}, u32[]{:S(2)}) async-start(f32[128,2,128]{2,1,0:T(2,128)} %spread.1), calls=%async_computation | async-start | bytes 262144 | tf_op jit(solution)/shard_map/all_to_all | solution.py:623
  34.3 0.7 %collective-permute-start.4 = (f32[2,128,128]{2,1,0:T(8,128)S(1)}, f32[2,128,128]{2,1,0:T(8,128)S(1)}, u32[]{:S(2)}, u32[]{:S(2)}) collective-permute-start(f32[2,128,128]{2,1,0:T(8,128)S(1)} %get-tuple-element.27), channel_id=1, source_target_pairs={{0,8},{8,0},{16,24},{24,16},{32,40},{40,32},{48,56},{56,48},{64,72... | collective-permute-start | bytes 393224 | tf_op jit(solution)/shard_map/ppermute | solution.py:558
  35.0 4.6 %collective-permute-start.5 = (f32[2,128,128]{2,1,0:T(8,128)S(1)}, f32[2,128,128]{2,1,0:T(8,128)S(1)}, u32[]{:S(2)}, u32[]{:S(2)}) collective-permute-start(f32[2,128,128]{2,1,0:T(8,128)S(1)} %get-tuple-element.28), channel_id=1, source_target_pairs={{8,16},{16,8},{24,32},{32,24},{40,48},{48,40},{56,64},{64,56},{72,... | collective-permute-start | bytes 393224 | tf_op jit(solution)/shard_map/ppermute | solution.py:558
  39.6 0.0 collective-permute-done.4.refs_4_
  39.6 0.0 copy-start.3
  39.6 5.5 %collective-permute-done.5.refs_5_ = f32[2,128,128]{2,1,0:T(8,128)S(1)} collective-permute-done((f32[2,128,128]{2,1,0:T(8,128)S(1)}, f32[2,128,128]{2,1,0:T(8,128)S(1)}, u32[]{:S(2)}, u32[]{:S(2)}) %collective-permute-start.5) | collective-permute-done | bytes 131104 | tf_op jit(solution)/shard_map/ppermute | solution.py:558
  45.1 0.0 copy-start.4
  45.1 0.0 copy-done.3
  45.1 0.6 %copy-done.4 = f32[2,128,128]{2,1,0:T(8,128)} copy-done((f32[2,128,128]{2,1,0:T(8,128)}, f32[2,128,128]{2,1,0:T(8,128)S(1)}, u32[]{:S(2)}) %copy-start.4) | copy-done | bytes 131096
  45.8 0.0 copy-done.2
  45.8 9.1 %bulk.1 = (f32[128,32,128]{2,1,0:T(8,128)}, bf16[32,96,256]{2,1,0:T(8,128)(2,1)S(1)}, bf16[32,96,256]{2,1,0:T(8,128)(2,1)S(1)}, f32[8,128]{1,0:T(8,128)S(1)}) custom-call(f32[128]{0:T(128)S(1)} %copy-done.1, f32[128,32,128]{2,1,0:T(8,128)} %refs_1_.3, f32[94,64,1,128]{3,2,1,0:T(1,128)} %bitcast.12, f32[208,128]{1,0:T(8,128)} %get-tuple-element.26.refs_3_, ...), custom_call_target="tpu_custom_call" | custom-call | flops 100000000 | bytes 10485760 | tf_op jit(solution)/shard_map/bulk/pallas_call | solution.py:627
  54.9 0.0 all-to-all-done
  54.9 3.4 %core.1 = f32[96,64,1,128]{3,2,1,0:T(1,128)} custom-call(f32[32,8,128]{2,1,0:T(8,128)S(1)} %bitcast.7, f32[8,128]{1,0:T(8,128)S(1)} %get-tuple-element.31.refs_1_, bf16[32,96,256]{2,1,0:T(8,128)(2,1)S(1)} %get-tuple-element.32.refs_2_, bf16[32,96,256]{2,1,0:T(8,128)(2,1)S(1)} %get-tuple-element.33.refs_3_), custom_call_target="tpu_custom_call" | custom-call | flops 100000000 | bytes 6291456 | tf_op jit(solution)/shard_map/core/pallas_call | solution.py:643
  (1 shorter events, 0.0 us)
Async XLA Ops:
  0.6 9.7 %copy-start = (f32[2,32,128]{2,1,0:T(8,128)S(1)}, f32[2,32,128]{2,1,0:T(8,128)}, u32[]{:S(2)}) copy-start(f32[2,32,128]{2,1,0:T(8,128)} %refs_6_.1) | copy-start | bytes 98308
  3.6 4.2 %collective-permute-start = (f32[3,32,128]{2,1,0:T(8,128)S(1)}, f32[3,32,128]{2,1,0:T(8,128)S(1)}, u32[]{:S(2)}, u32[]{:S(2)}) collective-permute-start(f32[3,32,128]{2,1,0:T(8,128)S(1)} %get-tuple-element.20), channel_id=1, source_target_pairs={{0,1},{1,0},{2,3},{3,2},{4,5},{5,4},{6,7},{7,6},{8,9},{9,8},{10,11... | collective-permute-start | bytes 147464 | tf_op jit(solution)/shard_map/ppermute | solution.py:558
  6.8 3.5 %collective-permute-start.1 = (f32[3,32,128]{2,1,0:T(8,128)S(1)}, f32[3,32,128]{2,1,0:T(8,128)S(1)}, u32[]{:S(2)}, u32[]{:S(2)}) collective-permute-start(f32[3,32,128]{2,1,0:T(8,128)S(1)} %get-tuple-element.21), channel_id=1, source_target_pairs={{1,2},{2,1},{3,4},{4,3},{5,6},{6,5},{7,0},{0,7},{9,10},{10,9},{11,... | collective-permute-start | bytes 147464 | tf_op jit(solution)/shard_map/ppermute | solution.py:558
  10.4 8.8 %collective-permute-start.2 = (f32[24,128]{1,0:T(8,128)S(1)}, f32[24,128]{1,0:T(8,128)S(1)}, u32[]{:S(2)}, u32[]{:S(2)}) collective-permute-start(f32[24,128]{1,0:T(8,128)S(1)} %get-tuple-element.24), channel_id=1, source_target_pairs={{0,8},{8,0},{16,24},{24,16},{32,40},{40,32},{48,56},{56,48},{64,72... | collective-permute-start | bytes 36872 | tf_op jit(solution)/shard_map/ppermute | solution.py:558
  10.5 8.7 %collective-permute-start.3 = (f32[24,128]{1,0:T(8,128)S(1)}, f32[24,128]{1,0:T(8,128)S(1)}, u32[]{:S(2)}, u32[]{:S(2)}) collective-permute-start(f32[24,128]{1,0:T(8,128)S(1)} %get-tuple-element.25), channel_id=1, source_target_pairs={{8,16},{16,8},{24,32},{32,24},{40,48},{48,40},{56,64},{64,56},{72,... | collective-permute-start | bytes 36872 | tf_op jit(solution)/shard_map/ppermute | solution.py:558
  17.3 1.9 %copy-start.1 = (f32[128]{0:T(128)S(1)}, f32[128]{0:T(128)}, u32[]{:S(2)}) copy-start(f32[128]{0:T(128)} %refs_0_.1) | copy-start | bytes 1540
  19.2 26.6 %copy-start.2 = (f32[94]{0:T(128)S(1)}, f32[94]{0:T(128)}, u32[]{:S(2)}) copy-start(f32[94]{0:T(128)} %param.8) | copy-start | bytes 1132
  21.2 2.8 %collective-permute-start.6 = (f32[2,128]{1,0:T(2,128)S(1)}, f32[2,128]{1,0:T(2,128)S(1)}, u32[]{:S(2)}, u32[]{:S(2)}) collective-permute-start(f32[2,128]{1,0:T(2,128)S(1)} %get-tuple-element.30.mine), channel_id=1, source_target_pairs={{0,1},{1,0},{2,3},{3,2},{4,5},{5,4},{6,7},{7,6},{8,9},{9,8},{10,11... | collective-permute-start | bytes 3080 | tf_op jit(solution)/shard_map/ppermute | solution.py:618
  24.6 30.3 %all-to-all-start = ((f32[128,2,128]{2,1,0:T(2,128)}), f32[128,2,128]{2,1,0:T(2,128)S(1)}, u32[]{:S(2)}, u32[]{:S(2)}) async-start(f32[128,2,128]{2,1,0:T(2,128)} %spread.1), calls=%async_computation | async-start | bytes 262144 | tf_op jit(solution)/shard_map/all_to_all | solution.py:623
  34.3 5.3 %collective-permute-start.4 = (f32[2,128,128]{2,1,0:T(8,128)S(1)}, f32[2,128,128]{2,1,0:T(8,128)S(1)}, u32[]{:S(2)}, u32[]{:S(2)}) collective-permute-start(f32[2,128,128]{2,1,0:T(8,128)S(1)} %get-tuple-element.27), channel_id=1, source_target_pairs={{0,8},{8,0},{16,24},{24,16},{32,40},{40,32},{48,56},{56,48},{64,72... | collective-permute-start | bytes 393224 | tf_op jit(solution)/shard_map/ppermute | solution.py:558
  35.0 10.1 %collective-permute-start.5 = (f32[2,128,128]{2,1,0:T(8,128)S(1)}, f32[2,128,128]{2,1,0:T(8,128)S(1)}, u32[]{:S(2)}, u32[]{:S(2)}) collective-permute-start(f32[2,128,128]{2,1,0:T(8,128)S(1)} %get-tuple-element.28), channel_id=1, source_target_pairs={{8,16},{16,8},{24,32},{32,24},{40,48},{48,40},{56,64},{64,56},{72,... | collective-permute-start | bytes 393224 | tf_op jit(solution)/shard_map/ppermute | solution.py:558
  39.6 5.5 %copy-start.3 = (f32[2,128,128]{2,1,0:T(8,128)}, f32[2,128,128]{2,1,0:T(8,128)S(1)}, u32[]{:S(2)}) copy-start(f32[2,128,128]{2,1,0:T(8,128)S(1)} %collective-permute-done.4.refs_4_) | copy-start | bytes 393220
  45.1 0.6 %copy-start.4 = (f32[2,128,128]{2,1,0:T(8,128)}, f32[2,128,128]{2,1,0:T(8,128)S(1)}, u32[]{:S(2)}) copy-start(f32[2,128,128]{2,1,0:T(8,128)S(1)} %collective-permute-done.5.refs_5_) | copy-start | bytes 393220

commit v5 on v4

--- a/solution.py
+++ b/solution.py
@@ -66,60 +66,71 @@
 
 
 def pack_columns_kernel(
-    chunks, tracer_hbm, velocity_hbm, near, far, window, rows_near, rows_far, mine,
-    tracer, velocity, sems,
+    chunks, tracer_hbm, by_row_hbm, velocity_hbm, near, far, window, tops, bottoms, mine, velocity,
+    tracer, sems,
 ):
     nx, ny = velocity.shape[1:]
     nz = tracer.shape[0] // nx
     size = nz // chunks
-    loads = [
-        pltpu.make_async_copy(
-            tracer_hbm.at[pl.ds(i * size * nx, size * nx)],
-            tracer.at[pl.ds(i * size * nx, size * nx)], sems.at[i],
-        )
+
+    def rows_of_level(at, count, dst):
+        return tracer_hbm.at[pl.ds(at * nx, count * nx)], dst
+
+    moves = [
+        rows_of_level(i * size, size, tracer.at[pl.ds(i * size * nx, size * nx)])
         for i in range(chunks)
     ]
-    loads.append(pltpu.make_async_copy(velocity_hbm, velocity, sems.at[chunks]))
+    moves.append((velocity_hbm, velocity))
+    moves.append(rows_of_level(nz - 2, 2, window.at[0 : 2 * nx]))
+    moves.append(rows_of_level(0, 4, window.at[2 * nx : 6 * nx]))
+    for i in range(2):
+        part = pl.ds(i * nz, nz)
+        moves.append((by_row_hbm.at[:, i, 0, :], tops.at[part]))
+        moves.append((by_row_hbm.at[:, nx - 1 - i, 0, :], bottoms.at[part]))
+    loads = [pltpu.make_async_copy(src, dst, sems.at[i]) for i, (src, dst) in enumerate(moves)]
     for load in loads:
         load.start()
     lane = lanes_of((nx, ny))
 
-    def level(z, carry):
-        a, b, y, w = carry
-        r = pltpu.roll(tracer[pl.ds(pl.multiple_of(z * nx, nx), nx), :], z, 1)
-        rel = (lane - z) & (ny - 1)
-        a = jnp.where(rel == 0, r, a)
-        b = jnp.where(rel == 1, r, b)
-        y = jnp.where(rel == ny - 1, r, y)
-        w = jnp.where(rel == ny - 2, r, w)
-        return a, b, y, w
+    def four(i, carry):
+        out = []
+        for j in range(4):
+            z = 4 * i + j
+            r = pltpu.roll(tracer[z * nx : (z + 1) * nx], z, 1)
+            out.append(jnp.where(((lane - z + 2) & (ny - 1)) < 4, r, carry[j]))
+        return tuple(out)
 
     carry = (jnp.zeros((nx, ny), F32),) * 4
     for i in range(chunks):
         loads[i].wait()
-        carry = lax.fori_loop(i * size, (i + 1) * size, level, carry, unroll=8)
-    a, b, y, w = carry
+        for k in range(i * size // 4, (i + 1) * size // 4):
+            carry = four(k, carry)
+    phase = lane & 3
+
+    def column(shift):
+        c = [pltpu.roll(x, shift, 1) if shift else x for x in carry]
+        return jnp.where(
+            phase < 2, jnp.where(phase == 0, c[0], c[1]), jnp.where(phase == 2, c[2], c[3])
+        )
+
     loads[chunks].wait()
     vx, vy = velocity[0], velocity[1]
-    left = (a, pltpu.roll(b, ny - 1, 1), jnp.where(lane == 0, vx, pltpu.roll(vy, 1, 1)))
+    left = (column(0), column(ny - 1), jnp.where(lane == 0, vx, pltpu.roll(vy, 1, 1)))
     right = (
-        pltpu.roll(y, 1, 1), pltpu.roll(w, 2, 1),
+        column(1), column(2),
         jnp.where(lane == ny - 1, vx, pltpu.roll(vy, ny - 1, 1)),
     )
     even = gy_is_even()
     for i in range(3):
         near[i], far[i] = to_pairs(even, left[i], right[i])
     mine[0], mine[1] = left[0], right[0]
-    window[0 : 2 * nx] = tracer[(nz - 2) * nx : nz * nx]
-    window[2 * nx : 6 * nx] = tracer[0 : 4 * nx]
-    even = gx_is_even()
-    for i in range(2):
-        top = tracer[pl.ds(i, nz, stride=nx), :]
-        bottom = tracer[pl.ds(nx - 1 - i, nz, stride=nx), :]
-        rows_near[i], rows_far[i] = to_pairs(even, top, bottom)
-
-
-def pack_rows_kernel(window, velocity, sides_near, sides_far, near, far, up, down):
+    for load in loads[chunks + 1 :]:
+        load.wait()
+
+
+def pack_rows_kernel(
+    window, velocity, tops, bottoms, sides_near, sides_far, near, far, up, down
+):
     nx, ny = velocity.shape[1:]
     from_left, from_right = from_pairs(gy_is_even(), sides_near[0], sides_far[0])
     for edge, inner, out in ((0, 1, up), (nx - 1, nx - 2, down)):
@@ -132,13 +143,15 @@
         out[17:18, :] = velocity[1, edge : edge + 1, :]
         out[18:19, :] = from_left[edge : edge + 1, :]
         out[19:20, :] = from_right[edge : edge + 1, :]
-    near[...], far[...] = to_pairs(gx_is_even(), up[...], down[...])
+    even = gx_is_even()
+    near[0:24], far[0:24] = to_pairs(even, up[...], down[...])
+    near[24:], far[24:] = to_pairs(even, tops[...], bottoms[...])
 
 
 def window_kernel(
     diff, near, velocity, diff_row, mine, sides_near, sides_far,
     own_up, own_down, rows_near, rows_far, basis,
-    kept_hbm, sums, snaps, sides, q0, q1, sems,
+    kept_hbm, sums, near_hbm, far_hbm, snaps, sides, q0, q1, sems,
 ):
     nz, nx, ny = diff.shape[0], velocity.shape[1], velocity.shape[2]
     count = basis.shape[0]
@@ -146,7 +159,7 @@
     even = gy_is_even()
     pairs = [from_pairs(even, sides_near[i], sides_far[i]) for i in range(3)]
     from_left, from_right = [p[0] for p in pairs], [p[1] for p in pairs]
-    from_up, from_down = from_pairs(gx_is_even(), rows_near[...], rows_far[...])
+    from_up, from_down = from_pairs(gx_is_even(), rows_near[0:24], rows_far[0:24])
     for gin, inner, outer, corner, vx_at, vy_at, out in (
         (from_left, None, mine[0], 18, ny - 1, ny - 2, sides.at[0:nx]),
         (from_right, mine[1], None, 19, 0, 1, sides.at[nx : 2 * nx]),
@@ -209,6 +222,9 @@
             ((snaps.at[0], 0), (snaps.at[1], rows), (sides, 2 * rows))
         )
     ]
+    bulk = pl.ds(24, 2 * nz)
+    keep.append(pltpu.make_async_copy(rows_near.at[bulk], near_hbm, sems.at[3]))
+    keep.append(pltpu.make_async_copy(rows_far.at[bulk], far_hbm, sems.at[4]))
     for copy in keep:
         copy.start()
 
@@ -244,8 +260,9 @@
         copy.wait()
 
 
-def split(vectors, snaps, upper, lower):
+def split(vectors, snaps, halves):
     rows, ny = vectors.shape[0], vectors.shape[2]
+    size = halves.shape[1] // 2
     for r in range(rows):
         pair, half = r // 2, r % 2
         lanes = slice(half * ny, (half + 1) * ny)
@@ -253,8 +270,8 @@
             [vectors[r], snaps[r : r + 1, :], snaps[rows + r : rows + r + 1, :]], axis=0
         )
         hi = v.astype(BF16)
-        upper[pair, :, lanes] = hi
-        lower[pair, :, lanes] = (v - hi.astype(F32)).astype(BF16)
+        halves[pair, :size, lanes] = hi
+        halves[pair, size:, lanes] = (v - hi.astype(F32)).astype(BF16)
 
 
 def load_kernel(src, dst, sems):
@@ -361,7 +378,7 @@
 
 def bulk_kernel(
     chunks, diff, tracer, basis, kept_hbm, rows_near, rows_far, velocity, diff_row, singular,
-    sides_near, sides_far, out, upper, lower, line, now, then, vectors, kept, got_near, got_far,
+    sides_near, sides_far, out, halves, line, now, then, vectors, kept, got_near, got_far,
     load_sems, store_sems, sems,
 ):
     nz, nx, _ = tracer.shape
@@ -390,7 +407,7 @@
     small[0].wait()
     small[1].wait()
     even = gx_is_even()
-    from_up, from_down = from_pairs(even, got_near[0], got_far[0])
+    from_up, from_down = from_pairs(even, got_near[0:nz], got_far[0:nz])
     now[pl.ds(7, nz, stride=pitch), :] = from_up
     now[pl.ds(8 + nx, nz, stride=pitch), :] = from_down
     chunk, end, final = loads
@@ -409,8 +426,8 @@
     from_left, from_right = from_pairs(gy_is_even(), sides_near[0], sides_far[0])
     sweep(diff, velocity, now, then, from_left, from_right, wait, lambda k: None, chunks)
     small[2].wait()
-    nearest = from_pairs(even, got_near[0], got_far[0])
-    beyonds = from_pairs(even, got_near[1], got_far[1])
+    nearest = from_pairs(even, got_near[0:nz], got_far[0:nz])
+    beyonds = from_pairs(even, got_near[nz:], got_far[nz:])
     for is_top, c, beyond, at in zip((True, False), nearest, beyonds, (6 * nx, 6 * nx + 8)):
         gin = kept[at : at + 8, :]
         inside = now[pl.ds(8 if is_top else 7 + nx, nz, stride=pitch), :]
@@ -430,7 +447,7 @@
     )
     for gather in gathers:
         gather.wait()
-    split(vectors, kept, upper, lower)
+    split(vectors, kept, halves)
     for k in range(chunks):
         store(k).wait()
 
@@ -440,7 +457,7 @@
     out[...] = jnp.broadcast_to(both[None], out.shape)
 
 
-def core_kernel(rows_all, parts, singular, upper, lower, out, block, sems):
+def core_kernel(rows_all, parts, singular, halves, out, block, sems):
     count = out.shape[0] - 2
     n = parts.shape[2]
     total = jnp.sum(parts[...], axis=0)
@@ -511,19 +528,23 @@
     full = full[: count + 2, : count + 2]
     hi = full.astype(BF16)
     lo = (full - hi.astype(F32)).astype(BF16)
-    both = jnp.concatenate([hi, lo], axis=0)
-
+    twice = jnp.concatenate([hi, hi], axis=1)
     size = count + 2
+    blocks = block.shape[1] // 8
     copies = []
-    for pair in range(upper.shape[0]):
-        r = jnp.dot(both, upper[pair], preferred_element_type=F32)
-        r = r[:size] + r[size:] + jnp.dot(hi, lower[pair], preferred_element_type=F32)
-        for half in range(2):
-            at = 2 * pair + half
-            block[at] = r[:, half * n : (half + 1) * n]
-            copy = pltpu.make_async_copy(block.at[at], out.at[:, at, 0, :], sems.at[at])
-            copy.start()
-            copies.append(copy)
+    for b in range(blocks):
+        tiles = []
+        for pair in range(4 * b, 4 * b + 4):
+            r = jnp.dot(twice, halves[pair], preferred_element_type=F32)
+            r = r + jnp.dot(lo, halves[pair, :size], preferred_element_type=F32)
+            tiles.append(r[:, :n])
+            tiles.append(r[:, n:])
+        block[:, 8 * b : 8 * b + 8, :] = jnp.swapaxes(jnp.stack(tiles), 0, 1)
+        copy = pltpu.make_async_copy(
+            block.at[:, pl.ds(8 * b, 8), :], out.at[:, pl.ds(8 * b, 8), :], sems.at[b]
+        )
+        copy.start()
+        copies.append(copy)
     for copy in copies:
         copy.wait()
 
@@ -568,30 +589,30 @@
     diff_row = diffusivity.reshape(1, nz)
 
     columns = shaped(3, nx, ny)
-    bulk_rows = shaped(2, nz, ny)
+    bulk_rows = shaped(2 * nz, ny)
     hbm_space, any_space = (pl.BlockSpec(memory_space=m) for m in (pltpu.HBM, pl.ANY))
-    columns_near, columns_far, near, sent_near, sent_far, mine = pl.pallas_call(
-        lambda *refs: pack_columns_kernel(8, *refs),
+    columns_near, columns_far, near, tops, bottoms, mine, speeds = pl.pallas_call(
+        lambda *refs: pack_columns_kernel(4, *refs),
         out_shape=(
             columns, columns, shaped(6 * nx, ny), bulk_rows, bulk_rows, shaped(2, nx, ny),
+            shaped(2, nx, ny),
         ),
-        in_specs=[hbm_space] * 2, out_specs=tuple(whole(6)),
+        in_specs=[hbm_space] * 3, out_specs=tuple(whole(7)),
         scratch_shapes=[
-            VMEM((nz * nx, ny), F32), VMEM((2, nx, ny), F32), pltpu.SemaphoreType.DMA((9,)),
+            VMEM((nz * nx, ny), F32), pltpu.SemaphoreType.DMA((11,)),
         ],
         compiler_params=limit(4), cost_estimate=cost(10**6, 2 * 2**20), name="columns",
-    )(in_hbm(tracer.reshape(nz * nx, ny)), in_hbm(velocity))
+    )(
+        in_hbm(tracer.reshape(nz * nx, ny)), in_hbm(tracer.reshape(nz, nx, 1, ny)), in_hbm(velocity)
+    )
     sides_far = swap(columns_far, GY, True)
     sides_near = swap(columns_near, GY, False)
-    sent_near, sent_far = in_hbm(sent_near), in_hbm(sent_far)
-    rows_far = in_hbm(swap(sent_far, GX, True))
-    rows_near = in_hbm(swap(sent_near, GX, False))
-
-    edge = shaped(24, ny)
+    edge, message = shaped(24, ny), shaped(24 + 2 * nz, ny)
     edges_near, edges_far, own_up, own_down = pl.pallas_call(
-        pack_rows_kernel, out_shape=(edge,) * 4, in_specs=whole(4), out_specs=tuple(whole(4)),
+        pack_rows_kernel, out_shape=(message, message, edge, edge),
+        in_specs=whole(6), out_specs=tuple(whole(4)),
         compiler_params=limit(2), cost_estimate=cost(10**4, 2**17), name="edges",
-    )(near, velocity, sides_near, sides_far)
+    )(near, speeds, tops, bottoms, sides_near, sides_far)
     window_far = swap(edges_far, GX, True)
     window_near = swap(edges_near, GX, False)
 
@@ -601,17 +622,20 @@
         scratch_shapes=[pltpu.SemaphoreType.DMA((2,))],
         compiler_params=limit(2), cost_estimate=cost(0, 6 * 2**20), name="load",
     )(in_hbm(basis))
-    kept, local = pl.pallas_call(
+    kept, local, rows_near, rows_far = pl.pallas_call(
         window_kernel,
-        out_shape=(pltpu.HBM((6 * nx + 16, ny), F32), shaped(2, ny)),
-        in_specs=[SMEM_SPEC] + whole(11), out_specs=(hbm_space, *whole(1)),
+        out_shape=(
+            pltpu.HBM((6 * nx + 16, ny), F32), shaped(2, ny),
+            pltpu.HBM((2 * nz, ny), F32), pltpu.HBM((2 * nz, ny), F32),
+        ),
+        in_specs=[SMEM_SPEC] + whole(11), out_specs=(hbm_space, *whole(1), hbm_space, hbm_space),
         scratch_shapes=[
             VMEM((2, rows, ny), F32), VMEM((rows + 16, ny), F32), VMEM((ny, ny), F32),
-            VMEM((ny, ny), F32), pltpu.SemaphoreType.DMA((3,)),
+            VMEM((ny, ny), F32), pltpu.SemaphoreType.DMA((5,)),
         ],
         compiler_params=limit(4), cost_estimate=cost(10**7, 4 * 2**20), name="window",
     )(
-        diffusivity, near, velocity, diff_row, mine, sides_near, sides_far,
+        diffusivity, near, speeds, diff_row, mine, sides_near, sides_far,
         own_up, own_down, window_near, window_far, vectors,
     )
 
@@ -622,35 +646,35 @@
     )(local, other)
     parts = lax.all_to_all(sent, CHIPS, 0, 0, tiled=True)
 
-    halves = shaped(rows // 2, count + 2, 2 * ny, dtype=BF16)
+    halves = shaped(rows // 2, 2 * (count + 2), 2 * ny, dtype=BF16)
     padded = VMEM((nz * (nx + 16), ny), F32)
-    tracer_next, upper, lower, line = pl.pallas_call(
+    tracer_next, split_halves, line = pl.pallas_call(
         lambda *refs: bulk_kernel(8, *refs),
-        out_shape=(shaped(nz, nx, ny), halves, halves, shaped(8, ny)),
-        in_specs=[SMEM_SPEC] + [hbm_space] * 3 + [hbm_space] * 2 + whole(5),
-        out_specs=(any_space, *whole(3)),
+        out_shape=(shaped(nz, nx, ny), halves, shaped(8, ny)),
+        in_specs=[SMEM_SPEC] + [hbm_space] * 5 + whole(5),
+        out_specs=(any_space, *whole(2)),
         scratch_shapes=[
             padded, padded, VMEM((rows, count, ny), F32), VMEM((6 * nx + 16, ny), F32),
-            VMEM((2, nz, ny), F32), VMEM((2, nz, ny), F32), pltpu.SemaphoreType.DMA((9,)),
+            VMEM((2 * nz, ny), F32), VMEM((2 * nz, ny), F32), pltpu.SemaphoreType.DMA((9,)),
             pltpu.SemaphoreType.DMA((8,)), pltpu.SemaphoreType.DMA((3 + rows,)),
         ],
         compiler_params=limit(12), cost_estimate=cost(10**8, 10 * 2**20), name="bulk",
     )(
         diffusivity, in_hbm(tracer), in_hbm(basis.reshape(count, rows, 1, ny)), in_hbm(kept),
-        rows_near, rows_far, velocity, diff_row, singular.reshape(1, count), sides_near, sides_far,
+        in_hbm(rows_near), in_hbm(rows_far), velocity, diff_row, singular.reshape(1, count), sides_near, sides_far,
     )
 
     basis_next = pl.pallas_call(
         lambda *refs: core_kernel(rows_all, *refs),
-        out_shape=shaped(count + 2, rows, 1, ny),
-        in_specs=whole(4), out_specs=pl.BlockSpec(memory_space=pl.ANY),
+        out_shape=shaped(count + 2, rows, ny),
+        in_specs=whole(3), out_specs=pl.BlockSpec(memory_space=pl.ANY),
         scratch_shapes=[
-            VMEM((rows, count + 2, ny), F32),
-            pltpu.SemaphoreType.DMA((rows,)),
+            VMEM((count + 2, rows, ny), F32),
+            pltpu.SemaphoreType.DMA((rows // 8,)),
         ],
         compiler_params=limit(16), cost_estimate=cost(10**8, 6 * 2**20), name="core",
     )(
-        parts.reshape(chips // 4, 8, ny), line, upper, lower,
+        parts.reshape(chips // 4, 8, ny), line, split_halves,
     )
     return tracer_next, basis_next.reshape(count + 2, window, nx, ny)
 

time: 58.5 us -> 50.2 us (0.86)
  starting transfers between devices: 27 us -> 23.6 us
  waiting for transfers between devices: 9.88 us -> 6.91 us
  Pallas kernels: 20 us -> 18.8 us
  local copies, waits for them, and re-layouts: 0.65 us -> 0.02 us
    ppermute x6 -> x4, starting transfers between devices: 15.4 us -> 10.2 us  [swap(): return lax.ppermute(x, axes, pairs)]
    ppermute x6 -> x4, waiting for transfers between devices: 9.06 us -> 4.07 us  [swap(): return lax.ppermute(x, axes, pairs)]
    all_to_all x1, waiting for transfers between devices: 0.01 us -> 2.03 us  [steps(): parts = lax.all_to_all(sent, CHIPS, 0, 0, tiled=True)]
    all_to_all x1, starting transfers between devices: 9.67 us -> 10.9 us  [steps(): parts = lax.all_to_all(sent, CHIPS, 0, 0, tiled=True)]
    pallas_call x2, Pallas kernels: 2.93 us -> 2.13 us  [the longest x1 2.08 us: steps(): pl.pallas_call(lambda *refs: pack_columns_kernel(4, *refs), out_shape=(co...]
    unnamed x10 -> x6, local copies, waits for them, and re-layouts: 0.65 us -> 0.02 us
    ppermute x1, starting transfers between devices: 1.96 us -> 2.55 us  [steps(): other = lax.ppermute(local, 'c', [(0, 1), (1, 0)])]
  transfers between devices with their start and end apart: 8 -> 6, of which waited for: 4 -> 5; matrix products, arithmetic and copies ran while one was open for 0% -> 0% of each run, Pallas kernels for 19% -> 22%
where the time goes in v5:
time: 50.2 us; the launch traced here: 50 us
  starting transfers between devices  23.6 us (47%)
  Pallas kernels  18.8 us (37%)
  waiting for transfers between devices  6.91 us (14%)
  between operations  0.73 us (1%)
    all_to_all x1, starting transfers between devices, steps(): parts = lax.all_to_all(sent, CHIPS, 0, 0, tiled=True)  10.9 us
    ppermute x4, starting transfers between devices, swap(): return lax.ppermute(x, axes, pairs)  10.2 us
    pallas_call x1, Pallas kernels, steps(): pl.pallas_call(lambda *refs: bulk_kernel(8, *refs), out_shape=(shaped(nz,...  9.15 us
    ppermute x4, waiting for transfers between devices, swap(): return lax.ppermute(x, axes, pairs)  4.07 us
    pallas_call x1, Pallas kernels, steps(): pl.pallas_call(lambda *refs: core_kernel(rows_all, *refs), out_shape=shap...  2.96 us
    ppermute x1, starting transfers between devices, steps(): other = lax.ppermute(local, 'c', [(0, 1), (1, 0)])  2.55 us
    pallas_call x1, Pallas kernels, steps(): pl.pallas_call(lambda *refs: pack_columns_kernel(4, *refs), out_shape=(co...  2.08 us
    all_to_all x1, waiting for transfers between devices, steps(): parts = lax.all_to_all(sent, CHIPS, 0, 0, tiled=True)  2.03 us
  transfers between devices with their start and end apart: 6, of which 5 were waited for; matrix products, arithmetic and copies ran while one was open for 0% of the time, Pallas kernels for 22%

profile of v5, /device:TPU:1, one launch (start us, length us, event | category | flops | bytes accessed | tf_op | source)
XLA Modules:
  0.0 50.0 jit_solution(3056830134828387838)
XLA Ops:
  0.6 2.1 %columns.1 = (f32[3,32,128]{2,1,0:T(8,128)S(1)}, f32[3,32,128]{2,1,0:T(8,128)S(1)}, f32[192,128]{1,0:T(8,128)S(1)}, f32[256,128]{1,0:T(8,128)S(1)}, f32[256,128]...) custom-call(f32[4096,128]{1,0:T(8,128)} %bitcast.12, f32[128,32,1,128]{3,2,1,0:T(1,128)} %bitcast.13, ...), custom_call_target="tpu_custom_call" | custom-call | flops 1000000 | bytes 2097152 | tf_op jit(solution)/shard_map/columns/pallas_call | solution.py:594
  2.7 3.3 %collective-permute-start = (f32[3,32,128]{2,1,0:T(8,128)S(1)}, f32[3,32,128]{2,1,0:T(8,128)S(1)}, u32[]{:S(2)}, u32[]{:S(2)}) collective-permute-start(f32[3,32,128]{2,1,0:T(8,128)S(1)} %get-tuple-element.23), channel_id=1, source_target_pairs={{0,1},{1,0},{2,3},{3,2},{4,5},{5,4},{6,7},{7,6},{8,9},{9,8},{10,11... | collective-permute-start | bytes 147464 | tf_op jit(solution)/shard_map/ppermute | solution.py:579
  6.0 0.0 collective-permute-start.1
  6.0 0.9 %collective-permute-done.sides_near.refs_9_ = f32[3,32,128]{2,1,0:T(8,128)S(1)} collective-permute-done((f32[3,32,128]{2,1,0:T(8,128)S(1)}, f32[3,32,128]{2,1,0:T(8,128)S(1)}, u32[]{:S(2)}, u32[]{:S(2)}) %collective-permute-start) | collective-permute-done | bytes 49184 | tf_op jit(solution)/shard_map/ppermute | solution.py:579
  6.9 2.6 %collective-permute-done.1.sides_far.refs_10_ = f32[3,32,128]{2,1,0:T(8,128)S(1)} collective-permute-done((f32[3,32,128]{2,1,0:T(8,128)S(1)}, f32[3,32,128]{2,1,0:T(8,128)S(1)}, u32[]{:S(2)}, u32[]{:S(2)}) %collective-permute-start.1) | collective-permute-done | bytes 49184 | tf_op jit(solution)/shard_map/ppermute | solution.py:579
  9.6 0.1 collective-permute-start.2
  9.7 6.8 %collective-permute-start.3 = (f32[280,128]{1,0:T(8,128)S(1)}, f32[280,128]{1,0:T(8,128)S(1)}, u32[]{:S(2)}, u32[]{:S(2)}) collective-permute-start(f32[280,128]{1,0:T(8,128)S(1)} %get-tuple-element.30), channel_id=1, source_target_pairs={{8,16},{16,8},{24,32},{32,24},{40,48},{48,40},{56,64},{64,56},{72,... | collective-permute-start | bytes 430088 | tf_op jit(solution)/shard_map/ppermute | solution.py:579
  16.4 0.0 copy-start.1
  16.4 1.9 %load.1.basis = f32[94,64,128]{2,1,0:T(8,128)S(1)} custom-call(f32[94,64,128]{2,1,0:T(8,128)} %bitcast.14), custom_call_target="tpu_custom_call" | custom-call | bytes 6291456 | tf_op jit(solution)/shard_map/load/pallas_call | solution.py:619
  18.3 0.0 copy-start
  18.4 0.0 copy-start.2
  18.4 0.0 collective-permute-done.2.rows_near
  18.4 0.6 %collective-permute-done.3.rows_far = f32[280,128]{1,0:T(8,128)S(1)} collective-permute-done((f32[280,128]{1,0:T(8,128)S(1)}, f32[280,128]{1,0:T(8,128)S(1)}, u32[]{:S(2)}, u32[]{:S(2)}) %collective-permute-start.3) | collective-permute-done | bytes 143392 | tf_op jit(solution)/shard_map/ppermute | solution.py:579
  18.9 0.0 copy-done.1
  18.9 2.0 %window.1 = (f32[208,128]{1,0:T(8,128)}, f32[2,128]{1,0:T(2,128)S(1)}, f32[256,128]{1,0:T(8,128)}, f32[256,128]{1,0:T(8,128)}) custom-call(f32[128]{0:T(128)S(1)} %copy-done.1, f32[192,128]{1,0:T(8,128)S(1)} %get-tuple-element.20.window.near, f32[2,32,128]{2,1,0:T(8,128)S(1)} %get-tuple-element.21.velocity, f32[1,128]{1,0:T(1,128)S(1)} %bitcast.9, ...), custom_call_target="tpu_custom_call" | custom-call | flops 10000000 | bytes 4194304 | tf_op jit(solution)/shard_map/window/pallas_call | solution.py:625
  20.9 2.5 %collective-permute-start.4 = (f32[2,128]{1,0:T(2,128)S(1)}, f32[2,128]{1,0:T(2,128)S(1)}, u32[]{:S(2)}, u32[]{:S(2)}) collective-permute-start(f32[2,128]{1,0:T(2,128)S(1)} %get-tuple-element.35.mine), channel_id=1, source_target_pairs={{0,1},{1,0},{2,3},{3,2},{4,5},{5,4},{6,7},{7,6},{8,9},{9,8},{10,11... | collective-permute-start | bytes 3080 | tf_op jit(solution)/shard_map/ppermute | solution.py:642
  23.5 0.8 %collective-permute-done.4.other = f32[2,128]{1,0:T(2,128)S(1)} collective-permute-done((f32[2,128]{1,0:T(2,128)S(1)}, f32[2,128]{1,0:T(2,128)S(1)}, u32[]{:S(2)}, u32[]{:S(2)}) %collective-permute-start.4) | collective-permute-done | bytes 1056 | tf_op jit(solution)/shard_map/ppermute | solution.py:642
  24.3 0.7 %spread.1 = f32[128,2,128]{2,1,0:T(2,128)} custom-call(f32[2,128]{1,0:T(2,128)S(1)} %get-tuple-element.35.mine, f32[2,128]{1,0:T(2,128)S(1)} %collective-permute-done.4.other), custom_call_target="tpu_custom_call" | custom-call | flops 10000 | bytes 131072 | tf_op jit(solution)/shard_map/spread/pallas_call | solution.py:643
  25.0 10.9 %all-to-all-start = ((f32[128,2,128]{2,1,0:T(2,128)}), f32[128,2,128]{2,1,0:T(2,128)S(1)}, u32[]{:S(2)}, u32[]{:S(2)}) async-start(f32[128,2,128]{2,1,0:T(2,128)} %spread.1), calls=%async_computation | async-start | bytes 262144 | tf_op jit(solution)/shard_map/all_to_all | solution.py:647
  35.9 0.0 copy-done
  35.9 0.0 copy-done.2
  35.9 9.1 %bulk.1 = (f32[128,32,128]{2,1,0:T(8,128)}, bf16[32,192,256]{2,1,0:T(8,128)(2,1)S(1)}, f32[8,128]{1,0:T(8,128)S(1)}) custom-call(f32[128]{0:T(128)S(1)} %copy-done.1, f32[128,32,128]{2,1,0:T(8,128)} %refs_1_.1, f32[94,64,1,128]{3,2,1,0:T(1,128)} %bitcast.15, f32[208,128]{1,0:T(8,128)} %get-tuple-element.31.refs_3_, f32[256,128]{1,0:T(8,128)} %get-tuple-element.32.refs_4_, ...), custom_call_target="tpu_custom_call" | custom-call | flops 100000000 | bytes 10485760 | tf_op jit(solution)/shard_map/bulk/pallas_call | solution.py:651
  45.0 2.0 %all-to-all-done = f32[128,2,128]{2,1,0:T(2,128)S(1)} async-done(((f32[128,2,128]{2,1,0:T(2,128)}), f32[128,2,128]{2,1,0:T(2,128)S(1)}, u32[]{:S(2)}, u32[]{:S(2)}) %all-to-all-start) | async-done | bytes 131104 | tf_op jit(solution)/shard_map/all_to_all | solution.py:647
  47.1 3.0 %core.1 = f32[96,64,128]{2,1,0:T(8,128)} custom-call(f32[32,8,128]{2,1,0:T(8,128)S(1)} %bitcast.8, f32[8,128]{1,0:T(8,128)S(1)} %get-tuple-element.36.refs_1_, bf16[32,192,256]{2,1,0:T(8,128)(2,1)S(1)} %get-tuple-element.37.refs_2_), custom_call_target="tpu_custom_call" | custom-call | flops 100000000 | bytes 6291456 | tf_op jit(solution)/shard_map/core/pallas_call | solution.py:667
  (1 shorter events, 0.0 us)
Async XLA Ops:
  2.7 4.2 %collective-permute-start = (f32[3,32,128]{2,1,0:T(8,128)S(1)}, f32[3,32,128]{2,1,0:T(8,128)S(1)}, u32[]{:S(2)}, u32[]{:S(2)}) collective-permute-start(f32[3,32,128]{2,1,0:T(8,128)S(1)} %get-tuple-element.23), channel_id=1, source_target_pairs={{0,1},{1,0},{2,3},{3,2},{4,5},{5,4},{6,7},{7,6},{8,9},{9,8},{10,11... | collective-permute-start | bytes 147464 | tf_op jit(solution)/shard_map/ppermute | solution.py:579
  6.0 3.5 %collective-permute-start.1 = (f32[3,32,128]{2,1,0:T(8,128)S(1)}, f32[3,32,128]{2,1,0:T(8,128)S(1)}, u32[]{:S(2)}, u32[]{:S(2)}) collective-permute-start(f32[3,32,128]{2,1,0:T(8,128)S(1)} %get-tuple-element.24), channel_id=1, source_target_pairs={{1,2},{2,1},{3,4},{4,3},{5,6},{6,5},{7,0},{0,7},{9,10},{10,9},{11,... | collective-permute-start | bytes 147464 | tf_op jit(solution)/shard_map/ppermute | solution.py:579
  9.6 8.8 %collective-permute-start.2 = (f32[280,128]{1,0:T(8,128)S(1)}, f32[280,128]{1,0:T(8,128)S(1)}, u32[]{:S(2)}, u32[]{:S(2)}) collective-permute-start(f32[280,128]{1,0:T(8,128)S(1)} %get-tuple-element.29), channel_id=1, source_target_pairs={{0,8},{8,0},{16,24},{24,16},{32,40},{40,32},{48,56},{56,48},{64,72... | collective-permute-start | bytes 430088 | tf_op jit(solution)/shard_map/ppermute | solution.py:579
  9.7 9.3 %collective-permute-start.3 = (f32[280,128]{1,0:T(8,128)S(1)}, f32[280,128]{1,0:T(8,128)S(1)}, u32[]{:S(2)}, u32[]{:S(2)}) collective-permute-start(f32[280,128]{1,0:T(8,128)S(1)} %get-tuple-element.30), channel_id=1, source_target_pairs={{8,16},{16,8},{24,32},{32,24},{40,48},{48,40},{56,64},{64,56},{72,... | collective-permute-start | bytes 430088 | tf_op jit(solution)/shard_map/ppermute | solution.py:579
  16.4 2.5 %copy-start.1 = (f32[128]{0:T(128)S(1)}, f32[128]{0:T(128)}, u32[]{:S(2)}) copy-start(f32[128]{0:T(128)} %refs_0_.1) | copy-start | bytes 1540
  18.3 17.5 %copy-start = (f32[2,32,128]{2,1,0:T(8,128)S(1)}, f32[2,32,128]{2,1,0:T(8,128)}, u32[]{:S(2)}) copy-start(f32[2,32,128]{2,1,0:T(8,128)} %refs_6_.1) | copy-start | bytes 98308
  18.4 17.5 %copy-start.2 = (f32[94]{0:T(128)S(1)}, f32[94]{0:T(128)}, u32[]{:S(2)}) copy-start(f32[94]{0:T(128)} %param.8) | copy-start | bytes 1132
  20.9 3.4 %collective-permute-start.4 = (f32[2,128]{1,0:T(2,128)S(1)}, f32[2,128]{1,0:T(2,128)S(1)}, u32[]{:S(2)}, u32[]{:S(2)}) collective-permute-start(f32[2,128]{1,0:T(2,128)S(1)} %get-tuple-element.35.mine), channel_id=1, source_target_pairs={{0,1},{1,0},{2,3},{3,2},{4,5},{5,4},{6,7},{7,6},{8,9},{9,8},{10,11... | collective-permute-start | bytes 3080 | tf_op jit(solution)/shard_map/ppermute | solution.py:642
  25.0 22.1 %all-to-all-start = ((f32[128,2,128]{2,1,0:T(2,128)}), f32[128,2,128]{2,1,0:T(2,128)S(1)}, u32[]{:S(2)}, u32[]{:S(2)}) async-start(f32[128,2,128]{2,1,0:T(2,128)} %spread.1), calls=%async_computation | async-start | bytes 262144 | tf_op jit(solution)/shard_map/all_to_all | solution.py:647

commit v6 on v5

--- a/solution.py
+++ b/solution.py
@@ -66,7 +66,7 @@
 
 
 def pack_columns_kernel(
-    chunks, tracer_hbm, by_row_hbm, velocity_hbm, near, far, window, tops, bottoms, mine, velocity,
+    chunks, tracer_hbm, by_row_hbm, velocity_hbm, near, far, window, rows_near, rows_far, mine, velocity,
     tracer, sems,
 ):
     nx, ny = velocity.shape[1:]
@@ -83,10 +83,12 @@
     moves.append((velocity_hbm, velocity))
     moves.append(rows_of_level(nz - 2, 2, window.at[0 : 2 * nx]))
     moves.append(rows_of_level(0, 4, window.at[2 * nx : 6 * nx]))
+    even = gx_is_even()
     for i in range(2):
-        part = pl.ds(i * nz, nz)
-        moves.append((by_row_hbm.at[:, i, 0, :], tops.at[part]))
-        moves.append((by_row_hbm.at[:, nx - 1 - i, 0, :], bottoms.at[part]))
+        part, first, last = pl.ds(i * nz, nz), i, nx - 1 - i
+        at_near, at_far = jnp.where(even, last, first), jnp.where(even, first, last)
+        moves.append((by_row_hbm.at[:, at_near, 0, :], rows_near.at[part]))
+        moves.append((by_row_hbm.at[:, at_far, 0, :], rows_far.at[part]))
     loads = [pltpu.make_async_copy(src, dst, sems.at[i]) for i, (src, dst) in enumerate(moves)]
     for load in loads:
         load.start()
@@ -128,9 +130,7 @@
         load.wait()
 
 
-def pack_rows_kernel(
-    window, velocity, tops, bottoms, sides_near, sides_far, near, far, up, down
-):
+def pack_rows_kernel(window, velocity, sides_near, sides_far, near, far, up, down):
     nx, ny = velocity.shape[1:]
     from_left, from_right = from_pairs(gy_is_even(), sides_near[0], sides_far[0])
     for edge, inner, out in ((0, 1, up), (nx - 1, nx - 2, down)):
@@ -143,15 +143,13 @@
         out[17:18, :] = velocity[1, edge : edge + 1, :]
         out[18:19, :] = from_left[edge : edge + 1, :]
         out[19:20, :] = from_right[edge : edge + 1, :]
-    even = gx_is_even()
-    near[0:24], far[0:24] = to_pairs(even, up[...], down[...])
-    near[24:], far[24:] = to_pairs(even, tops[...], bottoms[...])
+    near[...], far[...] = to_pairs(gx_is_even(), up[...], down[...])
 
 
 def window_kernel(
     diff, near, velocity, diff_row, mine, sides_near, sides_far,
     own_up, own_down, rows_near, rows_far, basis,
-    kept_hbm, sums, near_hbm, far_hbm, snaps, sides, q0, q1, sems,
+    kept_hbm, sums, snaps, sides, q0, q1, sems,
 ):
     nz, nx, ny = diff.shape[0], velocity.shape[1], velocity.shape[2]
     count = basis.shape[0]
@@ -159,7 +157,7 @@
     even = gy_is_even()
     pairs = [from_pairs(even, sides_near[i], sides_far[i]) for i in range(3)]
     from_left, from_right = [p[0] for p in pairs], [p[1] for p in pairs]
-    from_up, from_down = from_pairs(gx_is_even(), rows_near[0:24], rows_far[0:24])
+    from_up, from_down = from_pairs(gx_is_even(), rows_near[...], rows_far[...])
     for gin, inner, outer, corner, vx_at, vy_at, out in (
         (from_left, None, mine[0], 18, ny - 1, ny - 2, sides.at[0:nx]),
         (from_right, mine[1], None, 19, 0, 1, sides.at[nx : 2 * nx]),
@@ -222,9 +220,6 @@
             ((snaps.at[0], 0), (snaps.at[1], rows), (sides, 2 * rows))
         )
     ]
-    bulk = pl.ds(24, 2 * nz)
-    keep.append(pltpu.make_async_copy(rows_near.at[bulk], near_hbm, sems.at[3]))
-    keep.append(pltpu.make_async_copy(rows_far.at[bulk], far_hbm, sems.at[4]))
     for copy in keep:
         copy.start()
 
@@ -591,7 +586,7 @@
     columns = shaped(3, nx, ny)
     bulk_rows = shaped(2 * nz, ny)
     hbm_space, any_space = (pl.BlockSpec(memory_space=m) for m in (pltpu.HBM, pl.ANY))
-    columns_near, columns_far, near, tops, bottoms, mine, speeds = pl.pallas_call(
+    columns_near, columns_far, near, sent_near, sent_far, mine, speeds = pl.pallas_call(
         lambda *refs: pack_columns_kernel(4, *refs),
         out_shape=(
             columns, columns, shaped(6 * nx, ny), bulk_rows, bulk_rows, shaped(2, nx, ny),
@@ -607,14 +602,16 @@
     )
     sides_far = swap(columns_far, GY, True)
     sides_near = swap(columns_near, GY, False)
-    edge, message = shaped(24, ny), shaped(24 + 2 * nz, ny)
+    edge = shaped(24, ny)
     edges_near, edges_far, own_up, own_down = pl.pallas_call(
-        pack_rows_kernel, out_shape=(message, message, edge, edge),
-        in_specs=whole(6), out_specs=tuple(whole(4)),
+        pack_rows_kernel, out_shape=(edge,) * 4, in_specs=whole(4), out_specs=tuple(whole(4)),
         compiler_params=limit(2), cost_estimate=cost(10**4, 2**17), name="edges",
-    )(near, speeds, tops, bottoms, sides_near, sides_far)
+    )(near, speeds, sides_near, sides_far)
     window_far = swap(edges_far, GX, True)
     window_near = swap(edges_near, GX, False)
+
+    rows_far = in_hbm(swap(in_hbm(sent_far), GX, True))
+    rows_near = in_hbm(swap(in_hbm(sent_near), GX, False))
 
     vectors = pl.pallas_call(
         load_kernel, out_shape=shaped(count, rows, ny),
@@ -622,16 +619,13 @@
         scratch_shapes=[pltpu.SemaphoreType.DMA((2,))],
         compiler_params=limit(2), cost_estimate=cost(0, 6 * 2**20), name="load",
     )(in_hbm(basis))
-    kept, local, rows_near, rows_far = pl.pallas_call(
+    kept, local = pl.pallas_call(
         window_kernel,
-        out_shape=(
-            pltpu.HBM((6 * nx + 16, ny), F32), shaped(2, ny),
-            pltpu.HBM((2 * nz, ny), F32), pltpu.HBM((2 * nz, ny), F32),
-        ),
-        in_specs=[SMEM_SPEC] + whole(11), out_specs=(hbm_space, *whole(1), hbm_space, hbm_space),
+        out_shape=(pltpu.HBM((6 * nx + 16, ny), F32), shaped(2, ny)),
+        in_specs=[SMEM_SPEC] + whole(11), out_specs=(hbm_space, *whole(1)),
         scratch_shapes=[
             VMEM((2, rows, ny), F32), VMEM((rows + 16, ny), F32), VMEM((ny, ny), F32),
-            VMEM((ny, ny), F32), pltpu.SemaphoreType.DMA((5,)),
+            VMEM((ny, ny), F32), pltpu.SemaphoreType.DMA((3,)),
         ],
         compiler_params=limit(4), cost_estimate=cost(10**7, 4 * 2**20), name="window",
     )(

time: 50.2 us -> 57.3 us (1.14)
  starting transfers between devices: 23.6 us -> 27 us
  waiting for transfers between devices: 6.91 us -> 9.88 us
  local copies, waits for them, and re-layouts: 0.02 us -> 0.66 us
    ppermute x4 -> x6, starting transfers between devices: 10.2 us -> 15.4 us  [swap(): return lax.ppermute(x, axes, pairs)]
    ppermute x4 -> x6, waiting for transfers between devices: 4.07 us -> 9.06 us  [swap(): return lax.ppermute(x, axes, pairs)]
    all_to_all x1, waiting for transfers between devices: 2.03 us -> 0.01 us  [steps(): parts = lax.all_to_all(sent, CHIPS, 0, 0, tiled=True)]
    all_to_all x1, starting transfers between devices: 10.9 us -> 9.66 us  [steps(): parts = lax.all_to_all(sent, CHIPS, 0, 0, tiled=True)]
    unnamed x6 -> x10, local copies, waits for them, and re-layouts: 0.02 us -> 0.66 us
    ppermute x1, starting transfers between devices: 2.55 us -> 1.96 us  [steps(): other = lax.ppermute(local, 'c', [(0, 1), (1, 0)])]
  transfers between devices with their start and end apart: 6 -> 8, of which waited for: 5 -> 4; matrix products, arithmetic and copies ran while one was open for 0% -> 0% of each run, Pallas kernels for 22% -> 19%
where the time goes in v6:
time: 57.3 us; the launch traced here: 57.1 us
  starting transfers between devices  27 us (47%)
  Pallas kernels  18.8 us (33%)
  waiting for transfers between devices  9.88 us (17%)
  between operations  0.74 us (1%)
  local copies, waits for them, and re-layouts  0.66 us (1%)
    ppermute x6, starting transfers between devices, swap(): return lax.ppermute(x, axes, pairs)  15.4 us
    all_to_all x1, starting transfers between devices, steps(): parts = lax.all_to_all(sent, CHIPS, 0, 0, tiled=True)  9.66 us
    pallas_call x1, Pallas kernels, steps(): pl.pallas_call(lambda *refs: bulk_kernel(8, *refs), out_shape=(shaped(nz,...  9.14 us
    ppermute x6, waiting for transfers between devices, swap(): return lax.ppermute(x, axes, pairs)  9.06 us
    pallas_call x1, Pallas kernels, steps(): pl.pallas_call(lambda *refs: core_kernel(rows_all, *refs), out_shape=shap...  2.97 us
    pallas_call x1, Pallas kernels, steps(): pl.pallas_call(lambda *refs: pack_columns_kernel(4, *refs), out_shape=(co...  2.08 us
    pallas_call x1, Pallas kernels, steps(): pl.pallas_call(window_kernel, out_shape=(pltpu.HBM((6 * nx + 16, ny), F32...  1.97 us
    ppermute x1, starting transfers between devices, steps(): other = lax.ppermute(local, 'c', [(0, 1), (1, 0)])  1.96 us
  transfers between devices with their start and end apart: 8, of which 4 were waited for; matrix products, arithmetic and copies ran while one was open for 0% of the time, Pallas kernels for 19%

profile of v6, /device:TPU:1, one launch (start us, length us, event | category | flops | bytes accessed | tf_op | source)
XLA Modules:
  0.0 57.1 jit_solution(7928523524256712229)
XLA Ops:
  0.6 2.1 %columns.1 = (f32[3,32,128]{2,1,0:T(8,128)S(1)}, f32[3,32,128]{2,1,0:T(8,128)S(1)}, f32[192,128]{1,0:T(8,128)S(1)}, f32[256,128]{1,0:T(8,128)S(1)}, f32[256,128]...) custom-call(f32[4096,128]{1,0:T(8,128)} %bitcast.12, f32[128,32,1,128]{3,2,1,0:T(1,128)} %bitcast.13, ...), custom_call_target="tpu_custom_call" | custom-call | flops 1000000 | bytes 2097152 | tf_op jit(solution)/shard_map/columns/pallas_call | solution.py:589
  2.7 3.3 %collective-permute-start = (f32[3,32,128]{2,1,0:T(8,128)S(1)}, f32[3,32,128]{2,1,0:T(8,128)S(1)}, u32[]{:S(2)}, u32[]{:S(2)}) collective-permute-start(f32[3,32,128]{2,1,0:T(8,128)S(1)} %get-tuple-element.21), channel_id=1, source_target_pairs={{0,1},{1,0},{2,3},{3,2},{4,5},{5,4},{6,7},{7,6},{8,9},{9,8},{10,11... | collective-permute-start | bytes 147464 | tf_op jit(solution)/shard_map/ppermute | solution.py:574
  6.0 0.0 collective-permute-start.1
  6.0 0.9 %collective-permute-done.sides_near.refs_9_ = f32[3,32,128]{2,1,0:T(8,128)S(1)} collective-permute-done((f32[3,32,128]{2,1,0:T(8,128)S(1)}, f32[3,32,128]{2,1,0:T(8,128)S(1)}, u32[]{:S(2)}, u32[]{:S(2)}) %collective-permute-start) | collective-permute-done | bytes 49184 | tf_op jit(solution)/shard_map/ppermute | solution.py:574
  6.9 2.6 %collective-permute-done.1.sides_far.refs_10_ = f32[3,32,128]{2,1,0:T(8,128)S(1)} collective-permute-done((f32[3,32,128]{2,1,0:T(8,128)S(1)}, f32[3,32,128]{2,1,0:T(8,128)S(1)}, u32[]{:S(2)}, u32[]{:S(2)}) %collective-permute-start.1) | collective-permute-done | bytes 49184 | tf_op jit(solution)/shard_map/ppermute | solution.py:574
  9.6 0.1 collective-permute-start.2
  9.7 6.8 %collective-permute-start.3 = (f32[24,128]{1,0:T(8,128)S(1)}, f32[24,128]{1,0:T(8,128)S(1)}, u32[]{:S(2)}, u32[]{:S(2)}) collective-permute-start(f32[24,128]{1,0:T(8,128)S(1)} %get-tuple-element.26), channel_id=1, source_target_pairs={{8,16},{16,8},{24,32},{32,24},{40,48},{48,40},{56,64},{64,56},{72,... | collective-permute-start | bytes 36872 | tf_op jit(solution)/shard_map/ppermute | solution.py:574
  16.4 0.0 copy-start.1
  16.4 1.9 %load.1.basis = f32[94,64,128]{2,1,0:T(8,128)S(1)} custom-call(f32[94,64,128]{2,1,0:T(8,128)} %bitcast.14), custom_call_target="tpu_custom_call" | custom-call | bytes 6291456 | tf_op jit(solution)/shard_map/load/pallas_call | solution.py:616
  18.3 0.0 copy-start
  18.3 0.0 copy-start.2
  18.3 0.0 collective-permute-done.2.rows_near
  18.4 0.0 collective-permute-done.3.rows_far
  18.4 0.0 copy-done.1
  18.4 2.0 %window.1 = (f32[208,128]{1,0:T(8,128)}, f32[2,128]{1,0:T(2,128)S(1)}) custom-call(f32[128]{0:T(128)S(1)} %copy-done.1, f32[192,128]{1,0:T(8,128)S(1)} %get-tuple-element.18.window.near, f32[2,32,128]{2,1,0:T(8,128)S(1)} %get-tuple-element.19.velocity, f32[1,128]{1,0:T(1,128)S(1)} %bitcast.9, f32[2,32,128]{2,1,0:T(8,128)S(1)} %get-tuple-element.20.mine, ...), custom_call_target="tpu_custom_call" | custom-call | flops 10000000 | bytes 4194304 | tf_op jit(solution)/shard_map/window/pallas_call | solution.py:622
  20.4 2.0 %collective-permute-start.6 = (f32[2,128]{1,0:T(2,128)S(1)}, f32[2,128]{1,0:T(2,128)S(1)}, u32[]{:S(2)}, u32[]{:S(2)}) collective-permute-start(f32[2,128]{1,0:T(2,128)S(1)} %get-tuple-element.31.mine), channel_id=1, source_target_pairs={{0,1},{1,0},{2,3},{3,2},{4,5},{5,4},{6,7},{7,6},{8,9},{9,8},{10,11... | collective-permute-start | bytes 3080 | tf_op jit(solution)/shard_map/ppermute | solution.py:636
  22.3 0.8 %collective-permute-done.6.other = f32[2,128]{1,0:T(2,128)S(1)} collective-permute-done((f32[2,128]{1,0:T(2,128)S(1)}, f32[2,128]{1,0:T(2,128)S(1)}, u32[]{:S(2)}, u32[]{:S(2)}) %collective-permute-start.6) | collective-permute-done | bytes 1056 | tf_op jit(solution)/shard_map/ppermute | solution.py:636
  23.1 0.7 %spread.1 = f32[128,2,128]{2,1,0:T(2,128)} custom-call(f32[2,128]{1,0:T(2,128)S(1)} %get-tuple-element.31.mine, f32[2,128]{1,0:T(2,128)S(1)} %collective-permute-done.6.other), custom_call_target="tpu_custom_call" | custom-call | flops 10000 | bytes 131072 | tf_op jit(solution)/shard_map/spread/pallas_call | solution.py:637
  23.8 9.7 %all-to-all-start = ((f32[128,2,128]{2,1,0:T(2,128)}), f32[128,2,128]{2,1,0:T(2,128)S(1)}, u32[]{:S(2)}, u32[]{:S(2)}) async-start(f32[128,2,128]{2,1,0:T(2,128)} %spread.1), calls=%async_computation | async-start | bytes 262144 | tf_op jit(solution)/shard_map/all_to_all | solution.py:641
  33.5 0.7 %collective-permute-start.4 = (f32[256,128]{1,0:T(8,128)S(1)}, f32[256,128]{1,0:T(8,128)S(1)}, u32[]{:S(2)}, u32[]{:S(2)}) collective-permute-start(f32[256,128]{1,0:T(8,128)S(1)} %get-tuple-element.28), channel_id=1, source_target_pairs={{0,8},{8,0},{16,24},{24,16},{32,40},{40,32},{48,56},{56,48},{64,72... | collective-permute-start | bytes 393224 | tf_op jit(solution)/shard_map/ppermute | solution.py:574
  34.2 4.6 %collective-permute-start.5 = (f32[256,128]{1,0:T(8,128)S(1)}, f32[256,128]{1,0:T(8,128)S(1)}, u32[]{:S(2)}, u32[]{:S(2)}) collective-permute-start(f32[256,128]{1,0:T(8,128)S(1)} %get-tuple-element.29), channel_id=1, source_target_pairs={{8,16},{16,8},{24,32},{32,24},{40,48},{48,40},{56,64},{64,56},{72,... | collective-permute-start | bytes 393224 | tf_op jit(solution)/shard_map/ppermute | solution.py:574
  38.8 0.0 collective-permute-done.4.refs_4_
  38.8 0.0 copy-start.3
  38.8 5.5 %collective-permute-done.5.refs_5_ = f32[256,128]{1,0:T(8,128)S(1)} collective-permute-done((f32[256,128]{1,0:T(8,128)S(1)}, f32[256,128]{1,0:T(8,128)S(1)}, u32[]{:S(2)}, u32[]{:S(2)}) %collective-permute-start.5) | collective-permute-done | bytes 131104 | tf_op jit(solution)/shard_map/ppermute | solution.py:574
  44.3 0.0 copy-start.4
  44.3 0.0 copy-done.3
  44.3 0.6 %copy-done.4 = f32[256,128]{1,0:T(8,128)} copy-done((f32[256,128]{1,0:T(8,128)}, f32[256,128]{1,0:T(8,128)S(1)}, u32[]{:S(2)}) %copy-start.4) | copy-done | bytes 131096
  44.9 0.0 copy-done
  44.9 0.0 copy-done.2
  44.9 9.1 %bulk.1 = (f32[128,32,128]{2,1,0:T(8,128)}, bf16[32,192,256]{2,1,0:T(8,128)(2,1)S(1)}, f32[8,128]{1,0:T(8,128)S(1)}) custom-call(f32[128]{0:T(128)S(1)} %copy-done.1, f32[128,32,128]{2,1,0:T(8,128)} %refs_1_.1, f32[94,64,1,128]{3,2,1,0:T(1,128)} %bitcast.15, f32[208,128]{1,0:T(8,128)} %get-tuple-element.27.refs_3_, f32[256,128]{1,0:T(8,128)} %copy-done.3, ...), custom_call_target="tpu_custom_call" | custom-call | flops 100000000 | bytes 10485760 | tf_op jit(solution)/shard_map/bulk/pallas_call | solution.py:645
  54.1 0.0 all-to-all-done
  54.1 3.0 %core.1 = f32[96,64,128]{2,1,0:T(8,128)} custom-call(f32[32,8,128]{2,1,0:T(8,128)S(1)} %bitcast.8, f32[8,128]{1,0:T(8,128)S(1)} %get-tuple-element.32.refs_1_, bf16[32,192,256]{2,1,0:T(8,128)(2,1)S(1)} %get-tuple-element.33.refs_2_), custom_call_target="tpu_custom_call" | custom-call | flops 100000000 | bytes 6291456 | tf_op jit(solution)/shard_map/core/pallas_call | solution.py:661
  (1 shorter events, 0.0 us)
Async XLA Ops:
  2.7 4.2 %collective-permute-start = (f32[3,32,128]{2,1,0:T(8,128)S(1)}, f32[3,32,128]{2,1,0:T(8,128)S(1)}, u32[]{:S(2)}, u32[]{:S(2)}) collective-permute-start(f32[3,32,128]{2,1,0:T(8,128)S(1)} %get-tuple-element.21), channel_id=1, source_target_pairs={{0,1},{1,0},{2,3},{3,2},{4,5},{5,4},{6,7},{7,6},{8,9},{9,8},{10,11... | collective-permute-start | bytes 147464 | tf_op jit(solution)/shard_map/ppermute | solution.py:574
  6.0 3.5 %collective-permute-start.1 = (f32[3,32,128]{2,1,0:T(8,128)S(1)}, f32[3,32,128]{2,1,0:T(8,128)S(1)}, u32[]{:S(2)}, u32[]{:S(2)}) collective-permute-start(f32[3,32,128]{2,1,0:T(8,128)S(1)} %get-tuple-element.22), channel_id=1, source_target_pairs={{1,2},{2,1},{3,4},{4,3},{5,6},{6,5},{7,0},{0,7},{9,10},{10,9},{11,... | collective-permute-start | bytes 147464 | tf_op jit(solution)/shard_map/ppermute | solution.py:574
  9.6 8.8 %collective-permute-start.2 = (f32[24,128]{1,0:T(8,128)S(1)}, f32[24,128]{1,0:T(8,128)S(1)}, u32[]{:S(2)}, u32[]{:S(2)}) collective-permute-start(f32[24,128]{1,0:T(8,128)S(1)} %get-tuple-element.25), channel_id=1, source_target_pairs={{0,8},{8,0},{16,24},{24,16},{32,40},{40,32},{48,56},{56,48},{64,72... | collective-permute-start | bytes 36872 | tf_op jit(solution)/shard_map/ppermute | solution.py:574
  9.7 8.7 %collective-permute-start.3 = (f32[24,128]{1,0:T(8,128)S(1)}, f32[24,128]{1,0:T(8,128)S(1)}, u32[]{:S(2)}, u32[]{:S(2)}) collective-permute-start(f32[24,128]{1,0:T(8,128)S(1)} %get-tuple-element.26), channel_id=1, source_target_pairs={{8,16},{16,8},{24,32},{32,24},{40,48},{48,40},{56,64},{64,56},{72,... | collective-permute-start | bytes 36872 | tf_op jit(solution)/shard_map/ppermute | solution.py:574
  16.4 1.9 %copy-start.1 = (f32[128]{0:T(128)S(1)}, f32[128]{0:T(128)}, u32[]{:S(2)}) copy-start(f32[128]{0:T(128)} %refs_0_.1) | copy-start | bytes 1540
  18.3 26.6 %copy-start = (f32[2,32,128]{2,1,0:T(8,128)S(1)}, f32[2,32,128]{2,1,0:T(8,128)}, u32[]{:S(2)}) copy-start(f32[2,32,128]{2,1,0:T(8,128)} %refs_6_.1) | copy-start | bytes 98308
  18.3 26.6 %copy-start.2 = (f32[94]{0:T(128)S(1)}, f32[94]{0:T(128)}, u32[]{:S(2)}) copy-start(f32[94]{0:T(128)} %param.8) | copy-start | bytes 1132
  20.4 2.8 %collective-permute-start.6 = (f32[2,128]{1,0:T(2,128)S(1)}, f32[2,128]{1,0:T(2,128)S(1)}, u32[]{:S(2)}, u32[]{:S(2)}) collective-permute-start(f32[2,128]{1,0:T(2,128)S(1)} %get-tuple-element.31.mine), channel_id=1, source_target_pairs={{0,1},{1,0},{2,3},{3,2},{4,5},{5,4},{6,7},{7,6},{8,9},{9,8},{10,11... | collective-permute-start | bytes 3080 | tf_op jit(solution)/shard_map/ppermute | solution.py:636
  23.8 30.3 %all-to-all-start = ((f32[128,2,128]{2,1,0:T(2,128)}), f32[128,2,128]{2,1,0:T(2,128)S(1)}, u32[]{:S(2)}, u32[]{:S(2)}) async-start(f32[128,2,128]{2,1,0:T(2,128)} %spread.1), calls=%async_computation | async-start | bytes 262144 | tf_op jit(solution)/shard_map/all_to_all | solution.py:641
  33.5 5.3 %collective-permute-start.4 = (f32[256,128]{1,0:T(8,128)S(1)}, f32[256,128]{1,0:T(8,128)S(1)}, u32[]{:S(2)}, u32[]{:S(2)}) collective-permute-start(f32[256,128]{1,0:T(8,128)S(1)} %get-tuple-element.28), channel_id=1, source_target_pairs={{0,8},{8,0},{16,24},{24,16},{32,40},{40,32},{48,56},{56,48},{64,72... | collective-permute-start | bytes 393224 | tf_op jit(solution)/shard_map/ppermute | solution.py:574
  34.2 10.1 %collective-permute-start.5 = (f32[256,128]{1,0:T(8,128)S(1)}, f32[256,128]{1,0:T(8,128)S(1)}, u32[]{:S(2)}, u32[]{:S(2)}) collective-permute-start(f32[256,128]{1,0:T(8,128)S(1)} %get-tuple-element.29), channel_id=1, source_target_pairs={{8,16},{16,8},{24,32},{32,24},{40,48},{48,40},{56,64},{64,56},{72,... | collective-permute-start | bytes 393224 | tf_op jit(solution)/shard_map/ppermute | solution.py:574
  38.8 5.5 %copy-start.3 = (f32[256,128]{1,0:T(8,128)}, f32[256,128]{1,0:T(8,128)S(1)}, u32[]{:S(2)}) copy-start(f32[256,128]{1,0:T(8,128)S(1)} %collective-permute-done.4.refs_4_) | copy-start | bytes 393220
  44.3 0.6 %copy-start.4 = (f32[256,128]{1,0:T(8,128)}, f32[256,128]{1,0:T(8,128)S(1)}, u32[]{:S(2)}) copy-start(f32[256,128]{1,0:T(8,128)S(1)} %collective-permute-done.5.refs_5_) | copy-start | bytes 393220

commit v7 on v6

--- a/solution.py
+++ b/solution.py
@@ -523,25 +523,27 @@
     full = full[: count + 2, : count + 2]
     hi = full.astype(BF16)
     lo = (full - hi.astype(F32)).astype(BF16)
-    twice = jnp.concatenate([hi, hi], axis=1)
+    stacked = jnp.concatenate(
+        [jnp.concatenate([hi, hi], axis=1), jnp.concatenate([lo, jnp.zeros_like(lo)], axis=1)], axis=0
+    )
     size = count + 2
-    blocks = block.shape[1] // 8
-    copies = []
-    for b in range(blocks):
-        tiles = []
-        for pair in range(4 * b, 4 * b + 4):
-            r = jnp.dot(twice, halves[pair], preferred_element_type=F32)
-            r = r + jnp.dot(lo, halves[pair, :size], preferred_element_type=F32)
-            tiles.append(r[:, :n])
-            tiles.append(r[:, n:])
-        block[:, 8 * b : 8 * b + 8, :] = jnp.swapaxes(jnp.stack(tiles), 0, 1)
-        copy = pltpu.make_async_copy(
-            block.at[:, pl.ds(8 * b, 8), :], out.at[:, pl.ds(8 * b, 8), :], sems.at[b]
-        )
-        copy.start()
-        copies.append(copy)
-    for copy in copies:
-        copy.wait()
+
+    def row_copy(at):
+        return pltpu.make_async_copy(block.at[at], out.at[:, at, 0, :], sems.at[at])
+
+    def product(pair, carry):
+        r = jnp.dot(stacked, halves[pair], preferred_element_type=F32)
+        r = r[:size] + r[size:]
+        for half in range(2):
+            at = 2 * pair + half
+            block[at] = r[:, half * n : (half + 1) * n]
+            row_copy(at).start()
+        return carry
+
+    pairs = halves.shape[0]
+    lax.fori_loop(0, pairs, product, 0, unroll=8)
+    for at in range(2 * pairs):
+        row_copy(at).wait()
 
 
 def whole(n):
@@ -635,7 +637,7 @@
 
     other = lax.ppermute(local, "c", [(0, 1), (1, 0)])
     sent = pl.pallas_call(
-        spread_kernel, out_shape=shaped(chips, 2, ny), in_specs=whole(2), out_specs=whole(1)[0],
+        spread_kernel, out_shape=VMEM((chips, 2, ny), F32), in_specs=whole(2), out_specs=whole(1)[0],
         compiler_params=limit(4), cost_estimate=cost(10**4, 2**17), name="spread",
     )(local, other)
     parts = lax.all_to_all(sent, CHIPS, 0, 0, tiled=True)
@@ -660,11 +662,11 @@
 
     basis_next = pl.pallas_call(
         lambda *refs: core_kernel(rows_all, *refs),
-        out_shape=shaped(count + 2, rows, ny),
+        out_shape=shaped(count + 2, rows, 1, ny),
         in_specs=whole(3), out_specs=pl.BlockSpec(memory_space=pl.ANY),
         scratch_shapes=[
-            VMEM((count + 2, rows, ny), F32),
-            pltpu.SemaphoreType.DMA((rows // 8,)),
+            VMEM((rows, count + 2, ny), F32),
+            pltpu.SemaphoreType.DMA((rows,)),
         ],
         compiler_params=limit(16), cost_estimate=cost(10**8, 6 * 2**20), name="core",
     )(

time: 57.3 us -> 57.9 us (1.010)
  Pallas kernels: 18.8 us -> 19.4 us
    pallas_call x1, Pallas kernels: 2.97 us -> 3.59 us  [steps(): pl.pallas_call(lambda *refs: core_kernel(rows_all, *refs), out_shape=shap...]
where the time goes in v7:
time: 57.9 us; the launch traced here: 57.7 us
  starting transfers between devices  27 us (47%)
  Pallas kernels  19.4 us (34%)
  waiting for transfers between devices  9.88 us (17%)
  between operations  0.74 us (1%)
  local copies, waits for them, and re-layouts  0.66 us (1%)
    ppermute x6, starting transfers between devices, swap(): return lax.ppermute(x, axes, pairs)  15.4 us
    all_to_all x1, starting transfers between devices, steps(): parts = lax.all_to_all(sent, CHIPS, 0, 0, tiled=True)  9.66 us
    pallas_call x1, Pallas kernels, steps(): pl.pallas_call(lambda *refs: bulk_kernel(8, *refs), out_shape=(shaped(nz,...  9.14 us
    ppermute x6, waiting for transfers between devices, swap(): return lax.ppermute(x, axes, pairs)  9.06 us
    pallas_call x1, Pallas kernels, steps(): pl.pallas_call(lambda *refs: core_kernel(rows_all, *refs), out_shape=shap...  3.59 us
    pallas_call x1, Pallas kernels, steps(): pl.pallas_call(lambda *refs: pack_columns_kernel(4, *refs), out_shape=(co...  2.08 us
    pallas_call x1, Pallas kernels, steps(): pl.pallas_call(window_kernel, out_shape=(pltpu.HBM((6 * nx + 16, ny), F32...  1.97 us
    ppermute x1, starting transfers between devices, steps(): other = lax.ppermute(local, 'c', [(0, 1), (1, 0)])  1.96 us
  transfers between devices with their start and end apart: 8, of which 4 were waited for; matrix products, arithmetic and copies ran while one was open for 0% of the time, Pallas kernels for 19%

profile of v7, /device:TPU:1, one launch (start us, length us, event | category | flops | bytes accessed | tf_op | source)
XLA Modules:
  0.0 57.7 jit_solution(8297055428334444837)
XLA Ops:
  0.6 2.1 %columns.1 = (f32[3,32,128]{2,1,0:T(8,128)S(1)}, f32[3,32,128]{2,1,0:T(8,128)S(1)}, f32[192,128]{1,0:T(8,128)S(1)}, f32[256,128]{1,0:T(8,128)S(1)}, f32[256,128]...) custom-call(f32[4096,128]{1,0:T(8,128)} %bitcast.12, f32[128,32,1,128]{3,2,1,0:T(1,128)} %bitcast.13, ...), custom_call_target="tpu_custom_call" | custom-call | flops 1000000 | bytes 2097152 | tf_op jit(solution)/shard_map/columns/pallas_call | solution.py:591
  2.7 3.3 %collective-permute-start = (f32[3,32,128]{2,1,0:T(8,128)S(1)}, f32[3,32,128]{2,1,0:T(8,128)S(1)}, u32[]{:S(2)}, u32[]{:S(2)}) collective-permute-start(f32[3,32,128]{2,1,0:T(8,128)S(1)} %get-tuple-element.21), channel_id=1, source_target_pairs={{0,1},{1,0},{2,3},{3,2},{4,5},{5,4},{6,7},{7,6},{8,9},{9,8},{10,11... | collective-permute-start | bytes 147464 | tf_op jit(solution)/shard_map/ppermute | solution.py:576
  6.0 0.0 collective-permute-start.1
  6.0 0.9 %collective-permute-done.sides_near.refs_9_ = f32[3,32,128]{2,1,0:T(8,128)S(1)} collective-permute-done((f32[3,32,128]{2,1,0:T(8,128)S(1)}, f32[3,32,128]{2,1,0:T(8,128)S(1)}, u32[]{:S(2)}, u32[]{:S(2)}) %collective-permute-start) | collective-permute-done | bytes 49184 | tf_op jit(solution)/shard_map/ppermute | solution.py:576
  6.9 2.6 %collective-permute-done.1.sides_far.refs_10_ = f32[3,32,128]{2,1,0:T(8,128)S(1)} collective-permute-done((f32[3,32,128]{2,1,0:T(8,128)S(1)}, f32[3,32,128]{2,1,0:T(8,128)S(1)}, u32[]{:S(2)}, u32[]{:S(2)}) %collective-permute-start.1) | collective-permute-done | bytes 49184 | tf_op jit(solution)/shard_map/ppermute | solution.py:576
  9.6 0.1 collective-permute-start.2
  9.7 6.8 %collective-permute-start.3 = (f32[24,128]{1,0:T(8,128)S(1)}, f32[24,128]{1,0:T(8,128)S(1)}, u32[]{:S(2)}, u32[]{:S(2)}) collective-permute-start(f32[24,128]{1,0:T(8,128)S(1)} %get-tuple-element.26), channel_id=1, source_target_pairs={{8,16},{16,8},{24,32},{32,24},{40,48},{48,40},{56,64},{64,56},{72,... | collective-permute-start | bytes 36872 | tf_op jit(solution)/shard_map/ppermute | solution.py:576
  16.4 0.0 copy-start.1
  16.4 1.9 %load.1.basis = f32[94,64,128]{2,1,0:T(8,128)S(1)} custom-call(f32[94,64,128]{2,1,0:T(8,128)} %bitcast.14), custom_call_target="tpu_custom_call" | custom-call | bytes 6291456 | tf_op jit(solution)/shard_map/load/pallas_call | solution.py:618
  18.3 0.0 copy-start
  18.3 0.0 copy-start.2
  18.3 0.0 collective-permute-done.2.rows_near
  18.4 0.0 collective-permute-done.3.rows_far
  18.4 0.0 copy-done.1
  18.4 2.0 %window.1 = (f32[208,128]{1,0:T(8,128)}, f32[2,128]{1,0:T(2,128)S(1)}) custom-call(f32[128]{0:T(128)S(1)} %copy-done.1, f32[192,128]{1,0:T(8,128)S(1)} %get-tuple-element.18.window.near, f32[2,32,128]{2,1,0:T(8,128)S(1)} %get-tuple-element.19.velocity, f32[1,128]{1,0:T(1,128)S(1)} %bitcast.9, f32[2,32,128]{2,1,0:T(8,128)S(1)} %get-tuple-element.20.mine, ...), custom_call_target="tpu_custom_call" | custom-call | flops 10000000 | bytes 4194304 | tf_op jit(solution)/shard_map/window/pallas_call | solution.py:624
  20.4 2.0 %collective-permute-start.6 = (f32[2,128]{1,0:T(2,128)S(1)}, f32[2,128]{1,0:T(2,128)S(1)}, u32[]{:S(2)}, u32[]{:S(2)}) collective-permute-start(f32[2,128]{1,0:T(2,128)S(1)} %get-tuple-element.31.mine), channel_id=1, source_target_pairs={{0,1},{1,0},{2,3},{3,2},{4,5},{5,4},{6,7},{7,6},{8,9},{9,8},{10,11... | collective-permute-start | bytes 3080 | tf_op jit(solution)/shard_map/ppermute | solution.py:638
  22.3 0.8 %collective-permute-done.6.other = f32[2,128]{1,0:T(2,128)S(1)} collective-permute-done((f32[2,128]{1,0:T(2,128)S(1)}, f32[2,128]{1,0:T(2,128)S(1)}, u32[]{:S(2)}, u32[]{:S(2)}) %collective-permute-start.6) | collective-permute-done | bytes 1056 | tf_op jit(solution)/shard_map/ppermute | solution.py:638
  23.1 0.7 %spread.1 = f32[128,2,128]{2,1,0:T(2,128)} custom-call(f32[2,128]{1,0:T(2,128)S(1)} %get-tuple-element.31.mine, f32[2,128]{1,0:T(2,128)S(1)} %collective-permute-done.6.other), custom_call_target="tpu_custom_call" | custom-call | flops 10000 | bytes 131072 | tf_op jit(solution)/shard_map/spread/pallas_call | solution.py:639
  23.8 9.7 %all-to-all-start = ((f32[128,2,128]{2,1,0:T(2,128)}), f32[128,2,128]{2,1,0:T(2,128)S(1)}, u32[]{:S(2)}, u32[]{:S(2)}) async-start(f32[128,2,128]{2,1,0:T(2,128)} %spread.1), calls=%async_computation | async-start | bytes 262144 | tf_op jit(solution)/shard_map/all_to_all | solution.py:643
  33.5 0.7 %collective-permute-start.4 = (f32[256,128]{1,0:T(8,128)S(1)}, f32[256,128]{1,0:T(8,128)S(1)}, u32[]{:S(2)}, u32[]{:S(2)}) collective-permute-start(f32[256,128]{1,0:T(8,128)S(1)} %get-tuple-element.28), channel_id=1, source_target_pairs={{0,8},{8,0},{16,24},{24,16},{32,40},{40,32},{48,56},{56,48},{64,72... | collective-permute-start | bytes 393224 | tf_op jit(solution)/shard_map/ppermute | solution.py:576
  34.2 4.6 %collective-permute-start.5 = (f32[256,128]{1,0:T(8,128)S(1)}, f32[256,128]{1,0:T(8,128)S(1)}, u32[]{:S(2)}, u32[]{:S(2)}) collective-permute-start(f32[256,128]{1,0:T(8,128)S(1)} %get-tuple-element.29), channel_id=1, source_target_pairs={{8,16},{16,8},{24,32},{32,24},{40,48},{48,40},{56,64},{64,56},{72,... | collective-permute-start | bytes 393224 | tf_op jit(solution)/shard_map/ppermute | solution.py:576
  38.8 0.0 collective-permute-done.4.refs_4_
  38.8 0.0 copy-start.3
  38.8 5.5 %collective-permute-done.5.refs_5_ = f32[256,128]{1,0:T(8,128)S(1)} collective-permute-done((f32[256,128]{1,0:T(8,128)S(1)}, f32[256,128]{1,0:T(8,128)S(1)}, u32[]{:S(2)}, u32[]{:S(2)}) %collective-permute-start.5) | collective-permute-done | bytes 131104 | tf_op jit(solution)/shard_map/ppermute | solution.py:576
  44.3 0.0 copy-start.4
  44.3 0.0 copy-done.3
  44.3 0.6 %copy-done.4 = f32[256,128]{1,0:T(8,128)} copy-done((f32[256,128]{1,0:T(8,128)}, f32[256,128]{1,0:T(8,128)S(1)}, u32[]{:S(2)}) %copy-start.4) | copy-done | bytes 131096
  44.9 0.0 copy-done
  44.9 0.0 copy-done.2
  44.9 9.1 %bulk.1 = (f32[128,32,128]{2,1,0:T(8,128)}, bf16[32,192,256]{2,1,0:T(8,128)(2,1)S(1)}, f32[8,128]{1,0:T(8,128)S(1)}) custom-call(f32[128]{0:T(128)S(1)} %copy-done.1, f32[128,32,128]{2,1,0:T(8,128)} %refs_1_.1, f32[94,64,1,128]{3,2,1,0:T(1,128)} %bitcast.15, f32[208,128]{1,0:T(8,128)} %get-tuple-element.27.refs_3_, f32[256,128]{1,0:T(8,128)} %copy-done.3, ...), custom_call_target="tpu_custom_call" | custom-call | flops 100000000 | bytes 10485760 | tf_op jit(solution)/shard_map/bulk/pallas_call | solution.py:647
  54.1 0.0 all-to-all-done
  54.1 3.6 %core.1 = f32[96,64,1,128]{3,2,1,0:T(1,128)} custom-call(f32[32,8,128]{2,1,0:T(8,128)S(1)} %bitcast.8, f32[8,128]{1,0:T(8,128)S(1)} %get-tuple-element.32.refs_1_, bf16[32,192,256]{2,1,0:T(8,128)(2,1)S(1)} %get-tuple-element.33.refs_2_), custom_call_target="tpu_custom_call" | custom-call | flops 100000000 | bytes 6291456 | tf_op jit(solution)/shard_map/core/pallas_call | solution.py:663
  (1 shorter events, 0.0 us)
Async XLA Ops:
  2.7 4.2 %collective-permute-start = (f32[3,32,128]{2,1,0:T(8,128)S(1)}, f32[3,32,128]{2,1,0:T(8,128)S(1)}, u32[]{:S(2)}, u32[]{:S(2)}) collective-permute-start(f32[3,32,128]{2,1,0:T(8,128)S(1)} %get-tuple-element.21), channel_id=1, source_target_pairs={{0,1},{1,0},{2,3},{3,2},{4,5},{5,4},{6,7},{7,6},{8,9},{9,8},{10,11... | collective-permute-start | bytes 147464 | tf_op jit(solution)/shard_map/ppermute | solution.py:576
  6.0 3.5 %collective-permute-start.1 = (f32[3,32,128]{2,1,0:T(8,128)S(1)}, f32[3,32,128]{2,1,0:T(8,128)S(1)}, u32[]{:S(2)}, u32[]{:S(2)}) collective-permute-start(f32[3,32,128]{2,1,0:T(8,128)S(1)} %get-tuple-element.22), channel_id=1, source_target_pairs={{1,2},{2,1},{3,4},{4,3},{5,6},{6,5},{7,0},{0,7},{9,10},{10,9},{11,... | collective-permute-start | bytes 147464 | tf_op jit(solution)/shard_map/ppermute | solution.py:576
  9.6 8.8 %collective-permute-start.2 = (f32[24,128]{1,0:T(8,128)S(1)}, f32[24,128]{1,0:T(8,128)S(1)}, u32[]{:S(2)}, u32[]{:S(2)}) collective-permute-start(f32[24,128]{1,0:T(8,128)S(1)} %get-tuple-element.25), channel_id=1, source_target_pairs={{0,8},{8,0},{16,24},{24,16},{32,40},{40,32},{48,56},{56,48},{64,72... | collective-permute-start | bytes 36872 | tf_op jit(solution)/shard_map/ppermute | solution.py:576
  9.7 8.7 %collective-permute-start.3 = (f32[24,128]{1,0:T(8,128)S(1)}, f32[24,128]{1,0:T(8,128)S(1)}, u32[]{:S(2)}, u32[]{:S(2)}) collective-permute-start(f32[24,128]{1,0:T(8,128)S(1)} %get-tuple-element.26), channel_id=1, source_target_pairs={{8,16},{16,8},{24,32},{32,24},{40,48},{48,40},{56,64},{64,56},{72,... | collective-permute-start | bytes 36872 | tf_op jit(solution)/shard_map/ppermute | solution.py:576
  16.4 1.9 %copy-start.1 = (f32[128]{0:T(128)S(1)}, f32[128]{0:T(128)}, u32[]{:S(2)}) copy-start(f32[128]{0:T(128)} %refs_0_.1) | copy-start | bytes 1540
  18.3 26.6 %copy-start = (f32[2,32,128]{2,1,0:T(8,128)S(1)}, f32[2,32,128]{2,1,0:T(8,128)}, u32[]{:S(2)}) copy-start(f32[2,32,128]{2,1,0:T(8,128)} %refs_6_.1) | copy-start | bytes 98308
  18.3 26.6 %copy-start.2 = (f32[94]{0:T(128)S(1)}, f32[94]{0:T(128)}, u32[]{:S(2)}) copy-start(f32[94]{0:T(128)} %param.8) | copy-start | bytes 1132
  20.4 2.8 %collective-permute-start.6 = (f32[2,128]{1,0:T(2,128)S(1)}, f32[2,128]{1,0:T(2,128)S(1)}, u32[]{:S(2)}, u32[]{:S(2)}) collective-permute-start(f32[2,128]{1,0:T(2,128)S(1)} %get-tuple-element.31.mine), channel_id=1, source_target_pairs={{0,1},{1,0},{2,3},{3,2},{4,5},{5,4},{6,7},{7,6},{8,9},{9,8},{10,11... | collective-permute-start | bytes 3080 | tf_op jit(solution)/shard_map/ppermute | solution.py:638
  23.8 30.3 %all-to-all-start = ((f32[128,2,128]{2,1,0:T(2,128)}), f32[128,2,128]{2,1,0:T(2,128)S(1)}, u32[]{:S(2)}, u32[]{:S(2)}) async-start(f32[128,2,128]{2,1,0:T(2,128)} %spread.1), calls=%async_computation | async-start | bytes 262144 | tf_op jit(solution)/shard_map/all_to_all | solution.py:643
  33.5 5.3 %collective-permute-start.4 = (f32[256,128]{1,0:T(8,128)S(1)}, f32[256,128]{1,0:T(8,128)S(1)}, u32[]{:S(2)}, u32[]{:S(2)}) collective-permute-start(f32[256,128]{1,0:T(8,128)S(1)} %get-tuple-element.28), channel_id=1, source_target_pairs={{0,8},{8,0},{16,24},{24,16},{32,40},{40,32},{48,56},{56,48},{64,72... | collective-permute-start | bytes 393224 | tf_op jit(solution)/shard_map/ppermute | solution.py:576
  34.2 10.1 %collective-permute-start.5 = (f32[256,128]{1,0:T(8,128)S(1)}, f32[256,128]{1,0:T(8,128)S(1)}, u32[]{:S(2)}, u32[]{:S(2)}) collective-permute-start(f32[256,128]{1,0:T(8,128)S(1)} %get-tuple-element.29), channel_id=1, source_target_pairs={{8,16},{16,8},{24,32},{32,24},{40,48},{48,40},{56,64},{64,56},{72,... | collective-permute-start | bytes 393224 | tf_op jit(solution)/shard_map/ppermute | solution.py:576
  38.8 5.5 %copy-start.3 = (f32[256,128]{1,0:T(8,128)}, f32[256,128]{1,0:T(8,128)S(1)}, u32[]{:S(2)}) copy-start(f32[256,128]{1,0:T(8,128)S(1)} %collective-permute-done.4.refs_4_) | copy-start | bytes 393220
  44.3 0.6 %copy-start.4 = (f32[256,128]{1,0:T(8,128)}, f32[256,128]{1,0:T(8,128)S(1)}, u32[]{:S(2)}) copy-start(f32[256,128]{1,0:T(8,128)S(1)} %collective-permute-done.5.refs_5_) | copy-start | bytes 393220

commit v8 on v6

--- a/solution.py
+++ b/solution.py
@@ -66,7 +66,7 @@
 
 
 def pack_columns_kernel(
-    chunks, tracer_hbm, by_row_hbm, velocity_hbm, near, far, window, rows_near, rows_far, mine, velocity,
+    chunks, tracer_hbm, velocity_hbm, near, far, window, mine, velocity,
     tracer, sems,
 ):
     nx, ny = velocity.shape[1:]
@@ -83,12 +83,6 @@
     moves.append((velocity_hbm, velocity))
     moves.append(rows_of_level(nz - 2, 2, window.at[0 : 2 * nx]))
     moves.append(rows_of_level(0, 4, window.at[2 * nx : 6 * nx]))
-    even = gx_is_even()
-    for i in range(2):
-        part, first, last = pl.ds(i * nz, nz), i, nx - 1 - i
-        at_near, at_far = jnp.where(even, last, first), jnp.where(even, first, last)
-        moves.append((by_row_hbm.at[:, at_near, 0, :], rows_near.at[part]))
-        moves.append((by_row_hbm.at[:, at_far, 0, :], rows_far.at[part]))
     loads = [pltpu.make_async_copy(src, dst, sems.at[i]) for i, (src, dst) in enumerate(moves)]
     for load in loads:
         load.start()
@@ -269,12 +263,23 @@
         halves[pair, size:, lanes] = (v - hi.astype(F32)).astype(BF16)
 
 
-def load_kernel(src, dst, sems):
-    parts = sems.shape[0]
+def load_kernel(src, by_row_hbm, dst, rows_near, rows_far, sems):
+    nz, nx = by_row_hbm.shape[:2]
+    parts = 2
     size = src.shape[0] // parts
     copies = [
         pltpu.make_async_copy(src.at[pl.ds(i * size, size)], dst.at[pl.ds(i * size, size)], sems.at[i])
         for i in range(parts)
+    ]
+    moves = []
+    even = gx_is_even()
+    for i in range(2):
+        part, first, last = pl.ds(i * nz, nz), i, nx - 1 - i
+        at_near, at_far = jnp.where(even, last, first), jnp.where(even, first, last)
+        moves.append((by_row_hbm.at[:, at_near, 0, :], rows_near.at[part]))
+        moves.append((by_row_hbm.at[:, at_far, 0, :], rows_far.at[part]))
+    copies += [
+        pltpu.make_async_copy(a, b, sems.at[parts + i]) for i, (a, b) in enumerate(moves)
     ]
     for copy in copies:
         copy.start()
@@ -586,19 +591,19 @@
     columns = shaped(3, nx, ny)
     bulk_rows = shaped(2 * nz, ny)
     hbm_space, any_space = (pl.BlockSpec(memory_space=m) for m in (pltpu.HBM, pl.ANY))
-    columns_near, columns_far, near, sent_near, sent_far, mine, speeds = pl.pallas_call(
+    columns_near, columns_far, near, mine, speeds = pl.pallas_call(
         lambda *refs: pack_columns_kernel(4, *refs),
         out_shape=(
-            columns, columns, shaped(6 * nx, ny), bulk_rows, bulk_rows, shaped(2, nx, ny),
+            columns, columns, shaped(6 * nx, ny), shaped(2, nx, ny),
             shaped(2, nx, ny),
         ),
-        in_specs=[hbm_space] * 3, out_specs=tuple(whole(7)),
+        in_specs=[hbm_space] * 2, out_specs=tuple(whole(5)),
         scratch_shapes=[
             VMEM((nz * nx, ny), F32), pltpu.SemaphoreType.DMA((11,)),
         ],
         compiler_params=limit(4), cost_estimate=cost(10**6, 2 * 2**20), name="columns",
     )(
-        in_hbm(tracer.reshape(nz * nx, ny)), in_hbm(tracer.reshape(nz, nx, 1, ny)), in_hbm(velocity)
+        in_hbm(tracer.reshape(nz * nx, ny)), in_hbm(velocity)
     )
     sides_far = swap(columns_far, GY, True)
     sides_near = swap(columns_near, GY, False)
@@ -610,15 +615,15 @@
     window_far = swap(edges_far, GX, True)
     window_near = swap(edges_near, GX, False)
 
+    vectors, sent_near, sent_far = pl.pallas_call(
+        load_kernel, out_shape=(shaped(count, rows, ny), bulk_rows, bulk_rows),
+        in_specs=[hbm_space] * 2, out_specs=tuple(whole(3)),
+        scratch_shapes=[pltpu.SemaphoreType.DMA((6,))],
+        compiler_params=limit(2), cost_estimate=cost(0, 6 * 2**20), name="load",
+    )(in_hbm(basis), in_hbm(tracer.reshape(nz, nx, 1, ny)))
     rows_far = in_hbm(swap(in_hbm(sent_far), GX, True))
     rows_near = in_hbm(swap(in_hbm(sent_near), GX, False))
 
-    vectors = pl.pallas_call(
-        load_kernel, out_shape=shaped(count, rows, ny),
-        in_specs=[hbm_space], out_specs=whole(1)[0],
-        scratch_shapes=[pltpu.SemaphoreType.DMA((2,))],
-        compiler_params=limit(2), cost_estimate=cost(0, 6 * 2**20), name="load",
-    )(in_hbm(basis))
     kept, local = pl.pallas_call(
         window_kernel,
         out_shape=(pltpu.HBM((6 * nx + 16, ny), F32), shaped(2, ny)),

time: 57.3 us -> 57.3 us (level)
  no operation moved by 1% of the time
where the time goes in v8:
time: 57.3 us; the launch traced here: 57.1 us
  starting transfers between devices  27 us (47%)
  Pallas kernels  18.8 us (33%)
  waiting for transfers between devices  9.88 us (17%)
  between operations  0.74 us (1%)
  local copies, waits for them, and re-layouts  0.67 us (1%)
    ppermute x6, starting transfers between devices, swap(): return lax.ppermute(x, axes, pairs)  15.4 us
    all_to_all x1, starting transfers between devices, steps(): parts = lax.all_to_all(sent, CHIPS, 0, 0, tiled=True)  9.64 us
    pallas_call x1, Pallas kernels, steps(): pl.pallas_call(lambda *refs: bulk_kernel(8, *refs), out_shape=(shaped(nz,...  9.14 us
    ppermute x6, waiting for transfers between devices, swap(): return lax.ppermute(x, axes, pairs)  9.06 us
    pallas_call x1, Pallas kernels, steps(): pl.pallas_call(lambda *refs: core_kernel(rows_all, *refs), out_shape=shap...  2.97 us
    pallas_call x1, Pallas kernels, steps(): pl.pallas_call(lambda *refs: pack_columns_kernel(4, *refs), out_shape=(co...  2.08 us
    pallas_call x1, Pallas kernels, steps(): pl.pallas_call(window_kernel, out_shape=(pltpu.HBM((6 * nx + 16, ny), F32...  1.97 us
    ppermute x1, starting transfers between devices, steps(): other = lax.ppermute(local, 'c', [(0, 1), (1, 0)])  1.96 us
  transfers between devices with their start and end apart: 8, of which 4 were waited for; matrix products, arithmetic and copies ran while one was open for 0% of the time, Pallas kernels for 19%

profile of v8, /device:TPU:1, one launch (start us, length us, event | category | flops | bytes accessed | tf_op | source)
XLA Modules:
  0.0 57.1 jit_solution(7572528682209265112)
XLA Ops:
  0.6 2.1 %columns.1 = (f32[3,32,128]{2,1,0:T(8,128)S(1)}, f32[3,32,128]{2,1,0:T(8,128)S(1)}, f32[192,128]{1,0:T(8,128)S(1)}, f32[2,32,128]{2,1,0:T(8,128)S(1)}, f32[2,32,128]{2,1,0:T(8,128)S(1)}) custom-call(f32[4096,128]{1,0:T(8,128)} %bitcast.12, f32[2,32,128]{2,1,0:T(8,128)} %refs_6_.1), custom_call_target="tpu_custom_call" | custom-call | flops 1000000 | bytes 2097152 | tf_op jit(solution)/shard_map/columns/pallas_call | solution.py:594
  2.7 0.0 copy-start.1
  2.7 3.3 %collective-permute-start = (f32[3,32,128]{2,1,0:T(8,128)S(1)}, f32[3,32,128]{2,1,0:T(8,128)S(1)}, u32[]{:S(2)}, u32[]{:S(2)}) collective-permute-start(f32[3,32,128]{2,1,0:T(8,128)S(1)} %get-tuple-element.22), channel_id=1, source_target_pairs={{0,1},{1,0},{2,3},{3,2},{4,5},{5,4},{6,7},{7,6},{8,9},{9,8},{10,11... | collective-permute-start | bytes 147464 | tf_op jit(solution)/shard_map/ppermute | solution.py:579
  6.0 0.0 collective-permute-start.1
  6.0 0.9 %collective-permute-done.sides_near.refs_9_ = f32[3,32,128]{2,1,0:T(8,128)S(1)} collective-permute-done((f32[3,32,128]{2,1,0:T(8,128)S(1)}, f32[3,32,128]{2,1,0:T(8,128)S(1)}, u32[]{:S(2)}, u32[]{:S(2)}) %collective-permute-start) | collective-permute-done | bytes 49184 | tf_op jit(solution)/shard_map/ppermute | solution.py:579
  6.9 2.6 %collective-permute-done.1.sides_far.refs_10_ = f32[3,32,128]{2,1,0:T(8,128)S(1)} collective-permute-done((f32[3,32,128]{2,1,0:T(8,128)S(1)}, f32[3,32,128]{2,1,0:T(8,128)S(1)}, u32[]{:S(2)}, u32[]{:S(2)}) %collective-permute-start.1) | collective-permute-done | bytes 49184 | tf_op jit(solution)/shard_map/ppermute | solution.py:579
  9.6 0.1 collective-permute-start.2
  9.7 6.8 %collective-permute-start.3 = (f32[24,128]{1,0:T(8,128)S(1)}, f32[24,128]{1,0:T(8,128)S(1)}, u32[]{:S(2)}, u32[]{:S(2)}) collective-permute-start(f32[24,128]{1,0:T(8,128)S(1)} %get-tuple-element.27), channel_id=1, source_target_pairs={{8,16},{16,8},{24,32},{32,24},{40,48},{48,40},{56,64},{64,56},{72,... | collective-permute-start | bytes 36872 | tf_op jit(solution)/shard_map/ppermute | solution.py:579
  16.4 1.9 %load.1 = (f32[94,64,128]{2,1,0:T(8,128)S(1)}, f32[256,128]{1,0:T(8,128)S(1)}, f32[256,128]{1,0:T(8,128)S(1)}) custom-call(f32[94,64,128]{2,1,0:T(8,128)} %bitcast.14, f32[128,32,1,128]{3,2,1,0:T(1,128)} %bitcast.13), custom_call_target="tpu_custom_call" | custom-call | bytes 6291456 | tf_op jit(solution)/shard_map/load/pallas_call | solution.py:618
  18.4 0.0 copy-start
  18.4 0.0 copy-start.2
  18.4 0.0 collective-permute-done.2.rows_near
  18.4 0.0 collective-permute-done.3.rows_far
  18.4 0.0 copy-done.1
  18.4 2.0 %window.1 = (f32[208,128]{1,0:T(8,128)}, f32[2,128]{1,0:T(2,128)S(1)}) custom-call(f32[128]{0:T(128)S(1)} %copy-done.1, f32[192,128]{1,0:T(8,128)S(1)} %get-tuple-element.19.window.near, f32[2,32,128]{2,1,0:T(8,128)S(1)} %get-tuple-element.20.velocity, f32[1,128]{1,0:T(1,128)S(1)} %bitcast.9, f32[2,32,128]{2,1,0:T(8,128)S(1)} %get-tuple-element.21.mine, ...), custom_call_target="tpu_custom_call" | custom-call | flops 10000000 | bytes 4194304 | tf_op jit(solution)/shard_map/window/pallas_call | solution.py:627
  20.4 2.0 %collective-permute-start.6 = (f32[2,128]{1,0:T(2,128)S(1)}, f32[2,128]{1,0:T(2,128)S(1)}, u32[]{:S(2)}, u32[]{:S(2)}) collective-permute-start(f32[2,128]{1,0:T(2,128)S(1)} %get-tuple-element.33.mine), channel_id=1, source_target_pairs={{0,1},{1,0},{2,3},{3,2},{4,5},{5,4},{6,7},{7,6},{8,9},{9,8},{10,11... | collective-permute-start | bytes 3080 | tf_op jit(solution)/shard_map/ppermute | solution.py:641
  22.3 0.8 %collective-permute-done.6.other = f32[2,128]{1,0:T(2,128)S(1)} collective-permute-done((f32[2,128]{1,0:T(2,128)S(1)}, f32[2,128]{1,0:T(2,128)S(1)}, u32[]{:S(2)}, u32[]{:S(2)}) %collective-permute-start.6) | collective-permute-done | bytes 1056 | tf_op jit(solution)/shard_map/ppermute | solution.py:641
  23.2 0.7 %spread.1 = f32[128,2,128]{2,1,0:T(2,128)} custom-call(f32[2,128]{1,0:T(2,128)S(1)} %get-tuple-element.33.mine, f32[2,128]{1,0:T(2,128)S(1)} %collective-permute-done.6.other), custom_call_target="tpu_custom_call" | custom-call | flops 10000 | bytes 131072 | tf_op jit(solution)/shard_map/spread/pallas_call | solution.py:642
  23.9 9.6 %all-to-all-start = ((f32[128,2,128]{2,1,0:T(2,128)}), f32[128,2,128]{2,1,0:T(2,128)S(1)}, u32[]{:S(2)}, u32[]{:S(2)}) async-start(f32[128,2,128]{2,1,0:T(2,128)} %spread.1), calls=%async_computation | async-start | bytes 262144 | tf_op jit(solution)/shard_map/all_to_all | solution.py:646
  33.5 0.7 %collective-permute-start.4 = (f32[256,128]{1,0:T(8,128)S(1)}, f32[256,128]{1,0:T(8,128)S(1)}, u32[]{:S(2)}, u32[]{:S(2)}) collective-permute-start(f32[256,128]{1,0:T(8,128)S(1)} %get-tuple-element.30), channel_id=1, source_target_pairs={{0,8},{8,0},{16,24},{24,16},{32,40},{40,32},{48,56},{56,48},{64,72... | collective-permute-start | bytes 393224 | tf_op jit(solution)/shard_map/ppermute | solution.py:579
  34.2 4.6 %collective-permute-start.5 = (f32[256,128]{1,0:T(8,128)S(1)}, f32[256,128]{1,0:T(8,128)S(1)}, u32[]{:S(2)}, u32[]{:S(2)}) collective-permute-start(f32[256,128]{1,0:T(8,128)S(1)} %get-tuple-element.31), channel_id=1, source_target_pairs={{8,16},{16,8},{24,32},{32,24},{40,48},{48,40},{56,64},{64,56},{72,... | collective-permute-start | bytes 393224 | tf_op jit(solution)/shard_map/ppermute | solution.py:579
  38.8 0.0 collective-permute-done.4.refs_4_
  38.8 0.0 copy-start.3
  38.8 5.5 %collective-permute-done.5.refs_5_ = f32[256,128]{1,0:T(8,128)S(1)} collective-permute-done((f32[256,128]{1,0:T(8,128)S(1)}, f32[256,128]{1,0:T(8,128)S(1)}, u32[]{:S(2)}, u32[]{:S(2)}) %collective-permute-start.5) | collective-permute-done | bytes 131104 | tf_op jit(solution)/shard_map/ppermute | solution.py:579
  44.3 0.0 copy-start.4
  44.3 0.0 copy-done.3
  44.3 0.6 %copy-done.4 = f32[256,128]{1,0:T(8,128)} copy-done((f32[256,128]{1,0:T(8,128)}, f32[256,128]{1,0:T(8,128)S(1)}, u32[]{:S(2)}) %copy-start.4) | copy-done | bytes 131096
  45.0 0.0 copy-done
  45.0 0.0 copy-done.2
  45.0 9.1 %bulk.1 = (f32[128,32,128]{2,1,0:T(8,128)}, bf16[32,192,256]{2,1,0:T(8,128)(2,1)S(1)}, f32[8,128]{1,0:T(8,128)S(1)}) custom-call(f32[128]{0:T(128)S(1)} %copy-done.1, f32[128,32,128]{2,1,0:T(8,128)} %refs_1_.3, f32[94,64,1,128]{3,2,1,0:T(1,128)} %bitcast.15, f32[208,128]{1,0:T(8,128)} %get-tuple-element.29.refs_3_, f32[256,128]{1,0:T(8,128)} %copy-done.3, ...), custom_call_target="tpu_custom_call" | custom-call | flops 100000000 | bytes 10485760 | tf_op jit(solution)/shard_map/bulk/pallas_call | solution.py:650
  54.1 0.0 all-to-all-done
  54.1 3.0 %core.1 = f32[96,64,128]{2,1,0:T(8,128)} custom-call(f32[32,8,128]{2,1,0:T(8,128)S(1)} %bitcast.8, f32[8,128]{1,0:T(8,128)S(1)} %get-tuple-element.34.refs_1_, bf16[32,192,256]{2,1,0:T(8,128)(2,1)S(1)} %get-tuple-element.35.refs_2_), custom_call_target="tpu_custom_call" | custom-call | flops 100000000 | bytes 6291456 | tf_op jit(solution)/shard_map/core/pallas_call | solution.py:666
  (1 shorter events, 0.0 us)
Async XLA Ops:
  2.7 15.7 %copy-start.1 = (f32[128]{0:T(128)S(1)}, f32[128]{0:T(128)}, u32[]{:S(2)}) copy-start(f32[128]{0:T(128)} %refs_0_.1) | copy-start | bytes 1540
  2.7 4.2 %collective-permute-start = (f32[3,32,128]{2,1,0:T(8,128)S(1)}, f32[3,32,128]{2,1,0:T(8,128)S(1)}, u32[]{:S(2)}, u32[]{:S(2)}) collective-permute-start(f32[3,32,128]{2,1,0:T(8,128)S(1)} %get-tuple-element.22), channel_id=1, source_target_pairs={{0,1},{1,0},{2,3},{3,2},{4,5},{5,4},{6,7},{7,6},{8,9},{9,8},{10,11... | collective-permute-start | bytes 147464 | tf_op jit(solution)/shard_map/ppermute | solution.py:579
  6.0 3.5 %collective-permute-start.1 = (f32[3,32,128]{2,1,0:T(8,128)S(1)}, f32[3,32,128]{2,1,0:T(8,128)S(1)}, u32[]{:S(2)}, u32[]{:S(2)}) collective-permute-start(f32[3,32,128]{2,1,0:T(8,128)S(1)} %get-tuple-element.23), channel_id=1, source_target_pairs={{1,2},{2,1},{3,4},{4,3},{5,6},{6,5},{7,0},{0,7},{9,10},{10,9},{11,... | collective-permute-start | bytes 147464 | tf_op jit(solution)/shard_map/ppermute | solution.py:579
  9.6 8.8 %collective-permute-start.2 = (f32[24,128]{1,0:T(8,128)S(1)}, f32[24,128]{1,0:T(8,128)S(1)}, u32[]{:S(2)}, u32[]{:S(2)}) collective-permute-start(f32[24,128]{1,0:T(8,128)S(1)} %get-tuple-element.26), channel_id=1, source_target_pairs={{0,8},{8,0},{16,24},{24,16},{32,40},{40,32},{48,56},{56,48},{64,72... | collective-permute-start | bytes 36872 | tf_op jit(solution)/shard_map/ppermute | solution.py:579
  9.7 8.7 %collective-permute-start.3 = (f32[24,128]{1,0:T(8,128)S(1)}, f32[24,128]{1,0:T(8,128)S(1)}, u32[]{:S(2)}, u32[]{:S(2)}) collective-permute-start(f32[24,128]{1,0:T(8,128)S(1)} %get-tuple-element.27), channel_id=1, source_target_pairs={{8,16},{16,8},{24,32},{32,24},{40,48},{48,40},{56,64},{64,56},{72,... | collective-permute-start | bytes 36872 | tf_op jit(solution)/shard_map/ppermute | solution.py:579
  18.4 26.6 %copy-start = (f32[2,32,128]{2,1,0:T(8,128)S(1)}, f32[2,32,128]{2,1,0:T(8,128)}, u32[]{:S(2)}) copy-start(f32[2,32,128]{2,1,0:T(8,128)} %refs_6_.1) | copy-start | bytes 98308
  18.4 26.6 %copy-start.2 = (f32[94]{0:T(128)S(1)}, f32[94]{0:T(128)}, u32[]{:S(2)}) copy-start(f32[94]{0:T(128)} %param.8) | copy-start | bytes 1132
  20.4 2.8 %collective-permute-start.6 = (f32[2,128]{1,0:T(2,128)S(1)}, f32[2,128]{1,0:T(2,128)S(1)}, u32[]{:S(2)}, u32[]{:S(2)}) collective-permute-start(f32[2,128]{1,0:T(2,128)S(1)} %get-tuple-element.33.mine), channel_id=1, source_target_pairs={{0,1},{1,0},{2,3},{3,2},{4,5},{5,4},{6,7},{7,6},{8,9},{9,8},{10,11... | collective-permute-start | bytes 3080 | tf_op jit(solution)/shard_map/ppermute | solution.py:641
  23.9 30.3 %all-to-all-start = ((f32[128,2,128]{2,1,0:T(2,128)}), f32[128,2,128]{2,1,0:T(2,128)S(1)}, u32[]{:S(2)}, u32[]{:S(2)}) async-start(f32[128,2,128]{2,1,0:T(2,128)} %spread.1), calls=%async_computation | async-start | bytes 262144 | tf_op jit(solution)/shard_map/all_to_all | solution.py:646
  33.5 5.3 %collective-permute-start.4 = (f32[256,128]{1,0:T(8,128)S(1)}, f32[256,128]{1,0:T(8,128)S(1)}, u32[]{:S(2)}, u32[]{:S(2)}) collective-permute-start(f32[256,128]{1,0:T(8,128)S(1)} %get-tuple-element.30), channel_id=1, source_target_pairs={{0,8},{8,0},{16,24},{24,16},{32,40},{40,32},{48,56},{56,48},{64,72... | collective-permute-start | bytes 393224 | tf_op jit(solution)/shard_map/ppermute | solution.py:579
  34.2 10.1 %collective-permute-start.5 = (f32[256,128]{1,0:T(8,128)S(1)}, f32[256,128]{1,0:T(8,128)S(1)}, u32[]{:S(2)}, u32[]{:S(2)}) collective-permute-start(f32[256,128]{1,0:T(8,128)S(1)} %get-tuple-element.31), channel_id=1, source_target_pairs={{8,16},{16,8},{24,32},{32,24},{40,48},{48,40},{56,64},{64,56},{72,... | collective-permute-start | bytes 393224 | tf_op jit(solution)/shard_map/ppermute | solution.py:579
  38.8 5.5 %copy-start.3 = (f32[256,128]{1,0:T(8,128)}, f32[256,128]{1,0:T(8,128)S(1)}, u32[]{:S(2)}) copy-start(f32[256,128]{1,0:T(8,128)S(1)} %collective-permute-done.4.refs_4_) | copy-start | bytes 393220
  44.3 0.7 %copy-start.4 = (f32[256,128]{1,0:T(8,128)}, f32[256,128]{1,0:T(8,128)S(1)}, u32[]{:S(2)}) copy-start(f32[256,128]{1,0:T(8,128)S(1)} %collective-permute-done.5.refs_5_) | copy-start | bytes 393220
